TPU v7x, 512 devices: a whole 4x8x8 slice. The times are simulated.
512 devices in a mesh: dp: 4 (over x_lo, core), blk: 128 (over y, z, x_hi).
Axes of the slice: x: 4 (x_hi: 2, x_lo: 2; x = x_hi * 2 + x_lo), y: 8, z: 8, core: 2. Of those that a mesh axis runs over, the one named last changes fastest.
Arguments:
- queries: bfloat16 [4, 24576, 512], P('dp', 'blk'), may hold values from -6 to 6, as said below
- key_in: bfloat16 [4, 24576, 512], P('dp', 'blk'), may hold values from -6 to 6, as said below
- value_in: bfloat16 [4, 24576, 512], P('dp', 'blk'), may hold values from -6 to 6
- out_weight: bfloat16 [512, 1024], replicated, may hold values from -2 to 2
- conv_kernel: float32 [31, 1024], replicated, may hold values from -1 to 1
- cotangent: bfloat16 [4, 24576, 1024], P('dp', 'blk'), may hold values from -6 to 6
Outputs:
- out_frames: bfloat16 [4, 24576, 1024], P('dp', 'blk')
- query_grad: bfloat16 [4, 24576, 512], P('dp', 'blk')
- key_grad: bfloat16 [4, 24576, 512], P('dp', 'blk')
- value_grad: bfloat16 [4, 24576, 512], P('dp', 'blk')
- weight_grad: float32 [512, 1024], replicated
- kernel_grad: float32 [31, 1024], replicated
Inputs may be any that keep to these rules, and one draw needn't show every extreme that they name: `queries`: independent entries. `key_in`: independent entries.
All inputs are finite; a program needn't handle non-finite values.
Results may differ from a plain program's by a relative error of at most 0.024.
Values may be sent and summed in bfloat16 or wider, within the bound.
A program may use at most 64 MiB of HBM per device.

v0:
```python
import math

import jax
import jax.numpy as jnp
from jax import lax
from jax.sharding import PartitionSpec as P

ATT_HEADS = 8
HEAD_DIM = 64
CTX_MAX = 3
ATT = 512


NEGATIVE = -1e30


def from_behind(block, axis, distance):
    devices = range(lax.axis_size(axis))
    route = [(i - distance, i) for i in devices if i - distance in devices]
    return lax.ppermute(block, axis, route)


def split_heads(matrix):
    return matrix.reshape(matrix.shape[0], ATT_HEADS, HEAD_DIM)


def tile_scores(query_heads, tile, query_pos, key_pos, usable, left_span, score_scale):
    key_heads = split_heads(tile[:, :ATT])
    scores = (
        jnp.einsum("qhd,khd->hqk", query_heads, key_heads, preferred_element_type=jnp.float32)
        * score_scale
    )
    distance = query_pos[:, None] - key_pos[None, :]
    visible = ((distance >= 0) & (distance < left_span) & usable)[None]
    return (jnp.where(visible, scores, NEGATIVE), visible)


def attend_tile(
    softmax_state, query_heads, tile, query_pos, key_pos, usable, left_span, score_scale
):
    running_max, running_sum, weighted = softmax_state
    scores, visible = tile_scores(
        query_heads, tile, query_pos, key_pos, usable, left_span, score_scale
    )
    new_max = jnp.maximum(running_max, jnp.max(scores, axis=-1))
    weights = jnp.where(visible, jnp.exp(scores - new_max[..., None]), 0.0)
    fading = jnp.exp(running_max - new_max)
    running_sum = running_sum * fading + jnp.sum(weights, axis=-1)
    value_heads = split_heads(tile[:, ATT:])
    update = jnp.einsum(
        "hqk,khd->qhd",
        weights.astype(jnp.bfloat16),
        value_heads,
        preferred_element_type=jnp.float32,
    )
    weighted = weighted * jnp.transpose(fading)[:, :, None] + update
    return (new_max, running_sum, weighted)


def tile_grads(
    query_heads,
    dout_heads,
    log_sums,
    deltas,
    tile,
    query_pos,
    key_pos,
    usable,
    left_span,
    score_scale,
):
    scores, visible = tile_scores(
        query_heads, tile, query_pos, key_pos, usable, left_span, score_scale
    )
    key_heads = split_heads(tile[:, :ATT])
    value_heads = split_heads(tile[:, ATT:])
    probs = jnp.where(visible, jnp.exp(scores - log_sums[..., None]), 0.0)
    dvalue_heads = jnp.einsum(
        "hqk,qhd->khd", probs.astype(jnp.bfloat16), dout_heads, preferred_element_type=jnp.float32
    )
    dprobs = jnp.einsum("qhd,khd->hqk", dout_heads, value_heads, preferred_element_type=jnp.float32)
    dscores = (probs * (dprobs - deltas[..., None])).astype(jnp.bfloat16)
    dquery = (
        jnp.einsum("hqk,khd->qhd", dscores, key_heads, preferred_element_type=jnp.float32)
        * score_scale
    )
    dkey_heads = (
        jnp.einsum("hqk,qhd->khd", dscores, query_heads, preferred_element_type=jnp.float32)
        * score_scale
    )
    row_count = tile.shape[0]
    return (
        dquery,
        jnp.concatenate(
            [dkey_heads.reshape(row_count, ATT), dvalue_heads.reshape(row_count, ATT)], axis=1
        ),
    )


def depthwise(extended, conv_kernel, row_count, ahead):
    tap_count = conv_kernel.shape[0]

    def add_tap(tap_index, running):
        first_row = tap_index if ahead else tap_count - 1 - tap_index
        return running + conv_kernel[tap_index] * lax.dynamic_slice_in_dim(
            extended, first_row, row_count, 0
        )

    empty = jnp.zeros((row_count, extended.shape[1]), jnp.float32)
    return lax.fori_loop(0, tap_count, add_tap, empty)


def sum_weights(weight_part, kernel_part):
    return lax.psum((weight_part, kernel_part), ("dp", "blk"))


def per_device(queries, key_in, value_in, out_weight, conv_kernel, cotangent):
    cycle_count = lax.axis_size("blk")
    device = lax.axis_index("blk")
    row_count = queries.shape[1]
    context = min(CTX_MAX, cycle_count // 4)
    left_span = context * row_count
    score_scale = 1.0 / math.sqrt(HEAD_DIM)
    edge_rows = conv_kernel.shape[0] - 1
    row_ids = jnp.arange(row_count, dtype=jnp.int32)
    query_heads = split_heads(queries[0])
    own_tile = jnp.concatenate([key_in[0], value_in[0]], axis=1)
    own_pos = device * row_count + row_ids
    always = jnp.array(True)

    def source(offset):
        anchor = device - offset
        return (anchor * row_count + row_ids, anchor >= 0)

    start_state = (
        jnp.full((ATT_HEADS, row_count), NEGATIVE, jnp.float32),
        jnp.zeros((ATT_HEADS, row_count), jnp.float32),
        jnp.zeros((row_count, ATT_HEADS, HEAD_DIM), jnp.float32),
    )
    first_state = attend_tile(
        start_state, query_heads, own_tile, own_pos, own_pos, always, left_span, score_scale
    )

    def forward_step(carry, offset):
        moving, softmax_state = carry
        arrived = from_behind(moving, "blk", 1)
        tile_pos, tile_usable = source(offset)
        softmax_state = attend_tile(
            softmax_state,
            query_heads,
            arrived,
            own_pos,
            tile_pos,
            tile_usable,
            left_span,
            score_scale,
        )
        return ((arrived, softmax_state), arrived)

    offsets = jnp.arange(1, context + 1, dtype=jnp.int32)
    (unused_tile, final_state), kept_tiles = lax.scan(
        forward_step, (own_tile, first_state), offsets
    )
    running_max, running_sum, weighted = final_state
    attended = (weighted / jnp.transpose(running_sum)[:, :, None]).astype(jnp.bfloat16)
    log_sums = running_max + jnp.log(running_sum)
    flat = attended.reshape(row_count, ATT)
    hidden = jnp.dot(flat, out_weight, preferred_element_type=jnp.float32).astype(jnp.bfloat16)
    before = from_behind(hidden[-edge_rows:], "blk", 1)
    extended = jnp.concatenate([before, hidden], axis=0).astype(jnp.float32)
    mixed = depthwise(extended, conv_kernel, row_count, False)
    sigma = jax.nn.sigmoid(mixed)
    out_frames = (mixed * sigma).astype(jnp.bfloat16)[None]
    upstream = cotangent[0].astype(jnp.float32)
    dmixed = upstream * sigma * (1.0 + mixed * (1.0 - sigma))
    after = from_behind(dmixed[:edge_rows].astype(jnp.bfloat16), "blk", -1).astype(jnp.float32)
    dextended = jnp.concatenate([dmixed, after], axis=0)
    dhidden = depthwise(dextended, conv_kernel, row_count, True).astype(jnp.bfloat16)

    def kernel_tap(tap_index):
        window = lax.dynamic_slice_in_dim(extended, edge_rows - tap_index, row_count, 0)
        return jnp.sum(dmixed * window, axis=0)

    kernel_part = lax.map(kernel_tap, jnp.arange(edge_rows + 1, dtype=jnp.int32))
    weight_part = jnp.einsum("ra,rd->ad", flat, dhidden, preferred_element_type=jnp.float32)
    dattended = jnp.einsum(
        "rd,ad->ra", dhidden, out_weight, preferred_element_type=jnp.float32
    ).astype(jnp.bfloat16)
    dout_heads = split_heads(dattended)
    deltas = jnp.einsum("rhe,rhe->hr", dout_heads, attended, preferred_element_type=jnp.float32)
    dquery_own, dkv_own = tile_grads(
        query_heads,
        dout_heads,
        log_sums,
        deltas,
        own_tile,
        own_pos,
        own_pos,
        always,
        left_span,
        score_scale,
    )
    zero_buffer = jnp.zeros((row_count, 2 * ATT), jnp.float32)

    def backward_step(carry, inputs):
        buffer, dquery_sum = carry
        tile, offset = inputs
        tile_pos, tile_usable = source(offset)
        dquery_part, dkv_part = tile_grads(
            query_heads,
            dout_heads,
            log_sums,
            deltas,
            tile,
            own_pos,
            tile_pos,
            tile_usable,
            left_span,
            score_scale,
        )
        arrived = from_behind((buffer + dkv_part).astype(jnp.bfloat16), "blk", -1).astype(
            jnp.float32
        )
        return ((arrived, dquery_sum + dquery_part), None)

    (buffer, dquery_sum), unused = lax.scan(
        backward_step, (zero_buffer, dquery_own), (kept_tiles, offsets), reverse=True
    )
    dkv_total = dkv_own + buffer
    weight_total, kernel_total = sum_weights(weight_part, kernel_part)
    query_grad = dquery_sum.reshape(row_count, ATT).astype(jnp.bfloat16)[None]
    key_grad = dkv_total[:, :ATT].astype(jnp.bfloat16)[None]
    value_grad = dkv_total[:, ATT:].astype(jnp.bfloat16)[None]
    return (out_frames, query_grad, key_grad, value_grad, weight_total, kernel_total)


def solution(mesh):
    return jax.shard_map(
        per_device,
        mesh=mesh,
        in_specs=(
            P("dp", "blk", None),
            P("dp", "blk", None),
            P("dp", "blk", None),
            P(),
            P(),
            P("dp", "blk", None),
        ),
        out_specs=(
            P("dp", "blk", None),
            P("dp", "blk", None),
            P("dp", "blk", None),
            P("dp", "blk", None),
            P(),
            P(),
        ),
        check_vma=False,
    )
```

profile of v0, /device:TPU:1, one launch (start us, length us, event | category | flops | bytes accessed | tf_op | source)
XLA Modules:
  0.0 621.3 jit_solution(3382806898935224929)
XLA Ops:
  12.4 51.5 %while.79 = (s32[]{:T(128)}, bf16[192,1024]{0,1:T(8,128)(2,1)S(1)}, f32[8,192]{1,0:T(8,128)S(1)}, f32[8,192]{1,0:T(8,128)S(1)}, f32[192,8,64]{0,2,1:T(8,128)S(1)...) while((s32[]{:T(128)}, bf16[192,1024]{0,1:T(8,128)(2,1)S(1)}, ...), condition=%wide.region_5.6_spmd.clone, body=%wide.region_2.5_spmd.clone.sunk | while | flops 78537600 | bytes 9227495 | solution.py:161
  12.4 5.5 collective-permute-start
  19.3 7.4 %collective-permute-done = bf16[192,1024]{0,1:T(8,128)(2,1)S(1)} collective-permute-done((bf16[192,1024]{0,1:T(8,128)(2,1)S(1)}, bf16[192,1024]{0,1:T(8,128)(2,1)S(1)}, u32[]{:S(2)}, u32[]{:S(2)}) %collective-permute-start) | collective-permute-done | bytes 393248 | tf_op jit(solution)/shard_map/while/body/eval_jaxpr/ppermute | solution.py:20
  28.9 5.7 collective-permute-start
  36.0 6.6 %collective-permute-done = bf16[192,1024]{0,1:T(8,128)(2,1)S(1)} collective-permute-done((bf16[192,1024]{0,1:T(8,128)(2,1)S(1)}, bf16[192,1024]{0,1:T(8,128)(2,1)S(1)}, u32[]{:S(2)}, u32[]{:S(2)}) %collective-permute-start) | collective-permute-done | bytes 393248 | tf_op jit(solution)/shard_map/while/body/eval_jaxpr/ppermute | solution.py:20
  44.8 8.2 %collective-permute-start = (bf16[192,1024]{0,1:T(8,128)(2,1)S(1)}, bf16[192,1024]{0,1:T(8,128)(2,1)S(1)}, u32[]{:S(2)}, u32[]{:S(2)}) collective-permute-start(bf16[192,1024]{0,1:T(8,128)(2,1)S(1)} %get-tuple-element.1015), channel_id=1, source_target_pairs={{0,1},{1,2},{2,3},{3,4},{4,5},{5,6},{6,7},{7,8},{8,9},{9,10},{10,1... | collective-permute-start | bytes 1179656 | tf_op jit(solution)/shard_map/while/body/eval_jaxpr/ppermute | solution.py:20
  54.4 7.3 %collective-permute-done = bf16[192,1024]{0,1:T(8,128)(2,1)S(1)} collective-permute-done((bf16[192,1024]{0,1:T(8,128)(2,1)S(1)}, bf16[192,1024]{0,1:T(8,128)(2,1)S(1)}, u32[]{:S(2)}, u32[]{:S(2)}) %collective-permute-start) | collective-permute-done | bytes 393248 | tf_op jit(solution)/shard_map/while/body/eval_jaxpr/ppermute | solution.py:20
  64.4 6.5 %collective-permute-start.2 = (bf16[30,1024]{1,0:T(8,128)(2,1)S(1)}, bf16[30,1024]{1,0:T(8,128)(2,1)S(1)}, u32[]{:S(2)}, u32[]{:S(2)}) collective-permute-start(bf16[30,1024]{1,0:T(8,128)(2,1)S(1)} %slice.52), channel_id=1, source_target_pairs={{0,1},{1,2},{2,3},{3,4},{4,5},{5,6},{6,7},{7,8},{8,9},{9,10},{10,1... | collective-permute-start | bytes 184328 | tf_op jit(solution)/shard_map/ppermute | solution.py:20
  73.4 36.2 %while.80 = (s32[]{:T(128)}, f32[192,1024]{1,0:T(8,128)S(1)}, f32[31,1024]{1,0:T(8,128)}, f32[222,1024]{1,0:T(8,128)S(1)}, s32[]{:T(128)}, /*index=5*/s32[]{:T(128)}, s32[]{:T(128)}, s32[]{:T(128)}) while((s32[]{:T(128)}, f32[192,1024]{1,0:T(8,128)S(1)}, f32[31,1024]{1,0:T(8,128)}, f32[222,1024]{1,0:T(8,128)S(1)}, s32[]{:T(128)}, ...), condition=%wide.region_7.8_spmd.clone, body=%wide.region_6.7_spmd.clone.sunk | while | flops 589831 | bytes 2371741 | solution.py:110
  110.5 2.3 fusion.39
  114.1 106.3 %while.78 = (s32[]{:T(128)}, f32[31,1024]{1,0:T(8,128)}, s32[31]{0:T(128)S(1)}, f32[222,1024]{1,0:T(8,128)S(1)}, f32[192,1024]{1,0:T(8,128)S(1)}, /*index=5*/s32[]{:T(128)}, s32[1]{0:T(128)}, s32[]{:T(128)}, s32[1]{0:T(128)}) while((s32[]{:T(128)}, f32[31,1024]{1,0:T(8,128)}, s32[31]{0:T(128)S(1)}, f32[222,1024]{1,0:T(8,128)S(1)}, ...), condition=%wide.region_15.16_spmd, body=%wide.region_13.15_spmd.sunk | while | flops 392198 | bytes 1585319 | solution.py:184
  221.9 71.2 %while.81 = (s32[]{:T(128)}, f32[192,1024]{1,0:T(8,128)S(1)}, f32[31,1024]{1,0:T(8,128)}, f32[222,1024]{1,0:T(8,128)}, s32[]{:T(128)}, /*index=5*/s32[]{:T(128)}) while((s32[]{:T(128)}, f32[192,1024]{1,0:T(8,128)S(1)}, f32[31,1024]{1,0:T(8,128)}, f32[222,1024]{1,0:T(8,128)}, s32[]{:T(128)}, /*index=5*/s32[]{:T(128)}) %tuple.190), condition=%wide.region_9.10_spmd.clone, body=%wide.region_8.9_spmd.clone.sunk | while | flops 589827 | bytes 2371679 | solution.py:110
  222.7 1.5 select_add_fusion.5
  294.0 2.4 convolution_convert_fusion.1
  302.3 1.8 fusion.48
  306.3 61.2 %while.82 = (s32[]{:T(128)}, f32[192,1024]{0,1:T(8,128)S(1)}, f32[192,8,64]{0,2,1:T(8,128)}, s32[3]{0:T(128)S(1)}, s32[]{:T(128)}, /*index=5*/bf16[3,192,1024]{1...) while((s32[]{:T(128)}, f32[192,1024]{0,1:T(8,128)S(1)}, ...), condition=%wide.region_11.12_spmd.clone, body=%wide.region_10.11_spmd.clone.sunk | while | flops 192565632 | bytes 15424801 | solution.py:226
  312.9 2.2 fusion.139
  315.1 12.0 %collective-permute-done.1 = bf16[192,1024]{0,1:T(8,128)(2,1)} collective-permute-done((bf16[192,1024]{0,1:T(8,128)(2,1)}, bf16[192,1024]{0,1:T(8,128)(2,1)}, u32[]{:S(2)}, u32[]{:S(2)}) %collective-permute-start.1) | collective-permute-done | bytes 393248 | tf_op jit(solution)/shard_map/while/body/eval_jaxpr/ppermute | solution.py:20
  334.8 2.2 fusion.139
  336.9 9.8 %collective-permute-done.1 = bf16[192,1024]{0,1:T(8,128)(2,1)} collective-permute-done((bf16[192,1024]{0,1:T(8,128)(2,1)}, bf16[192,1024]{0,1:T(8,128)(2,1)}, u32[]{:S(2)}, u32[]{:S(2)}) %collective-permute-start.1) | collective-permute-done | bytes 393248 | tf_op jit(solution)/shard_map/while/body/eval_jaxpr/ppermute | solution.py:20
  354.4 2.2 fusion.139
  356.6 9.8 %collective-permute-done.1 = bf16[192,1024]{0,1:T(8,128)(2,1)} collective-permute-done((bf16[192,1024]{0,1:T(8,128)(2,1)}, bf16[192,1024]{0,1:T(8,128)(2,1)}, u32[]{:S(2)}, u32[]{:S(2)}) %collective-permute-start.1) | collective-permute-done | bytes 393248 | tf_op jit(solution)/shard_map/while/body/eval_jaxpr/ppermute | solution.py:20
  371.7 238.9 %all-reduce.3.cloned.1.call-done = (f32[512,1024]{1,0:T(8,128)}, f32[31,1024]{1,0:T(8,128)}) async-done(((f32[512,1024]{1,0:T(8,128)}, f32[31,1024]{1,0:T(8,128)}), (f32[512,1024]{1,0:T(8,128)}, f32[31,1024]{1,0:T(8,128)})) %all-reduce.3.cloned.1.call-update) | async-done | bytes 2224144 | tf_op jit(solution)/shard_map/psum | solution.py:114
  610.6 3.2 copy.121
  (371 shorter events, 225.2 us)
Async XLA Ops:
  7.2 56.8 %copy-start = (bf16[512,1024]{1,0:T(8,128)(2,1)S(1)}, bf16[512,1024]{1,0:T(8,128)(2,1)}, u32[]{:S(2)}) copy-start(bf16[512,1024]{1,0:T(8,128)(2,1)} %param.19) | copy-start | bytes 3145732
  7.2 603.4 %all-reduce.3.cloned.1.call-start = ((), (), s32[]{:S(2)}) async-start(), calls=%async_computation | async-start | bytes 4456448 | tf_op jit(solution)/shard_map/psum | solution.py:114
  8.6 3.1 copy-start.10
  11.3 1.1 copy-start.1
  12.4 14.3 %collective-permute-start = (bf16[192,1024]{0,1:T(8,128)(2,1)S(1)}, bf16[192,1024]{0,1:T(8,128)(2,1)S(1)}, u32[]{:S(2)}, u32[]{:S(2)}) collective-permute-start(bf16[192,1024]{0,1:T(8,128)(2,1)S(1)} %get-tuple-element.1015), channel_id=1, source_target_pairs={{0,1},{1,2},{2,3},{3,4},{4,5},{5,6},{6,7},{7,8},{8,9},{9,10},{10,1... | collective-permute-start | bytes 1179656 | tf_op jit(solution)/shard_map/while/body/eval_jaxpr/ppermute | solution.py:20
  28.9 13.7 %collective-permute-start = (bf16[192,1024]{0,1:T(8,128)(2,1)S(1)}, bf16[192,1024]{0,1:T(8,128)(2,1)S(1)}, u32[]{:S(2)}, u32[]{:S(2)}) collective-permute-start(bf16[192,1024]{0,1:T(8,128)(2,1)S(1)} %get-tuple-element.1015), channel_id=1, source_target_pairs={{0,1},{1,2},{2,3},{3,4},{4,5},{5,6},{6,7},{7,8},{8,9},{9,10},{10,1... | collective-permute-start | bytes 1179656 | tf_op jit(solution)/shard_map/while/body/eval_jaxpr/ppermute | solution.py:20
  44.8 16.9 %collective-permute-start = (bf16[192,1024]{0,1:T(8,128)(2,1)S(1)}, bf16[192,1024]{0,1:T(8,128)(2,1)S(1)}, u32[]{:S(2)}, u32[]{:S(2)}) collective-permute-start(bf16[192,1024]{0,1:T(8,128)(2,1)S(1)} %get-tuple-element.1015), channel_id=1, source_target_pairs={{0,1},{1,2},{2,3},{3,4},{4,5},{5,6},{6,7},{7,8},{8,9},{9,10},{10,1... | collective-permute-start | bytes 1179656 | tf_op jit(solution)/shard_map/while/body/eval_jaxpr/ppermute | solution.py:20
  63.9 7.1 %copy-start.7 = (f32[192,8,64]{0,2,1:T(8,128)}, f32[192,8,64]{0,2,1:T(8,128)S(1)}, u32[]{:S(2)}) copy-start(f32[192,8,64]{0,2,1:T(8,128)S(1)} %get-tuple-element.557) | copy-start | bytes 1179652
  64.0 7.1 %copy-start.12 = (bf16[192,8,64]{0,2,1:T(8,128)(2,1)}, bf16[192,8,64]{0,2,1:T(8,128)(2,1)S(1)}, u32[]{:S(2)}) copy-start(bf16[192,8,64]{0,2,1:T(8,128)(2,1)S(1)} %divide_convert_fusion) | copy-start | bytes 589828
  64.4 6.6 %copy-start.15 = (bf16[192,1024]{1,0:T(8,128)(2,1)}, bf16[192,1024]{1,0:T(8,128)(2,1)S(1)}, u32[]{:S(2)}) copy-start(bf16[192,1024]{1,0:T(8,128)(2,1)S(1)} %convolution_convert_fusion) | copy-start | bytes 1179652
  64.4 7.8 %collective-permute-start.2 = (bf16[30,1024]{1,0:T(8,128)(2,1)S(1)}, bf16[30,1024]{1,0:T(8,128)(2,1)S(1)}, u32[]{:S(2)}, u32[]{:S(2)}) collective-permute-start(bf16[30,1024]{1,0:T(8,128)(2,1)S(1)} %slice.52), channel_id=1, source_target_pairs={{0,1},{1,2},{2,3},{3,4},{4,5},{5,6},{6,7},{7,8},{8,9},{9,10},{10,1... | collective-permute-start | bytes 184328 | tf_op jit(solution)/shard_map/ppermute | solution.py:20
  109.6 0.9 copy-start.8
  112.8 107.6 %collective-permute-start.3 = (bf16[30,1024]{1,0:T(8,128)(2,1)S(1)}, bf16[30,1024]{1,0:T(8,128)(2,1)S(1)}, u32[]{:S(2)}, u32[]{:S(2)}) collective-permute-start(bf16[30,1024]{1,0:T(8,128)(2,1)S(1)} %slice.59), channel_id=1, source_target_pairs={{1,0},{2,1},{3,2},{4,3},{5,4},{6,5},{7,6},{8,7},{9,8},{10,9},{11,1... | collective-permute-start | bytes 184328 | tf_op jit(solution)/shard_map/ppermute | solution.py:20
  220.4 1.5 copy-start.3
  294.0 4.7 copy-start.2
  299.8 0.9 copy-start.11
  300.8 1.4 copy-start.5
  300.8 1.4 copy-start.13
  302.3 1.8 copy-start.14
  305.0 1.4 copy-start.6
  311.6 15.4 %collective-permute-start.1 = (bf16[192,1024]{0,1:T(8,128)(2,1)}, bf16[192,1024]{0,1:T(8,128)(2,1)}, u32[]{:S(2)}, u32[]{:S(2)}) collective-permute-start(bf16[192,1024]{0,1:T(8,128)(2,1)} %fusion.138), channel_id=1, source_target_pairs={{1,0},{2,1},{3,2},{4,3},{5,4},{6,5},{7,6},{8,7},{9,8},{10,9},{11,1... | collective-permute-start | bytes 1179656 | tf_op jit(solution)/shard_map/while/body/eval_jaxpr/ppermute | solution.py:20
  333.5 13.2 %collective-permute-start.1 = (bf16[192,1024]{0,1:T(8,128)(2,1)}, bf16[192,1024]{0,1:T(8,128)(2,1)}, u32[]{:S(2)}, u32[]{:S(2)}) collective-permute-start(bf16[192,1024]{0,1:T(8,128)(2,1)} %fusion.138), channel_id=1, source_target_pairs={{1,0},{2,1},{3,2},{4,3},{5,4},{6,5},{7,6},{8,7},{9,8},{10,9},{11,1... | collective-permute-start | bytes 1179656 | tf_op jit(solution)/shard_map/while/body/eval_jaxpr/ppermute | solution.py:20
  353.1 13.2 %collective-permute-start.1 = (bf16[192,1024]{0,1:T(8,128)(2,1)}, bf16[192,1024]{0,1:T(8,128)(2,1)}, u32[]{:S(2)}, u32[]{:S(2)}) collective-permute-start(bf16[192,1024]{0,1:T(8,128)(2,1)} %fusion.138), channel_id=1, source_target_pairs={{1,0},{2,1},{3,2},{4,3},{5,4},{6,5},{7,6},{8,7},{9,8},{10,9},{11,1... | collective-permute-start | bytes 1179656 | tf_op jit(solution)/shard_map/while/body/eval_jaxpr/ppermute | solution.py:20
  610.6 3.2 copy-start.16
  (4 other events, 3.2 us)
Sparse Core Ops, SparseCore 0:
  306.1 304.5 all-reduce.2
where the time goes:
time: 632 us; the launch traced here: 621 us
  waiting for transfers between devices  293 us (46%)
  local copies, waits for them, and re-layouts  134 us (21%)
  other arithmetic  79.2 us (13%)
  loops' own time  46.3 us (7%)
  starting transfers between devices  31.1 us (5%)
  matrix products  23.3 us (4%)
  between operations  14.4 us (2%)
    psum x1, waiting for transfers between devices, sum_weights(): return lax.psum((weight_part, kernel_part), ('dp', 'blk'))  239 us
    add x62, other arithmetic, add_tap(): running + conv_kernel[tap_index] * lax.dynamic_slice_in_dim(extended, fir...  58.3 us
    ppermute x8, waiting for transfers between devices, from_behind(): return lax.ppermute(block, axis, route)  54 us
    dynamic_slice x62, local copies, waits for them, and re-layouts, add_tap(): conv_kernel[tap_index]  47.7 us
    dynamic_update_slice x31, local copies, waits for them, and re-layouts, per_device(): lax.map(kernel_tap, jnp.arange(edge_rows + 1, dtype=jnp.int32))  43.4 us
    another operation x1, loops' own time, per_device(): lax.map(kernel_tap, jnp.arange(edge_rows + 1, dtype=jnp.int32))  40.4 us
    ppermute x8, starting transfers between devices, from_behind(): return lax.ppermute(block, axis, route)  31.1 us
    dynamic_slice x31, local copies, waits for them, and re-layouts, per_device(): lax.map(kernel_tap, jnp.arange(edge_rows + 1, dtype=jnp.int32))  18 us
  transfers between devices with their start and end apart: 9, of which 8 were waited for; matrix products, arithmetic and copies ran while one was open for 15% of the time, Pallas kernels for 0%

commit v1 on v0

v1 whole, which is shorter than its diff:
```python
import math

import jax
import jax.numpy as jnp
from jax import lax
from jax.sharding import PartitionSpec as P

ATT_HEADS = 8
HEAD_DIM = 64
CTX_MAX = 3
ATT = 512


NEGATIVE = -1e30


def from_behind(block, axis, distance):
    devices = range(lax.axis_size(axis))
    route = [(i - distance, i) for i in devices if i - distance in devices]
    return lax.ppermute(block, axis, route)


def split_heads(matrix):
    return matrix.reshape(matrix.shape[0], ATT_HEADS, HEAD_DIM)


def depthwise(extended, conv_kernel, row_count, ahead):
    tap_count = conv_kernel.shape[0]
    total = None
    for tap_index in range(tap_count):
        first_row = tap_index if ahead else tap_count - 1 - tap_index
        term = conv_kernel[tap_index] * extended[first_row:first_row + row_count]
        total = term if total is None else total + term
    return total


def sum_weights(weight_part, kernel_part):
    return lax.psum((weight_part, kernel_part), ("dp", "blk"))


def per_device(queries, key_in, value_in, out_weight, conv_kernel, cotangent):
    cycle_count = lax.axis_size("blk")
    device = lax.axis_index("blk")
    row_count = queries.shape[1]
    context = min(CTX_MAX, cycle_count // 4)
    left_span = context * row_count
    score_scale = 1.0 / math.sqrt(HEAD_DIM)
    edge_rows = conv_kernel.shape[0] - 1
    row_ids = jnp.arange(row_count, dtype=jnp.int32)
    query_heads = split_heads(queries[0])
    own_tile = jnp.concatenate([key_in[0], value_in[0]], axis=1)
    own_pos = device * row_count + row_ids

    offsets = list(range(context, 0, -1))
    window = jnp.concatenate(
        [from_behind(own_tile, "blk", offset) for offset in offsets] + [own_tile], axis=0
    )
    key_pos = jnp.concatenate([(device - offset) * row_count + row_ids for offset in offsets] + [own_pos])
    distance = own_pos[:, None] - key_pos[None, :]
    visible = ((distance >= 0) & (distance < left_span) & (key_pos[None, :] >= 0))[None]
    key_heads = split_heads(window[:, :ATT])
    value_heads = split_heads(window[:, ATT:])

    scores = (
        jnp.einsum("qhd,khd->hqk", query_heads, key_heads, preferred_element_type=jnp.float32)
        * score_scale
    )
    scores = jnp.where(visible, scores, NEGATIVE)
    row_max = jnp.max(scores, axis=-1)
    weights = jnp.where(visible, jnp.exp(scores - row_max[..., None]), 0.0)
    row_sum = jnp.sum(weights, axis=-1)
    weighted = jnp.einsum(
        "hqk,khd->qhd", weights.astype(jnp.bfloat16), value_heads, preferred_element_type=jnp.float32
    )
    attended = (weighted / jnp.transpose(row_sum)[:, :, None]).astype(jnp.bfloat16)
    log_sums = row_max + jnp.log(row_sum)
    flat = attended.reshape(row_count, ATT)

    hidden = jnp.dot(flat, out_weight, preferred_element_type=jnp.float32).astype(jnp.bfloat16)
    before = from_behind(hidden[-edge_rows:], "blk", 1)
    extended = jnp.concatenate([before, hidden], axis=0).astype(jnp.float32)
    mixed = depthwise(extended, conv_kernel, row_count, False)
    sigma = jax.nn.sigmoid(mixed)
    out_frames = (mixed * sigma).astype(jnp.bfloat16)[None]
    upstream = cotangent[0].astype(jnp.float32)
    dmixed = upstream * sigma * (1.0 + mixed * (1.0 - sigma))
    after = from_behind(dmixed[:edge_rows].astype(jnp.bfloat16), "blk", -1).astype(jnp.float32)
    dextended = jnp.concatenate([dmixed, after], axis=0)
    dhidden = depthwise(dextended, conv_kernel, row_count, True).astype(jnp.bfloat16)

    kernel_part = jnp.stack(
        [
            jnp.sum(dmixed * extended[edge_rows - tap:edge_rows - tap + row_count], axis=0)
            for tap in range(edge_rows + 1)
        ]
    )
    weight_part = jnp.einsum("ra,rd->ad", flat, dhidden, preferred_element_type=jnp.float32)
    weight_total, kernel_total = sum_weights(weight_part, kernel_part)

    dattended = jnp.einsum(
        "rd,ad->ra", dhidden, out_weight, preferred_element_type=jnp.float32
    ).astype(jnp.bfloat16)
    dout_heads = split_heads(dattended)
    deltas = jnp.einsum("rhe,rhe->hr", dout_heads, attended, preferred_element_type=jnp.float32)

    probs = jnp.where(visible, jnp.exp(scores - log_sums[..., None]), 0.0)
    dvalue_heads = jnp.einsum(
        "hqk,qhd->khd", probs.astype(jnp.bfloat16), dout_heads, preferred_element_type=jnp.float32
    )
    dprobs = jnp.einsum("qhd,khd->hqk", dout_heads, value_heads, preferred_element_type=jnp.float32)
    dscores = (probs * (dprobs - deltas[..., None])).astype(jnp.bfloat16)
    dquery = (
        jnp.einsum("hqk,khd->qhd", dscores, key_heads, preferred_element_type=jnp.float32)
        * score_scale
    )
    dkey_heads = (
        jnp.einsum("hqk,qhd->khd", dscores, query_heads, preferred_element_type=jnp.float32)
        * score_scale
    )
    window_rows = window.shape[0]
    dkv = jnp.concatenate(
        [dkey_heads.reshape(window_rows, ATT), dvalue_heads.reshape(window_rows, ATT)], axis=1
    )
    dkv_total = dkv[context * row_count:]
    for slot, offset in enumerate(offsets):
        part = dkv[slot * row_count:(slot + 1) * row_count].astype(jnp.bfloat16)
        dkv_total = dkv_total + from_behind(part, "blk", -offset).astype(jnp.float32)

    query_grad = dquery.reshape(row_count, ATT).astype(jnp.bfloat16)[None]
    key_grad = dkv_total[:, :ATT].astype(jnp.bfloat16)[None]
    value_grad = dkv_total[:, ATT:].astype(jnp.bfloat16)[None]
    return (out_frames, query_grad, key_grad, value_grad, weight_total, kernel_total)


def solution(mesh):
    return jax.shard_map(
        per_device,
        mesh=mesh,
        in_specs=(
            P("dp", "blk", None),
            P("dp", "blk", None),
            P("dp", "blk", None),
            P(),
            P(),
            P("dp", "blk", None),
        ),
        out_specs=(
            P("dp", "blk", None),
            P("dp", "blk", None),
            P("dp", "blk", None),
            P("dp", "blk", None),
            P(),
            P(),
        ),
        check_vma=False,
    )
```

time: 632 us -> 424 us (0.67); the launches traced: 621 us -> 422 us
  local copies, waits for them, and re-layouts: 134 us -> 24.2 us
  other arithmetic: 79.2 us -> 23 us
  loops' own time: 46.3 us -> 0 us
  waiting for transfers between devices: 293 us -> 314 us
  matrix products: 23.3 us -> 16.7 us
    dynamic_slice x99 -> x0, local copies, waits for them, and re-layouts: 69.3 us -> none  [the longest x62 47.7 us: add_tap(): conv_kernel[tap_index]]
    add x74 -> x3, other arithmetic: 58.3 us -> 0.62 us  [the longest x1 0.61 us: per_device(): log_sums = row_max + jnp.log(row_sum)]
    another operation x5 -> x0, loops' own time: 46.3 us -> none  [the longest x1 40.4 us: per_device(): lax.map(kernel_tap, jnp.arange(edge_rows + 1, dtype=jnp.int32))]
    dynamic_update_slice x34 -> x0, local copies, waits for them, and re-layouts: 45.9 us -> none  [the longest x31 43.4 us: per_device(): lax.map(kernel_tap, jnp.arange(edge_rows + 1, dtype=jnp.int32))]
    psum x1, waiting for transfers between devices: 239 us -> 267 us  [sum_weights(): return lax.psum((weight_part, kernel_part), ('dp', 'blk'))]
    ppermute x8, waiting for transfers between devices: 54 us -> 46.4 us  [from_behind(): return lax.ppermute(block, axis, route)]
    slice x6, local copies, waits for them, and re-layouts: 0.21 us -> 7.74 us  [the longest x2 3.68 us: depthwise(): term = conv_kernel[tap_index] * extended[first_row:first_row + row_count]]
    dot_general x27 -> x6, matrix products: 18.7 us -> 14 us  [the longest x1 5.07 us: per_device(): jnp.einsum('hqk,qhd->khd', probs.astype(jnp.bfloat16), dout_heads, prefer...]
  transfers between devices with their start and end apart: 9 -> 9, of which waited for: 8 -> 7; matrix products, arithmetic and copies ran while one was open for 15% -> 5% of each run, Pallas kernels for 0% -> 0%
where the time goes in v1:
time: 424 us; the launch traced here: 422 us
  waiting for transfers between devices  314 us (74%)
  starting transfers between devices  29.4 us (7%)
  local copies, waits for them, and re-layouts  24.2 us (6%)
  other arithmetic  23 us (5%)
  matrix products  16.7 us (4%)
  between operations  15.2 us (4%)
    psum x1, waiting for transfers between devices, sum_weights(): return lax.psum((weight_part, kernel_part), ('dp', 'blk'))  267 us
    ppermute x8, waiting for transfers between devices, from_behind(): return lax.ppermute(block, axis, route)  46.4 us
    ppermute x8, starting transfers between devices, from_behind(): return lax.ppermute(block, axis, route)  29.3 us
  transfers between devices with their start and end apart: 9, of which 7 were waited for; matrix products, arithmetic and copies ran while one was open for 5% of the time, Pallas kernels for 0%

profile of v1, /device:TPU:1, one launch (start us, length us, event | category | flops | bytes accessed | tf_op | source)
XLA Modules:
  0.0 422.2 jit_solution(7324746218160545406)
XLA Ops:
  8.4 5.5 %collective-permute-start.2 = (bf16[192,1024]{1,0:T(8,128)(2,1)S(1)}, bf16[192,1024]{1,0:T(8,128)(2,1)S(1)}, u32[]{:S(2)}, u32[]{:S(2)}) collective-permute-start(bf16[192,1024]{1,0:T(8,128)(2,1)S(1)} %pad_maximum_fusion.2), channel_id=1, source_target_pairs={{0,1},{1,2},{2,3},{3,4},{4,5},{5,6},{6,7},{7,8},{8,9},{9,10},{10,1... | collective-permute-start | bytes 1179656 | tf_op jit(solution)/shard_map/ppermute | solution.py:20
  13.9 4.0 collective-permute-start.1
  17.9 5.8 %collective-permute-start = (bf16[192,1024]{1,0:T(8,128)(2,1)S(1)}, bf16[192,1024]{1,0:T(8,128)(2,1)S(1)}, u32[]{:S(2)}, u32[]{:S(2)}) collective-permute-start(bf16[192,1024]{1,0:T(8,128)(2,1)S(1)} %pad_maximum_fusion.2), channel_id=1, source_target_pairs={{0,3},{1,4},{2,5},{3,6},{4,7},{5,8},{6,9},{7,10},{8,11},{9,12},{10... | collective-permute-start | bytes 1179656 | tf_op jit(solution)/shard_map/ppermute | solution.py:20
  25.4 1.9 fusion.130
  27.4 1.8 copy.23
  29.5 4.2 collective-permute-done
  36.5 2.0 fusion.4
  42.3 8.7 %collective-permute-start.3 = (bf16[30,1024]{1,0:T(8,128)(2,1)S(1)}, bf16[30,1024]{1,0:T(8,128)(2,1)S(1)}, u32[]{:S(2)}, u32[]{:S(2)}) collective-permute-start(bf16[30,1024]{1,0:T(8,128)(2,1)S(1)} %slice.478), channel_id=1, source_target_pairs={{0,1},{1,2},{2,3},{3,4},{4,5},{5,6},{6,7},{7,8},{8,9},{9,10},{10,1... | collective-permute-start | bytes 184328 | tf_op jit(solution)/shard_map/ppermute | solution.py:20
  52.8 6.6 %multiply_reduce_fusion = (f32[1024]{0:T(1024)S(1)}, f32[1024]{0:T(1024)S(1)}, f32[1024]{0:T(1024)S(1)}, f32[1024]{0:T(1024)S(1)}, f32[1024]{0:T(1024)S(1)}, /*i...) fusion(f32[222,1024]{1,0:T(8,128)S(1)} %maximum_convert_fusion,, ...), kind=kLoop, calls=%fused_computation.183 | loop fusion | flops 20822016 | bytes 26546176 | tf_op jit(solution)/shard_map/reduce_sum | solution.py:93
  62.2 2.7 stack.127
  66.7 3.8 fusion.25
  73.0 5.1 %fusion.5 = f32[8,64,768]{2,1,0:T(8,128)} fusion(bf16[192,8,64]{0,2,1:T(8,128)(2,1)S(1)} %bitcast.148, f32[8,768,192]{1,2,0:T(8,128)} %copy-done.1, f32[8,192]{1,0:T(8,128)} %log_add_fusion, pred[192,768]{1,0:T(8,128)(4,1)S(1)} %fusion.118), kind=kOutput, calls=%fused_computation.41 | convolution fusion | flops 156893184 | bytes 6641664 | tf_op jit(solution)/shard_map/hqk,qhd->khd/dot_general | solution.py:107
  78.1 2.1 multiply_convert_fusion
  80.3 1.9 convolution_multiply_fusion
  82.1 1.9 copy.25
  84.0 3.1 copy.26
  87.1 2.8 fusion.3
  89.9 2.5 fusion.128
  96.3 2.1 fusion.120
  101.8 12.6 %collective-permute-done.5 = bf16[192,1024]{1,0:T(8,128)(2,1)} collective-permute-done((bf16[192,1024]{1,0:T(8,128)(2,1)}, bf16[192,1024]{1,0:T(8,128)(2,1)}, u32[]{:S(2)}, u32[]{:S(2)}) %collective-permute-start.5) | collective-permute-done | bytes 393248 | tf_op jit(solution)/shard_map/ppermute | solution.py:20
  114.4 4.9 %collective-permute-done.7 = bf16[192,1024]{1,0:T(8,128)(2,1)} collective-permute-done((bf16[192,1024]{1,0:T(8,128)(2,1)}, bf16[192,1024]{1,0:T(8,128)(2,1)}, u32[]{:S(2)}, u32[]{:S(2)}) %collective-permute-start.7) | collective-permute-done | bytes 393248 | tf_op jit(solution)/shard_map/ppermute | solution.py:20
  119.3 22.4 %collective-permute-done.6 = bf16[192,1024]{1,0:T(8,128)(2,1)} collective-permute-done((bf16[192,1024]{1,0:T(8,128)(2,1)}, bf16[192,1024]{1,0:T(8,128)(2,1)}, u32[]{:S(2)}, u32[]{:S(2)}) %collective-permute-start.6) | collective-permute-done | bytes 393248 | tf_op jit(solution)/shard_map/ppermute | solution.py:20
  144.1 267.4 %all-reduce.3.cloned.1.call-done = (f32[512,1024]{1,0:T(8,128)}, f32[31,1024]{1,0:T(8,128)}) async-done(((f32[512,1024]{1,0:T(8,128)}, f32[31,1024]{1,0:T(8,128)}), (f32[512,1024]{1,0:T(8,128)}, f32[31,1024]{1,0:T(8,128)})) %all-reduce.3.cloned.1.call-update) | async-done | bytes 2224144 | tf_op jit(solution)/shard_map/psum | solution.py:38
  411.5 3.2 copy.39
  (160 shorter events, 28.1 us)
Async XLA Ops:
  7.2 34.7 %copy-start = (bf16[512,1024]{1,0:T(8,128)(2,1)S(1)}, bf16[512,1024]{1,0:T(8,128)(2,1)}, u32[]{:S(2)}) copy-start(bf16[512,1024]{1,0:T(8,128)(2,1)} %param.9) | copy-start | bytes 3145732
  7.2 404.3 %all-reduce.3.cloned.1.call-start = ((), (), s32[]{:S(2)}) async-start(), calls=%async_computation | async-start | bytes 4456448 | tf_op jit(solution)/shard_map/psum | solution.py:38
  8.4 21.2 %collective-permute-start.2 = (bf16[192,1024]{1,0:T(8,128)(2,1)S(1)}, bf16[192,1024]{1,0:T(8,128)(2,1)S(1)}, u32[]{:S(2)}, u32[]{:S(2)}) collective-permute-start(bf16[192,1024]{1,0:T(8,128)(2,1)S(1)} %pad_maximum_fusion.2), channel_id=1, source_target_pairs={{0,1},{1,2},{2,3},{3,4},{4,5},{5,6},{6,7},{7,8},{8,9},{9,10},{10,1... | collective-permute-start | bytes 1179656 | tf_op jit(solution)/shard_map/ppermute | solution.py:20
  13.9 15.7 %collective-permute-start.1 = (bf16[192,1024]{1,0:T(8,128)(2,1)S(1)}, bf16[192,1024]{1,0:T(8,128)(2,1)S(1)}, u32[]{:S(2)}, u32[]{:S(2)}) collective-permute-start(bf16[192,1024]{1,0:T(8,128)(2,1)S(1)} %pad_maximum_fusion.2), channel_id=1, source_target_pairs={{0,2},{1,3},{2,4},{3,5},{4,6},{5,7},{6,8},{7,9},{8,10},{9,11},{10,... | collective-permute-start | bytes 1179656 | tf_op jit(solution)/shard_map/ppermute | solution.py:20
  17.9 15.8 %collective-permute-start = (bf16[192,1024]{1,0:T(8,128)(2,1)S(1)}, bf16[192,1024]{1,0:T(8,128)(2,1)S(1)}, u32[]{:S(2)}, u32[]{:S(2)}) collective-permute-start(bf16[192,1024]{1,0:T(8,128)(2,1)S(1)} %pad_maximum_fusion.2), channel_id=1, source_target_pairs={{0,3},{1,4},{2,5},{3,6},{4,7},{5,8},{6,9},{7,10},{8,11},{9,12},{10... | collective-permute-start | bytes 1179656 | tf_op jit(solution)/shard_map/ppermute | solution.py:20
  41.6 10.9 %copy-start.7 = (bf16[1,192,1024]{2,1,0:T(8,128)(2,1)S(1)}, bf16[1,192,1024]{2,1,0:T(8,128)(2,1)}, u32[]{:S(2)}) copy-start(bf16[1,192,1024]{2,1,0:T(8,128)(2,1)} %param.11) | copy-start | bytes 1179652
  41.6 10.9 %copy-start.9 = (f32[1,1024]{1,0:T(1,128)S(1)}, f32[1,1024]{1,0:T(1,128)}, u32[]{:S(2)}) copy-start(f32[1,1024]{1,0:T(1,128)} %get-tuple-element.79) | copy-start | bytes 12292
  41.6 10.9 %copy-start.10 = (f32[1,1024]{1,0:T(1,128)S(1)}, f32[1,1024]{1,0:T(1,128)}, u32[]{:S(2)}) copy-start(f32[1,1024]{1,0:T(1,128)} %get-tuple-element.80) | copy-start | bytes 12292
  41.6 10.9 %copy-start.11 = (f32[1,1024]{1,0:T(1,128)S(1)}, f32[1,1024]{1,0:T(1,128)}, u32[]{:S(2)}) copy-start(f32[1,1024]{1,0:T(1,128)} %get-tuple-element.81) | copy-start | bytes 12292
  41.6 10.9 %copy-start.12 = (f32[1,1024]{1,0:T(1,128)S(1)}, f32[1,1024]{1,0:T(1,128)}, u32[]{:S(2)}) copy-start(f32[1,1024]{1,0:T(1,128)} %get-tuple-element.82) | copy-start | bytes 12292
  41.6 10.9 %copy-start.13 = (f32[1,1024]{1,0:T(1,128)S(1)}, f32[1,1024]{1,0:T(1,128)}, u32[]{:S(2)}) copy-start(f32[1,1024]{1,0:T(1,128)} %get-tuple-element.83) | copy-start | bytes 12292
  41.6 10.9 %copy-start.14 = (f32[1,1024]{1,0:T(1,128)S(1)}, f32[1,1024]{1,0:T(1,128)}, u32[]{:S(2)}) copy-start(f32[1,1024]{1,0:T(1,128)} %get-tuple-element.84) | copy-start | bytes 12292
  41.6 10.9 %copy-start.15 = (f32[1,1024]{1,0:T(1,128)S(1)}, f32[1,1024]{1,0:T(1,128)}, u32[]{:S(2)}) copy-start(f32[1,1024]{1,0:T(1,128)} %get-tuple-element.85) | copy-start | bytes 12292
  41.6 10.9 %copy-start.16 = (f32[1,1024]{1,0:T(1,128)S(1)}, f32[1,1024]{1,0:T(1,128)}, u32[]{:S(2)}) copy-start(f32[1,1024]{1,0:T(1,128)} %get-tuple-element.86) | copy-start | bytes 12292
  41.7 10.9 %copy-start.17 = (f32[1,1024]{1,0:T(1,128)S(1)}, f32[1,1024]{1,0:T(1,128)}, u32[]{:S(2)}) copy-start(f32[1,1024]{1,0:T(1,128)} %get-tuple-element.87) | copy-start | bytes 12292
  41.7 10.9 %copy-start.18 = (f32[1,1024]{1,0:T(1,128)S(1)}, f32[1,1024]{1,0:T(1,128)}, u32[]{:S(2)}) copy-start(f32[1,1024]{1,0:T(1,128)} %get-tuple-element.88) | copy-start | bytes 12292
  41.7 10.9 %copy-start.19 = (f32[1,1024]{1,0:T(1,128)S(1)}, f32[1,1024]{1,0:T(1,128)}, u32[]{:S(2)}) copy-start(f32[1,1024]{1,0:T(1,128)} %get-tuple-element.89) | copy-start | bytes 12292
  41.7 10.9 %copy-start.20 = (f32[1,1024]{1,0:T(1,128)S(1)}, f32[1,1024]{1,0:T(1,128)}, u32[]{:S(2)}) copy-start(f32[1,1024]{1,0:T(1,128)} %get-tuple-element.90) | copy-start | bytes 12292
  41.7 10.9 %copy-start.21 = (f32[1,1024]{1,0:T(1,128)S(1)}, f32[1,1024]{1,0:T(1,128)}, u32[]{:S(2)}) copy-start(f32[1,1024]{1,0:T(1,128)} %get-tuple-element.60) | copy-start | bytes 12292
  42.3 10.0 %collective-permute-start.3 = (bf16[30,1024]{1,0:T(8,128)(2,1)S(1)}, bf16[30,1024]{1,0:T(8,128)(2,1)S(1)}, u32[]{:S(2)}, u32[]{:S(2)}) collective-permute-start(bf16[30,1024]{1,0:T(8,128)(2,1)S(1)} %slice.478), channel_id=1, source_target_pairs={{0,1},{1,2},{2,3},{3,4},{4,5},{5,6},{6,7},{7,8},{8,9},{9,10},{10,1... | collective-permute-start | bytes 184328 | tf_op jit(solution)/shard_map/ppermute | solution.py:20
  59.6 6.8 %collective-permute-start.4 = (bf16[30,1024]{1,0:T(8,128)(2,1)S(1)}, bf16[30,1024]{1,0:T(8,128)(2,1)S(1)}, u32[]{:S(2)}, u32[]{:S(2)}) collective-permute-start(bf16[30,1024]{1,0:T(8,128)(2,1)S(1)} %slice.1049), channel_id=1, source_target_pairs={{1,0},{2,1},{3,2},{4,3},{5,4},{6,5},{7,6},{8,7},{9,8},{10,9},{11,1... | collective-permute-start | bytes 184328 | tf_op jit(solution)/shard_map/ppermute | solution.py:20
  92.4 22.0 %collective-permute-start.5 = (bf16[192,1024]{1,0:T(8,128)(2,1)}, bf16[192,1024]{1,0:T(8,128)(2,1)}, u32[]{:S(2)}, u32[]{:S(2)}) collective-permute-start(bf16[192,1024]{1,0:T(8,128)(2,1)} %get-tuple-element.53), channel_id=1, source_target_pairs={{3,0},{4,1},{5,2},{6,3},{7,4},{8,5},{9,6},{10,7},{11,8},{12,9},{13... | collective-permute-start | bytes 1179656 | tf_op jit(solution)/shard_map/ppermute | solution.py:20
  93.7 25.6 %collective-permute-start.7 = (bf16[192,1024]{1,0:T(8,128)(2,1)}, bf16[192,1024]{1,0:T(8,128)(2,1)}, u32[]{:S(2)}, u32[]{:S(2)}) collective-permute-start(bf16[192,1024]{1,0:T(8,128)(2,1)} %get-tuple-element.54), channel_id=1, source_target_pairs={{1,0},{2,1},{3,2},{4,3},{5,4},{6,5},{7,6},{8,7},{9,8},{10,9},{11,1... | collective-permute-start | bytes 1179656 | tf_op jit(solution)/shard_map/ppermute | solution.py:20
  95.0 46.7 %collective-permute-start.6 = (bf16[192,1024]{1,0:T(8,128)(2,1)}, bf16[192,1024]{1,0:T(8,128)(2,1)}, u32[]{:S(2)}, u32[]{:S(2)}) collective-permute-start(bf16[192,1024]{1,0:T(8,128)(2,1)} %get-tuple-element.55), channel_id=1, source_target_pairs={{2,0},{3,1},{4,2},{5,3},{6,4},{7,5},{8,6},{9,7},{10,8},{11,9},{12,... | collective-permute-start | bytes 1179656 | tf_op jit(solution)/shard_map/ppermute | solution.py:20
  (45 other events, 357.5 us)
Sparse Core Ops, SparseCore 0:
  90.0 321.4 all-reduce.2

commit v2 on v1

--- a/solution.py
+++ b/solution.py
@@ -1,8 +1,11 @@
+import functools
 import math
 
 import jax
 import jax.numpy as jnp
 from jax import lax
+from jax.experimental import pallas as pl
+from jax.experimental.pallas import tpu as pltpu
 from jax.sharding import PartitionSpec as P
 
 ATT_HEADS = 8
@@ -12,6 +15,100 @@
 
 
 NEGATIVE = -1e30
+MESH_ID = pl.DeviceIdType.MESH
+
+
+def reduce_bits(dp_size, blk_size):
+    if dp_size == 4 and blk_size == 128:
+        return [("dp", 1), ("dp", 2), ("blk", 16), ("blk", 2), ("blk", 32),
+                ("blk", 4), ("blk", 64), ("blk", 8), ("blk", 1)]
+    bits = []
+    for axis, size in (("dp", dp_size), ("blk", blk_size)):
+        m = 1
+        while m < size:
+            bits.append((axis, m))
+            m *= 2
+    return bits
+
+
+def allreduce_kernel(bits, n_halve, x_ref, o_ref, *scratch):
+    halves = scratch[:n_halve]
+    doubles = scratch[n_halve:len(bits)]
+    acc, send_sem, recv_sem = scratch[len(bits):]
+    me = {"dp": lax.axis_index("dp"), "blk": lax.axis_index("blk")}
+
+    def partner(axis, m):
+        bit = (me[axis] // m) % 2
+        peer = me[axis] + m - 2 * m * bit
+        ids = (peer, me["blk"]) if axis == "dp" else (me["dp"], peer)
+        return bit, ids
+
+    barrier = pltpu.get_barrier_semaphore()
+    for axis, m in bits:
+        pl.semaphore_signal(barrier, 1, device_id=partner(axis, m)[1], device_id_type=MESH_ID)
+    pl.semaphore_wait(barrier, len(bits))
+
+    offset = 0
+    length = o_ref.shape[0]
+    plan = []
+    for step in range(n_halve):
+        axis, m = bits[step]
+        half = length // 2
+        bit, ids = partner(axis, m)
+        keep = offset + bit * half
+        give = offset + (1 - bit) * half
+        source = x_ref if step == 0 else acc
+        copy = pltpu.make_async_remote_copy(
+            src_ref=source.at[pl.ds(give, half)], dst_ref=halves[step],
+            send_sem=send_sem.at[step], recv_sem=recv_sem.at[step],
+            device_id=ids, device_id_type=MESH_ID)
+        copy.start()
+        copy.wait()
+        acc[pl.ds(keep, half)] = source[pl.ds(keep, half)] + halves[step][...]
+        plan.append((ids, keep, half))
+        offset, length = keep, half
+    for slot, (axis, m) in enumerate(bits[n_halve:]):
+        step = n_halve + slot
+        bit, ids = partner(axis, m)
+        copy = pltpu.make_async_remote_copy(
+            src_ref=acc.at[pl.ds(offset, length)], dst_ref=doubles[slot],
+            send_sem=send_sem.at[step], recv_sem=recv_sem.at[step],
+            device_id=ids, device_id_type=MESH_ID)
+        copy.start()
+        copy.wait()
+        acc[pl.ds(offset, length)] = acc[pl.ds(offset, length)] + doubles[slot][...]
+    o_ref[pl.ds(offset, length)] = acc[pl.ds(offset, length)]
+    for back, (ids, keep, half) in enumerate(reversed(plan)):
+        step = len(bits) + back
+        copy = pltpu.make_async_remote_copy(
+            src_ref=o_ref.at[pl.ds(keep, half)], dst_ref=o_ref.at[pl.ds(keep, half)],
+            send_sem=send_sem.at[step], recv_sem=recv_sem.at[step],
+            device_id=ids, device_id_type=MESH_ID)
+        copy.start()
+        copy.wait()
+
+
+def allreduce(x, dp_size, blk_size, n_halve_max=5):
+    bits = reduce_bits(dp_size, blk_size)
+    rows = x.shape[0]
+    n_halve = 0
+    while n_halve < min(n_halve_max, len(bits)) and rows % (2 ** (n_halve + 1)) == 0:
+        n_halve += 1
+    lengths = [rows // 2 ** (s + 1) for s in range(n_halve)]
+    final = rows // 2 ** n_halve
+    tile = x.shape[1:]
+    scratch = [pltpu.VMEM((n,) + tile, x.dtype) for n in lengths]
+    scratch += [pltpu.VMEM((final,) + tile, x.dtype) for _ in bits[n_halve:]]
+    steps = len(bits) + n_halve
+    scratch += [pltpu.VMEM(x.shape, x.dtype), pltpu.SemaphoreType.DMA((steps,)), pltpu.SemaphoreType.DMA((steps,))]
+    return pl.pallas_call(
+        functools.partial(allreduce_kernel, bits, n_halve),
+        out_shape=jax.ShapeDtypeStruct(x.shape, x.dtype),
+        in_specs=[pl.BlockSpec(memory_space=pltpu.VMEM)],
+        out_specs=pl.BlockSpec(memory_space=pltpu.VMEM),
+        scratch_shapes=scratch,
+        compiler_params=pltpu.CompilerParams(collective_id=0, has_side_effects=True),
+    )(x)
 
 
 def from_behind(block, axis, distance):
@@ -35,7 +132,18 @@
 
 
 def sum_weights(weight_part, kernel_part):
-    return lax.psum((weight_part, kernel_part), ("dp", "blk"))
+    width = weight_part.shape[1]
+    rows = weight_part.shape[0] + kernel_part.shape[0]
+    padded = -(-rows // 32) * 32
+    packed = jnp.concatenate(
+        [weight_part, kernel_part, jnp.zeros((padded - rows, width), jnp.float32)], axis=0
+    )
+    total = allreduce(
+        packed.reshape(padded, 8, width // 8),
+        lax.axis_size("dp"),
+        lax.axis_size("blk"),
+    ).reshape(padded, width)
+    return total[: weight_part.shape[0]], total[weight_part.shape[0] : rows]
 
 
 def per_device(queries, key_in, value_in, out_weight, conv_kernel, cotangent):

time: 424 us -> 242 us (0.57)
  waiting for transfers between devices: 314 us -> 9.22 us
  Pallas kernels: 0 us -> 119 us
  local copies, waits for them, and re-layouts: 24.2 us -> 45.5 us
  between operations: 15.2 us -> 1.86 us
    psum x1 -> x0, waiting for transfers between devices: 267 us -> none  [sum_weights(): return lax.psum((weight_part, kernel_part), ('dp', 'blk'))]
    pallas_call x0 -> x1, Pallas kernels: none -> 119 us  [allreduce(): pl.pallas_call(functools.partial(allreduce_kernel, bits, n_halve), out_sh...]
    ppermute x8, waiting for transfers between devices: 46.4 us -> 9.22 us  [from_behind(): return lax.ppermute(block, axis, route)]
    unnamed x124 -> x193, local copies, waits for them, and re-layouts: 7.89 us -> 30.4 us
  transfers between devices with their start and end apart: 9 -> 8, of which waited for: 7 -> 3; matrix products, arithmetic and copies ran while one was open for 5% -> 17% of each run, Pallas kernels for 0% -> 49%
where the time goes in v2:
time: 242 us; the launch traced here: 241 us
  Pallas kernels  119 us (49%)
  local copies, waits for them, and re-layouts  45.5 us (19%)
  starting transfers between devices  29.3 us (12%)
  other arithmetic  21.2 us (9%)
  matrix products  15.6 us (6%)
  waiting for transfers between devices  9.22 us (4%)
    pallas_call x1, Pallas kernels, allreduce(): pl.pallas_call(functools.partial(allreduce_kernel, bits, n_halve), out_sh...  119 us
    unnamed x193, local copies, waits for them, and re-layouts  30.4 us
    ppermute x8, starting transfers between devices, from_behind(): return lax.ppermute(block, axis, route)  29.3 us
    ppermute x8, waiting for transfers between devices, from_behind(): return lax.ppermute(block, axis, route)  9.22 us
    reduce_sum x2, other arithmetic, per_device(): jnp.sum(dmixed * extended[edge_rows - tap:edge_rows - tap + row_count], a...  8.35 us
    dot_general x1, matrix products, per_device(): jnp.einsum('hqk,qhd->khd', probs.astype(jnp.bfloat16), dout_heads, prefer...  5.1 us
  transfers between devices with their start and end apart: 8, of which 3 were waited for; matrix products, arithmetic and copies ran while one was open for 17% of the time, Pallas kernels for 49%

profile of v2, /device:TPU:1, one launch (start us, length us, event | category | flops | bytes accessed | tf_op | source)
XLA Modules:
  0.0 241.5 jit_solution(583553362399477212)
XLA Ops:
  1.8 5.5 %collective-permute-start.2 = (bf16[192,1024]{1,0:T(8,128)(2,1)S(1)}, bf16[192,1024]{1,0:T(8,128)(2,1)S(1)}, u32[]{:S(2)}, u32[]{:S(2)}) collective-permute-start(bf16[192,1024]{1,0:T(8,128)(2,1)S(1)} %pad_maximum_fusion.2), channel_id=1, source_target_pairs={{0,1},{1,2},{2,3},{3,4},{4,5},{5,6},{6,7},{7,8},{8,9},{9,10},{10,1... | collective-permute-start | bytes 1179656 | tf_op jit(solution)/shard_map/ppermute | solution.py:117
  7.3 4.0 %collective-permute-start.1 = (bf16[192,1024]{1,0:T(8,128)(2,1)S(1)}, bf16[192,1024]{1,0:T(8,128)(2,1)S(1)}, u32[]{:S(2)}, u32[]{:S(2)}) collective-permute-start(bf16[192,1024]{1,0:T(8,128)(2,1)S(1)} %pad_maximum_fusion.2), channel_id=1, source_target_pairs={{0,2},{1,3},{2,4},{3,5},{4,6},{5,7},{6,8},{7,9},{8,10},{9,11},{10,... | collective-permute-start | bytes 1179656 | tf_op jit(solution)/shard_map/ppermute | solution.py:117
  11.3 5.8 %collective-permute-start = (bf16[192,1024]{1,0:T(8,128)(2,1)S(1)}, bf16[192,1024]{1,0:T(8,128)(2,1)S(1)}, u32[]{:S(2)}, u32[]{:S(2)}) collective-permute-start(bf16[192,1024]{1,0:T(8,128)(2,1)S(1)} %pad_maximum_fusion.2), channel_id=1, source_target_pairs={{0,3},{1,4},{2,5},{3,6},{4,7},{5,8},{6,9},{7,10},{8,11},{9,12},{10... | collective-permute-start | bytes 1179656 | tf_op jit(solution)/shard_map/ppermute | solution.py:117
  17.1 1.7 fusion.134
  18.8 2.0 fusion.133
  21.0 1.8 copy.26
  23.1 4.1 %collective-permute-done = bf16[192,1024]{1,0:T(8,128)(2,1)S(1)} collective-permute-done((bf16[192,1024]{1,0:T(8,128)(2,1)S(1)}, bf16[192,1024]{1,0:T(8,128)(2,1)S(1)}, u32[]{:S(2)}, u32[]{:S(2)}) %collective-permute-start) | collective-permute-done | bytes 393248 | tf_op jit(solution)/shard_map/ppermute | solution.py:117
  29.0 2.2 fusion.4
  35.5 8.7 %collective-permute-start.3 = (bf16[30,1024]{1,0:T(8,128)(2,1)S(1)}, bf16[30,1024]{1,0:T(8,128)(2,1)S(1)}, u32[]{:S(2)}, u32[]{:S(2)}) collective-permute-start(bf16[30,1024]{1,0:T(8,128)(2,1)S(1)} %slice.494), channel_id=1, source_target_pairs={{0,1},{1,2},{2,3},{3,4},{4,5},{5,6},{6,7},{7,8},{8,9},{9,10},{10,1... | collective-permute-start | bytes 184328 | tf_op jit(solution)/shard_map/ppermute | solution.py:117
  46.0 6.6 %multiply_reduce_fusion = (f32[1024]{0:T(1024)}, f32[1024]{0:T(1024)}, f32[1024]{0:T(1024)}, f32[1024]{0:T(1024)}, f32[1024]{0:T(1024)}, /*index=5*/f32[1024]{0:...) fusion(f32[222,1024]{1,0:T(8,128)S(1)} %maximum_convert_fusion,, ...), kind=kLoop, calls=%fused_computation.185 | loop fusion | flops 20822016 | bytes 26546176 | tf_op jit(solution)/shard_map/reduce_sum | solution.py:201
  52.7 1.7 multiply_reduce_fusion.18
  56.8 4.4 %collective-permute-done.4 = bf16[30,1024]{1,0:T(8,128)(2,1)S(1)} collective-permute-done((bf16[30,1024]{1,0:T(8,128)(2,1)S(1)}, bf16[30,1024]{1,0:T(8,128)(2,1)S(1)}, u32[]{:S(2)}, u32[]{:S(2)}) %collective-permute-start.4) | collective-permute-done | bytes 61472 | tf_op jit(solution)/shard_map/ppermute | solution.py:117
  61.3 3.8 %fusion.25 = bf16[192,1024]{1,0:T(8,128)(2,1)S(1)} fusion(f32[192,1024]{1,0:T(8,128)S(1)} %get-tuple-element.49, f32[30,1024]{1,0:T(8,128)S(1)} %convert_element_type.74, f32[1024]{0:T(1024)S(1)} %bitcast.229, f32[1024]{0:T(1024)S(1)} %bitcast.231, f32[1024]{0:T(1024)S(1)} %bitcast.235, f32[1024]{0:T(1024)S(1)} %bitcast.237, f32[1024]{0:T(1024)S(1)} %bitcast.239, ...), kind=kLoop, calls=%fused_computation.91 | loop fusion | flops 18087936 | bytes 1429504 | tf_op jit(solution)/shard_map/convert_element_type | solution.py:197
  66.6 5.1 %fusion.5 = f32[8,64,768]{2,1,0:T(8,128)} fusion(bf16[192,8,64]{0,2,1:T(8,128)(2,1)S(1)} %bitcast.197, f32[8,768,192]{1,2,0:T(8,128)} %copy-done.1, f32[8,192]{1,0:T(8,128)S(1)} %copy-done.75, pred[192,768]{1,0:T(8,128)(4,1)S(1)} %fusion.118), kind=kOutput, calls=%fused_computation.41 | convolution fusion | flops 156893184 | bytes 6641664 | tf_op jit(solution)/shard_map/hqk,qhd->khd/dot_general | solution.py:215
  71.8 2.1 multiply_convert_fusion
  73.9 1.9 convolution_multiply_fusion
  75.8 1.9 copy.28
  77.7 3.0 %copy.29 = f32[768,512]{1,0:T(8,128)} copy(f32[768,512]{0,1:T(8,128)} %bitcast.196) | data formatting | bytes 3145728 | tf_op jit(solution)/shard_map/reshape | solution.py:230
  80.7 1.6 fusion.3
  88.0 2.6 %copy_dynamic-update-slice_fusion = f32[544,8,128]{2,1,0:T(8,128)} fusion(f32[512,8,128]{2,0,1:T(8,128)S(1)} %fusion.120), kind=kLoop, calls=%fused_computation.46 | loop fusion | bytes 4194304
  109.6 118.8 %shard_map.109 = f32[544,8,128]{2,1,0:T(8,128)} custom-call(f32[544,8,128]{2,1,0:T(8,128)} %constant_dynamic-update-slice_fusion.x_ref), custom_call_target="tpu_custom_call" | custom-call | tf_op jit(solution)/shard_map/pallas_call | solution.py:104
  228.4 3.2 %slice.488 = f32[512,8,128]{2,1,0:T(8,128)} slice(f32[544,8,128]{2,1,0:T(8,128)} %shard_map.109), slice={[0:512], [0:8], [0:128]} | slice | bytes 4194304 | tf_op jit(solution)/shard_map/slice | solution.py:146
  233.2 1.8 copy.33
  235.0 3.5 %copy.54 = f32[64,8,8,128]{3,1,2,0:T(8,128)} copy(f32[64,8,8,128]{3,2,1,0:T(8,128)} %bitcast.187) | data formatting | bytes 4194304
  (230 shorter events, 41.8 us)
Async XLA Ops:
  0.6 34.5 %copy-start = (bf16[512,1024]{1,0:T(8,128)(2,1)S(1)}, bf16[512,1024]{1,0:T(8,128)(2,1)}, u32[]{:S(2)}) copy-start(bf16[512,1024]{1,0:T(8,128)(2,1)} %param.9) | copy-start | bytes 3145732
  1.8 21.2 %collective-permute-start.2 = (bf16[192,1024]{1,0:T(8,128)(2,1)S(1)}, bf16[192,1024]{1,0:T(8,128)(2,1)S(1)}, u32[]{:S(2)}, u32[]{:S(2)}) collective-permute-start(bf16[192,1024]{1,0:T(8,128)(2,1)S(1)} %pad_maximum_fusion.2), channel_id=1, source_target_pairs={{0,1},{1,2},{2,3},{3,4},{4,5},{5,6},{6,7},{7,8},{8,9},{9,10},{10,1... | collective-permute-start | bytes 1179656 | tf_op jit(solution)/shard_map/ppermute | solution.py:117
  7.3 15.7 %collective-permute-start.1 = (bf16[192,1024]{1,0:T(8,128)(2,1)S(1)}, bf16[192,1024]{1,0:T(8,128)(2,1)S(1)}, u32[]{:S(2)}, u32[]{:S(2)}) collective-permute-start(bf16[192,1024]{1,0:T(8,128)(2,1)S(1)} %pad_maximum_fusion.2), channel_id=1, source_target_pairs={{0,2},{1,3},{2,4},{3,5},{4,6},{5,7},{6,8},{7,9},{8,10},{9,11},{10,... | collective-permute-start | bytes 1179656 | tf_op jit(solution)/shard_map/ppermute | solution.py:117
  11.3 15.8 %collective-permute-start = (bf16[192,1024]{1,0:T(8,128)(2,1)S(1)}, bf16[192,1024]{1,0:T(8,128)(2,1)S(1)}, u32[]{:S(2)}, u32[]{:S(2)}) collective-permute-start(bf16[192,1024]{1,0:T(8,128)(2,1)S(1)} %pad_maximum_fusion.2), channel_id=1, source_target_pairs={{0,3},{1,4},{2,5},{3,6},{4,7},{5,8},{6,9},{7,10},{8,11},{9,12},{10... | collective-permute-start | bytes 1179656 | tf_op jit(solution)/shard_map/ppermute | solution.py:117
  34.8 31.7 %copy-start.8 = (bf16[192,8,64]{0,2,1:T(8,128)(2,1)}, bf16[192,8,64]{0,2,1:T(8,128)(2,1)S(1)}, u32[]{:S(2)}) copy-start(bf16[192,8,64]{0,2,1:T(8,128)(2,1)S(1)} %fusion.18) | copy-start | bytes 589828
  35.5 10.0 %collective-permute-start.3 = (bf16[30,1024]{1,0:T(8,128)(2,1)S(1)}, bf16[30,1024]{1,0:T(8,128)(2,1)S(1)}, u32[]{:S(2)}, u32[]{:S(2)}) collective-permute-start(bf16[30,1024]{1,0:T(8,128)(2,1)S(1)} %slice.494), channel_id=1, source_target_pairs={{0,1},{1,2},{2,3},{3,4},{4,5},{5,6},{6,7},{7,8},{8,9},{9,10},{10,1... | collective-permute-start | bytes 184328 | tf_op jit(solution)/shard_map/ppermute | solution.py:117
  54.4 6.8 %collective-permute-start.4 = (bf16[30,1024]{1,0:T(8,128)(2,1)S(1)}, bf16[30,1024]{1,0:T(8,128)(2,1)S(1)}, u32[]{:S(2)}, u32[]{:S(2)}) collective-permute-start(bf16[30,1024]{1,0:T(8,128)(2,1)S(1)} %slice.1065), channel_id=1, source_target_pairs={{1,0},{2,1},{3,2},{4,3},{5,4},{6,5},{7,6},{8,7},{9,8},{10,9},{11,1... | collective-permute-start | bytes 184328 | tf_op jit(solution)/shard_map/ppermute | solution.py:117
  83.4 155.8 %collective-permute-start.5 = (bf16[192,1024]{1,0:T(8,128)(2,1)}, bf16[192,1024]{1,0:T(8,128)(2,1)}, u32[]{:S(2)}, u32[]{:S(2)}) collective-permute-start(bf16[192,1024]{1,0:T(8,128)(2,1)} %get-tuple-element.51), channel_id=1, source_target_pairs={{3,0},{4,1},{5,2},{6,3},{7,4},{8,5},{9,6},{10,7},{11,8},{12,9},{13... | collective-permute-start | bytes 1179656 | tf_op jit(solution)/shard_map/ppermute | solution.py:117
  84.7 154.5 %collective-permute-start.7 = (bf16[192,1024]{1,0:T(8,128)(2,1)}, bf16[192,1024]{1,0:T(8,128)(2,1)}, u32[]{:S(2)}, u32[]{:S(2)}) collective-permute-start(bf16[192,1024]{1,0:T(8,128)(2,1)} %get-tuple-element.52), channel_id=1, source_target_pairs={{1,0},{2,1},{3,2},{4,3},{5,4},{6,5},{7,6},{8,7},{9,8},{10,9},{11,1... | collective-permute-start | bytes 1179656 | tf_op jit(solution)/shard_map/ppermute | solution.py:117
  86.0 153.2 %collective-permute-start.6 = (bf16[192,1024]{1,0:T(8,128)(2,1)}, bf16[192,1024]{1,0:T(8,128)(2,1)}, u32[]{:S(2)}, u32[]{:S(2)}) collective-permute-start(bf16[192,1024]{1,0:T(8,128)(2,1)} %get-tuple-element.53), channel_id=1, source_target_pairs={{2,0},{3,1},{4,2},{5,3},{6,4},{7,5},{8,6},{9,7},{10,8},{11,9},{12,... | collective-permute-start | bytes 1179656 | tf_op jit(solution)/shard_map/ppermute | solution.py:117
  87.9 12.8 %copy-start.70 = (f32[1024]{0:T(1024)S(1)}, f32[1024]{0:T(1024)}, u32[]{:S(2)}) copy-start(f32[1024]{0:T(1024)} %get-tuple-element.31) | copy-start | bytes 12292
  87.9 13.4 %copy-start.69 = (f32[1024]{0:T(1024)S(1)}, f32[1024]{0:T(1024)}, u32[]{:S(2)}) copy-start(f32[1024]{0:T(1024)} %get-tuple-element.30) | copy-start | bytes 12292
  87.9 14.0 %copy-start.68 = (f32[1024]{0:T(1024)S(1)}, f32[1024]{0:T(1024)}, u32[]{:S(2)}) copy-start(f32[1024]{0:T(1024)} %get-tuple-element.29) | copy-start | bytes 12292
  87.9 14.5 %copy-start.67 = (f32[1024]{0:T(1024)S(1)}, f32[1024]{0:T(1024)}, u32[]{:S(2)}) copy-start(f32[1024]{0:T(1024)} %get-tuple-element.28) | copy-start | bytes 12292
  87.9 15.1 %copy-start.66 = (f32[1024]{0:T(1024)S(1)}, f32[1024]{0:T(1024)}, u32[]{:S(2)}) copy-start(f32[1024]{0:T(1024)} %get-tuple-element.27) | copy-start | bytes 12292
  87.9 15.7 %copy-start.65 = (f32[1024]{0:T(1024)S(1)}, f32[1024]{0:T(1024)}, u32[]{:S(2)}) copy-start(f32[1024]{0:T(1024)} %get-tuple-element.26) | copy-start | bytes 12292
  88.0 16.3 %copy-start.64 = (f32[1024]{0:T(1024)S(1)}, f32[1024]{0:T(1024)}, u32[]{:S(2)}) copy-start(f32[1024]{0:T(1024)} %get-tuple-element.25) | copy-start | bytes 12292
  88.0 16.9 %copy-start.63 = (f32[1024]{0:T(1024)S(1)}, f32[1024]{0:T(1024)}, u32[]{:S(2)}) copy-start(f32[1024]{0:T(1024)} %get-tuple-element.24) | copy-start | bytes 12292
  88.0 17.5 %copy-start.62 = (f32[1024]{0:T(1024)S(1)}, f32[1024]{0:T(1024)}, u32[]{:S(2)}) copy-start(f32[1024]{0:T(1024)} %get-tuple-element.23) | copy-start | bytes 12292
  88.0 18.1 %copy-start.61 = (f32[1024]{0:T(1024)S(1)}, f32[1024]{0:T(1024)}, u32[]{:S(2)}) copy-start(f32[1024]{0:T(1024)} %get-tuple-element.22) | copy-start | bytes 12292
  88.0 18.6 %copy-start.60 = (f32[1024]{0:T(1024)S(1)}, f32[1024]{0:T(1024)}, u32[]{:S(2)}) copy-start(f32[1024]{0:T(1024)} %get-tuple-element.21) | copy-start | bytes 12292
  88.0 19.2 %copy-start.59 = (f32[1024]{0:T(1024)S(1)}, f32[1024]{0:T(1024)}, u32[]{:S(2)}) copy-start(f32[1024]{0:T(1024)} %get-tuple-element.20) | copy-start | bytes 12292
  88.0 19.8 %copy-start.58 = (f32[1024]{0:T(1024)S(1)}, f32[1024]{0:T(1024)}, u32[]{:S(2)}) copy-start(f32[1024]{0:T(1024)} %get-tuple-element.19) | copy-start | bytes 12292
  88.0 20.4 %copy-start.57 = (f32[1024]{0:T(1024)S(1)}, f32[1024]{0:T(1024)}, u32[]{:S(2)}) copy-start(f32[1024]{0:T(1024)} %get-tuple-element.18) | copy-start | bytes 12292
  (63 other events, 536.9 us)

commit v3 on v2

--- a/solution.py
+++ b/solution.py
@@ -186,22 +186,23 @@
 
     hidden = jnp.dot(flat, out_weight, preferred_element_type=jnp.float32).astype(jnp.bfloat16)
     before = from_behind(hidden[-edge_rows:], "blk", 1)
-    extended = jnp.concatenate([before, hidden], axis=0).astype(jnp.float32)
-    mixed = depthwise(extended, conv_kernel, row_count, False)
-    sigma = jax.nn.sigmoid(mixed)
-    out_frames = (mixed * sigma).astype(jnp.bfloat16)[None]
-    upstream = cotangent[0].astype(jnp.float32)
-    dmixed = upstream * sigma * (1.0 + mixed * (1.0 - sigma))
-    after = from_behind(dmixed[:edge_rows].astype(jnp.bfloat16), "blk", -1).astype(jnp.float32)
-    dextended = jnp.concatenate([dmixed, after], axis=0)
-    dhidden = depthwise(dextended, conv_kernel, row_count, True).astype(jnp.bfloat16)
-
-    kernel_part = jnp.stack(
-        [
-            jnp.sum(dmixed * extended[edge_rows - tap:edge_rows - tap + row_count], axis=0)
-            for tap in range(edge_rows + 1)
-        ]
-    )
+    following = from_behind(
+        jnp.concatenate([hidden[:edge_rows], cotangent[0][:edge_rows]], axis=1), "blk", -1
+    )
+    width = hidden.shape[1]
+    extended = jnp.concatenate([before, hidden, following[:, :width]], axis=0).astype(jnp.float32)
+    mixed_all = depthwise(extended, conv_kernel, row_count + edge_rows, False)
+    sigma_all = jax.nn.sigmoid(mixed_all)
+    upstream = jnp.concatenate([cotangent[0], following[:, width:]], axis=0).astype(jnp.float32)
+    dmixed_all = upstream * sigma_all * (1.0 + mixed_all * (1.0 - sigma_all))
+    out_frames = (mixed_all[:row_count] * sigma_all[:row_count]).astype(jnp.bfloat16)[None]
+    dmixed = dmixed_all[:row_count]
+    dhidden = depthwise(dmixed_all, conv_kernel, row_count, True).astype(jnp.bfloat16)
+
+    windows = jnp.stack(
+        [extended[edge_rows - tap:edge_rows - tap + row_count] for tap in range(edge_rows + 1)]
+    )
+    kernel_part = jnp.sum(windows * dmixed[None], axis=1)
     weight_part = jnp.einsum("ra,rd->ad", flat, dhidden, preferred_element_type=jnp.float32)
     weight_total, kernel_total = sum_weights(weight_part, kernel_part)
 

time: 242 us -> 262 us (1.083)
  local copies, waits for them, and re-layouts: 45.5 us -> 58.6 us
  other arithmetic: 21.2 us -> 31.2 us
  waiting for transfers between devices: 9.22 us -> 3.61 us
  matrix products: 15.6 us -> 18.7 us
    unnamed x193 -> x138, local copies, waits for them, and re-layouts: 30.4 us -> 38.2 us
    ppermute x8, waiting for transfers between devices: 9.22 us -> 3.61 us  [from_behind(): return lax.ppermute(block, axis, route)]
    mul x0 -> x1, other arithmetic: none -> 4.65 us  [per_device(): dmixed_all = upstream * sigma_all * (1.0 + mixed_all * (1.0 - sigma_all))]
    reduce_sum x2 -> x1, other arithmetic: 8.35 us -> 10.4 us  [per_device(): kernel_part = jnp.sum(windows * dmixed[None], axis=1)]
  transfers between devices with their start and end apart: 8 -> 8, of which waited for: 3 -> 2; matrix products, arithmetic and copies ran while one was open for 17% -> 23% of each run, Pallas kernels for 49% -> 45%
where the time goes in v3:
time: 262 us; the launch traced here: 261 us
  Pallas kernels  117 us (45%)
  local copies, waits for them, and re-layouts  58.6 us (22%)
  other arithmetic  31.2 us (12%)
  starting transfers between devices  30.2 us (12%)
  matrix products  18.7 us (7%)
  waiting for transfers between devices  3.61 us (1%)
    pallas_call x1, Pallas kernels, allreduce(): pl.pallas_call(functools.partial(allreduce_kernel, bits, n_halve), out_sh...  117 us
    unnamed x138, local copies, waits for them, and re-layouts  38.2 us
    ppermute x8, starting transfers between devices, from_behind(): return lax.ppermute(block, axis, route)  30.2 us
    reduce_sum x1, other arithmetic, per_device(): kernel_part = jnp.sum(windows * dmixed[None], axis=1)  10.4 us
  transfers between devices with their start and end apart: 8, of which 2 were waited for; matrix products, arithmetic and copies ran while one was open for 23% of the time, Pallas kernels for 45%

profile of v3, /device:TPU:1, one launch (start us, length us, event | category | flops | bytes accessed | tf_op | source)
XLA Modules:
  0.0 260.7 jit_solution(7338776482704517127)
XLA Ops:
  1.8 5.5 %collective-permute-start.2 = (bf16[192,1024]{1,0:T(8,128)(2,1)S(1)}, bf16[192,1024]{1,0:T(8,128)(2,1)S(1)}, u32[]{:S(2)}, u32[]{:S(2)}) collective-permute-start(bf16[192,1024]{1,0:T(8,128)(2,1)S(1)} %pad_maximum_fusion.1), channel_id=1, source_target_pairs={{0,1},{1,2},{2,3},{3,4},{4,5},{5,6},{6,7},{7,8},{8,9},{9,10},{10,1... | collective-permute-start | bytes 1179656 | tf_op jit(solution)/shard_map/ppermute | solution.py:117
  7.3 4.0 %collective-permute-start.1 = (bf16[192,1024]{1,0:T(8,128)(2,1)S(1)}, bf16[192,1024]{1,0:T(8,128)(2,1)S(1)}, u32[]{:S(2)}, u32[]{:S(2)}) collective-permute-start(bf16[192,1024]{1,0:T(8,128)(2,1)S(1)} %pad_maximum_fusion.1), channel_id=1, source_target_pairs={{0,2},{1,3},{2,4},{3,5},{4,6},{5,7},{6,8},{7,9},{8,10},{9,11},{10,... | collective-permute-start | bytes 1179656 | tf_op jit(solution)/shard_map/ppermute | solution.py:117
  11.3 5.8 %collective-permute-start = (bf16[192,1024]{1,0:T(8,128)(2,1)S(1)}, bf16[192,1024]{1,0:T(8,128)(2,1)S(1)}, u32[]{:S(2)}, u32[]{:S(2)}) collective-permute-start(bf16[192,1024]{1,0:T(8,128)(2,1)S(1)} %pad_maximum_fusion.1), channel_id=1, source_target_pairs={{0,3},{1,4},{2,5},{3,6},{4,7},{5,8},{6,9},{7,10},{8,11},{9,12},{10... | collective-permute-start | bytes 1179656 | tf_op jit(solution)/shard_map/ppermute | solution.py:117
  17.1 1.7 fusion.134
  18.8 1.9 fusion.133
  24.3 2.8 %collective-permute-done = bf16[192,1024]{1,0:T(8,128)(2,1)S(1)} collective-permute-done((bf16[192,1024]{1,0:T(8,128)(2,1)S(1)}, bf16[192,1024]{1,0:T(8,128)(2,1)S(1)}, u32[]{:S(2)}, u32[]{:S(2)}) %collective-permute-start) | collective-permute-done | bytes 393248 | tf_op jit(solution)/shard_map/ppermute | solution.py:117
  35.9 9.5 %collective-permute-start.3 = (bf16[30,1024]{1,0:T(8,128)(2,1)S(1)}, bf16[30,1024]{1,0:T(8,128)(2,1)S(1)}, u32[]{:S(2)}, u32[]{:S(2)}) collective-permute-start(bf16[30,1024]{1,0:T(8,128)(2,1)S(1)} %get-tuple-element.27), channel_id=1, source_target_pairs={{0,1},{1,2},{2,3},{3,4},{4,5},{5,6},{6,7},{7,8},{8,9},{9,10},{10,1... | collective-permute-start | bytes 184328 | tf_op jit(solution)/shard_map/ppermute | solution.py:117
  47.3 4.7 %add_multiply_fusion = (f32[222,1024]{1,0:T(8,128)S(1)}, f32[222,1024]{1,0:T(8,128)}) fusion(bf16[30,1024]{1,0:T(8,128)(2,1)S(1)} %get-tuple-element.61, bf16[192,1024]{1,0:T(8,128)(2,1)S(1)} %bitcast.261, f32[252,1024]{1,0:T(8,128)S(1)} %maximum_convert_fusion, f32[1024]{0:T(1024)S(1)} %bitcast.284, f32[1024]{0:T(1024)S(1)} %bitcast.286, ...), kind=kLoop, calls=%fused_computation.89 | loop fusion | flops 16594944 | bytes 30588928 | tf_op jit(solution)/shard_map/mul | solution.py:197
  52.0 3.0 %fusion.88 = bf16[192,1024]{1,0:T(8,128)(2,1)S(1)} fusion(f32[222,1024]{1,0:T(8,128)S(1)} %get-tuple-element.18, f32[1024]{0:T(1024)S(1)} %bitcast.285, f32[1024]{0:T(1024)S(1)} %bitcast.287, f32[1024]{0:T(1024)S(1)} %bitcast.291, f32[1024]{0:T(1024)S(1)} %bitcast.293, f32[1024]{0:T(1024)S(1)} %bitcast.295, f32[1024]{0:T(1024)S(1)} %bitcast.297, ...), kind=kLoop, calls=%fused_computation.162 | loop fusion | flops 12189696 | bytes 24899584 | tf_op jit(solution)/shard_map/convert_element_type | solution.py:200
  58.4 4.6 %multiply_convert_fusion = bf16[8,192,768]{2,1,0:T(8,128)(2,1)S(1)} fusion(f32[8,768,192]{1,2,0:T(8,128)} %copy-done.2, f32[8,192]{1,0:T(8,128)S(1)} %fusion.121, f32[8,192]{1,0:T(8,128)} %log_add_fusion, pred[192,768]{1,0:T(8,128)(4,1)S(1)} %fusion.120, bf16[192,8,64]{0,2,1:T(8,128)(2,1)} %bitcast.252, bf16[768,8,64]{0,2,1:T(8,128)(2,1)} %bitcast.255), kind=kOutput, calls=%fused_computation.2 | convolution fusion | flops 159252480 | bytes 8220672 | tf_op jit(solution)/shard_map/qhd,khd->hqk/dot_general | solution.py:219
  63.1 1.6 fusion.14
  64.7 1.7 convolution_multiply_fusion
  66.4 5.0 %fusion.5 = f32[8,64,768]{2,1,0:T(8,128)} fusion(bf16[192,8,64]{0,2,1:T(8,128)(2,1)S(1)} %bitcast.253, f32[8,768,192]{1,2,0:T(8,128)} %copy-done.2, f32[8,192]{1,0:T(8,128)S(1)} %copy-done.50, pred[192,768]{1,0:T(8,128)(4,1)S(1)} %fusion.120), kind=kOutput, calls=%fused_computation.13 | convolution fusion | flops 156893184 | bytes 6641664 | tf_op jit(solution)/shard_map/hqk,qhd->khd/dot_general | solution.py:216
  72.5 1.8 fusion.136
  74.2 3.1 %copy.25 = f32[768,512]{1,0:T(8,128)} copy(f32[768,512]{0,1:T(8,128)} %bitcast.245) | data formatting | bytes 3145728 | tf_op jit(solution)/shard_map/reshape | solution.py:231
  77.3 3.0 %copy.26 = f32[768,512]{1,0:T(8,128)} copy(f32[768,512]{0,1:T(8,128)} %bitcast.251) | data formatting | bytes 3145728 | tf_op jit(solution)/shard_map/reshape | solution.py:231
  80.3 2.1 fusion.3
  86.0 1.5 collective-permute-start.5
  116.7 10.4 %multiply_reduce_fusion = f32[31,1024]{1,0:T(8,128)S(1)} fusion(f32[31,192,1024]{2,1,0:T(8,128)} %fusion.56, f32[192,1024]{1,0:T(8,128)S(1)} %slice.652), kind=kLoop, calls=%fused_computation | loop fusion | flops 12157952 | bytes 25292800 | tf_op jit(solution)/shard_map/reduce_sum | solution.py:205
  129.4 1.9 copy.37
  131.3 116.8 %shard_map.109 = f32[544,8,128]{2,1,0:T(8,128)} custom-call(f32[544,8,128]{2,1,0:T(8,128)} %bitcast.241), custom_call_target="tpu_custom_call" | custom-call | tf_op jit(solution)/shard_map/pallas_call | solution.py:104
  248.1 3.1 %slice.609 = f32[512,8,128]{2,1,0:T(8,128)} slice(f32[544,8,128]{2,1,0:T(8,128)} %shard_map.109), slice={[0:512], [0:8], [0:128]} | slice | bytes 4194304 | tf_op jit(solution)/shard_map/slice | solution.py:146
  252.0 3.5 %copy.41 = f32[64,8,8,128]{3,1,2,0:T(8,128)} copy(f32[64,8,8,128]{3,2,1,0:T(8,128)} %bitcast.242) | data formatting | bytes 4194304
  256.2 2.2 fusion.122
  (179 shorter events, 58.0 us)
Async XLA Ops:
  0.6 33.5 %copy-start = (bf16[512,1024]{1,0:T(8,128)(2,1)S(1)}, bf16[512,1024]{1,0:T(8,128)(2,1)}, u32[]{:S(2)}) copy-start(bf16[512,1024]{1,0:T(8,128)(2,1)} %param.9) | copy-start | bytes 3145732
  1.8 22.5 %collective-permute-start.2 = (bf16[192,1024]{1,0:T(8,128)(2,1)S(1)}, bf16[192,1024]{1,0:T(8,128)(2,1)S(1)}, u32[]{:S(2)}, u32[]{:S(2)}) collective-permute-start(bf16[192,1024]{1,0:T(8,128)(2,1)S(1)} %pad_maximum_fusion.1), channel_id=1, source_target_pairs={{0,1},{1,2},{2,3},{3,4},{4,5},{5,6},{6,7},{7,8},{8,9},{9,10},{10,1... | collective-permute-start | bytes 1179656 | tf_op jit(solution)/shard_map/ppermute | solution.py:117
  7.3 17.0 %collective-permute-start.1 = (bf16[192,1024]{1,0:T(8,128)(2,1)S(1)}, bf16[192,1024]{1,0:T(8,128)(2,1)S(1)}, u32[]{:S(2)}, u32[]{:S(2)}) collective-permute-start(bf16[192,1024]{1,0:T(8,128)(2,1)S(1)} %pad_maximum_fusion.1), channel_id=1, source_target_pairs={{0,2},{1,3},{2,4},{3,5},{4,6},{5,7},{6,8},{7,9},{8,10},{9,11},{10,... | collective-permute-start | bytes 1179656 | tf_op jit(solution)/shard_map/ppermute | solution.py:117
  11.3 15.8 %collective-permute-start = (bf16[192,1024]{1,0:T(8,128)(2,1)S(1)}, bf16[192,1024]{1,0:T(8,128)(2,1)S(1)}, u32[]{:S(2)}, u32[]{:S(2)}) collective-permute-start(bf16[192,1024]{1,0:T(8,128)(2,1)S(1)} %pad_maximum_fusion.1), channel_id=1, source_target_pairs={{0,3},{1,4},{2,5},{3,6},{4,7},{5,8},{6,9},{7,10},{8,11},{9,12},{10... | collective-permute-start | bytes 1179656 | tf_op jit(solution)/shard_map/ppermute | solution.py:117
  32.4 14.6 %copy-start.16 = (bf16[1,192,1024]{2,1,0:T(8,128)(2,1)S(1)}, bf16[1,192,1024]{2,1,0:T(8,128)(2,1)}, u32[]{:S(2)}) copy-start(bf16[1,192,1024]{2,1,0:T(8,128)(2,1)} %param.11) | copy-start | bytes 1179652
  32.4 14.6 %copy-start.18 = (f32[1,1024]{1,0:T(1,128)S(1)}, f32[1,1024]{1,0:T(1,128)}, u32[]{:S(2)}) copy-start(f32[1,1024]{1,0:T(1,128)} %get-tuple-element.48) | copy-start | bytes 12292
  32.5 14.6 %copy-start.19 = (f32[1,1024]{1,0:T(1,128)S(1)}, f32[1,1024]{1,0:T(1,128)}, u32[]{:S(2)}) copy-start(f32[1,1024]{1,0:T(1,128)} %get-tuple-element.49) | copy-start | bytes 12292
  32.5 14.6 %copy-start.20 = (f32[1,1024]{1,0:T(1,128)S(1)}, f32[1,1024]{1,0:T(1,128)}, u32[]{:S(2)}) copy-start(f32[1,1024]{1,0:T(1,128)} %get-tuple-element.50) | copy-start | bytes 12292
  32.5 14.6 %copy-start.21 = (f32[1,1024]{1,0:T(1,128)S(1)}, f32[1,1024]{1,0:T(1,128)}, u32[]{:S(2)}) copy-start(f32[1,1024]{1,0:T(1,128)} %get-tuple-element.51) | copy-start | bytes 12292
  32.5 14.6 %copy-start.22 = (f32[1,1024]{1,0:T(1,128)S(1)}, f32[1,1024]{1,0:T(1,128)}, u32[]{:S(2)}) copy-start(f32[1,1024]{1,0:T(1,128)} %get-tuple-element.52) | copy-start | bytes 12292
  32.5 14.6 %copy-start.23 = (f32[1,1024]{1,0:T(1,128)S(1)}, f32[1,1024]{1,0:T(1,128)}, u32[]{:S(2)}) copy-start(f32[1,1024]{1,0:T(1,128)} %get-tuple-element.53) | copy-start | bytes 12292
  32.5 14.6 %copy-start.24 = (f32[1,1024]{1,0:T(1,128)S(1)}, f32[1,1024]{1,0:T(1,128)}, u32[]{:S(2)}) copy-start(f32[1,1024]{1,0:T(1,128)} %get-tuple-element.54) | copy-start | bytes 12292
  32.5 14.6 %copy-start.25 = (f32[1,1024]{1,0:T(1,128)S(1)}, f32[1,1024]{1,0:T(1,128)}, u32[]{:S(2)}) copy-start(f32[1,1024]{1,0:T(1,128)} %get-tuple-element.55) | copy-start | bytes 12292
  32.5 14.6 %copy-start.26 = (f32[1,1024]{1,0:T(1,128)S(1)}, f32[1,1024]{1,0:T(1,128)}, u32[]{:S(2)}) copy-start(f32[1,1024]{1,0:T(1,128)} %get-tuple-element.56) | copy-start | bytes 12292
  32.5 14.6 %copy-start.27 = (f32[1,1024]{1,0:T(1,128)S(1)}, f32[1,1024]{1,0:T(1,128)}, u32[]{:S(2)}) copy-start(f32[1,1024]{1,0:T(1,128)} %get-tuple-element.57) | copy-start | bytes 12292
  32.5 14.6 %copy-start.28 = (f32[1,1024]{1,0:T(1,128)S(1)}, f32[1,1024]{1,0:T(1,128)}, u32[]{:S(2)}) copy-start(f32[1,1024]{1,0:T(1,128)} %get-tuple-element.58) | copy-start | bytes 12292
  32.6 14.6 %copy-start.29 = (f32[1,1024]{1,0:T(1,128)S(1)}, f32[1,1024]{1,0:T(1,128)}, u32[]{:S(2)}) copy-start(f32[1,1024]{1,0:T(1,128)} %get-tuple-element.59) | copy-start | bytes 12292
  32.6 14.6 %copy-start.30 = (f32[1,1024]{1,0:T(1,128)S(1)}, f32[1,1024]{1,0:T(1,128)}, u32[]{:S(2)}) copy-start(f32[1,1024]{1,0:T(1,128)} %get-tuple-element.29) | copy-start | bytes 12292
  34.6 11.5 %collective-permute-start.4 = (bf16[30,2048]{1,0:T(8,128)(2,1)S(1)}, bf16[30,2048]{1,0:T(8,128)(2,1)S(1)}, u32[]{:S(2)}, u32[]{:S(2)}) collective-permute-start(bf16[30,2048]{1,0:T(8,128)(2,1)S(1)} %pad_maximum_fusion.2), channel_id=1, source_target_pairs={{1,0},{2,1},{3,2},{4,3},{5,4},{6,5},{7,6},{8,7},{9,8},{10,9},{11,1... | collective-permute-start | bytes 368648 | tf_op jit(solution)/shard_map/ppermute | solution.py:117
  35.9 10.9 %collective-permute-start.3 = (bf16[30,1024]{1,0:T(8,128)(2,1)S(1)}, bf16[30,1024]{1,0:T(8,128)(2,1)S(1)}, u32[]{:S(2)}, u32[]{:S(2)}) collective-permute-start(bf16[30,1024]{1,0:T(8,128)(2,1)S(1)} %get-tuple-element.27), channel_id=1, source_target_pairs={{0,1},{1,2},{2,3},{3,4},{4,5},{5,6},{6,7},{7,8},{8,9},{9,10},{10,1... | collective-permute-start | bytes 184328 | tf_op jit(solution)/shard_map/ppermute | solution.py:117
  83.4 175.0 %collective-permute-start.7 = (bf16[192,1024]{1,0:T(8,128)(2,1)}, bf16[192,1024]{1,0:T(8,128)(2,1)S(1)}, u32[]{:S(2)}, u32[]{:S(2)}) collective-permute-start(bf16[192,1024]{1,0:T(8,128)(2,1)} %get-tuple-element.21), channel_id=1, source_target_pairs={{1,0},{2,1},{3,2},{4,3},{5,4},{6,5},{7,6},{8,7},{9,8},{10,9},{11,1... | collective-permute-start | bytes 1179656 | tf_op jit(solution)/shard_map/ppermute | solution.py:117
  84.7 173.8 %collective-permute-start.6 = (bf16[192,1024]{1,0:T(8,128)(2,1)}, bf16[192,1024]{1,0:T(8,128)(2,1)}, u32[]{:S(2)}, u32[]{:S(2)}) collective-permute-start(bf16[192,1024]{1,0:T(8,128)(2,1)} %get-tuple-element.22), channel_id=1, source_target_pairs={{2,0},{3,1},{4,2},{5,3},{6,4},{7,5},{8,6},{9,7},{10,8},{11,9},{12,... | collective-permute-start | bytes 1179656 | tf_op jit(solution)/shard_map/ppermute | solution.py:117
  86.0 172.5 %collective-permute-start.5 = (bf16[192,1024]{1,0:T(8,128)(2,1)S(1)}, bf16[192,1024]{1,0:T(8,128)(2,1)}, u32[]{:S(2)}, u32[]{:S(2)}) collective-permute-start(bf16[192,1024]{1,0:T(8,128)(2,1)S(1)} %get-tuple-element.20), channel_id=1, source_target_pairs={{3,0},{4,1},{5,2},{6,3},{7,4},{8,5},{9,6},{10,7},{11,8},{12,9},{13... | collective-permute-start | bytes 1179656 | tf_op jit(solution)/shard_map/ppermute | solution.py:117
  131.3 119.9 %copy-start.14 = (bf16[8,64,192]{2,1,0:T(8,128)(2,1)S(1)}, bf16[8,64,192]{2,1,0:T(8,128)(2,1)}, u32[]{:S(2)}) copy-start(bf16[8,64,192]{2,1,0:T(8,128)(2,1)} %fusion.14) | copy-start | bytes 589828
  (36 other events, 362.5 us)

commit v4 on v3

--- a/solution.py
+++ b/solution.py
@@ -131,19 +131,37 @@
     return total
 
 
-def sum_weights(weight_part, kernel_part):
+def kernel_taps_body(tap_count, dmixed_ref, extended_ref, out_ref):
+    rows = dmixed_ref.shape[0]
+    first = tap_count - 1
+    grads = dmixed_ref[...]
+    for tap in range(tap_count):
+        window = extended_ref[pl.ds(first - tap, rows), :]
+        out_ref[pl.ds(tap, 1), :] = jnp.sum(grads * window, axis=0, keepdims=True)
+    out_ref[pl.ds(tap_count, out_ref.shape[0] - tap_count), :] = jnp.zeros(
+        (out_ref.shape[0] - tap_count, out_ref.shape[1]), jnp.float32
+    )
+
+
+def kernel_taps(dmixed, extended, tap_count):
+    padded = -(-tap_count // 8) * 8
+    return pl.pallas_call(
+        functools.partial(kernel_taps_body, tap_count),
+        out_shape=jax.ShapeDtypeStruct((padded, dmixed.shape[1]), jnp.float32),
+        in_specs=[pl.BlockSpec(memory_space=pltpu.VMEM)] * 2,
+        out_specs=pl.BlockSpec(memory_space=pltpu.VMEM),
+    )(dmixed, extended)
+
+
+def sum_weights(weight_part, kernel_part, kernel_rows):
     width = weight_part.shape[1]
     rows = weight_part.shape[0] + kernel_part.shape[0]
-    padded = -(-rows // 32) * 32
-    packed = jnp.concatenate(
-        [weight_part, kernel_part, jnp.zeros((padded - rows, width), jnp.float32)], axis=0
-    )
+    packed = jnp.concatenate([weight_part, kernel_part], axis=0)
     total = allreduce(
-        packed.reshape(padded, 8, width // 8),
-        lax.axis_size("dp"),
-        lax.axis_size("blk"),
-    ).reshape(padded, width)
-    return total[: weight_part.shape[0]], total[weight_part.shape[0] : rows]
+        packed.reshape(rows, 8, width // 8), lax.axis_size("dp"), lax.axis_size("blk")
+    ).reshape(rows, width)
+    start = weight_part.shape[0]
+    return total[:start], total[start:start + kernel_rows]
 
 
 def per_device(queries, key_in, value_in, out_weight, conv_kernel, cotangent):
@@ -199,12 +217,9 @@
     dmixed = dmixed_all[:row_count]
     dhidden = depthwise(dmixed_all, conv_kernel, row_count, True).astype(jnp.bfloat16)
 
-    windows = jnp.stack(
-        [extended[edge_rows - tap:edge_rows - tap + row_count] for tap in range(edge_rows + 1)]
-    )
-    kernel_part = jnp.sum(windows * dmixed[None], axis=1)
+    kernel_part = kernel_taps(dmixed, extended[: row_count + edge_rows], edge_rows + 1)
     weight_part = jnp.einsum("ra,rd->ad", flat, dhidden, preferred_element_type=jnp.float32)
-    weight_total, kernel_total = sum_weights(weight_part, kernel_part)
+    weight_total, kernel_total = sum_weights(weight_part, kernel_part, edge_rows + 1)
 
     dattended = jnp.einsum(
         "rd,ad->ra", dhidden, out_weight, preferred_element_type=jnp.float32

time: 262 us -> 227 us (0.87)
  local copies, waits for them, and re-layouts: 58.6 us -> 31 us
  other arithmetic: 31.2 us -> 19.8 us
  waiting for transfers between devices: 3.61 us -> 8.48 us
    unnamed x138 -> x102, local copies, waits for them, and re-layouts: 38.2 us -> 8.4 us
    reduce_sum x1 -> x0, other arithmetic: 10.4 us -> none  [per_device(): kernel_part = jnp.sum(windows * dmixed[None], axis=1)]
    pallas_call x0 -> x1, Pallas kernels: none -> 6.65 us  [kernel_taps(): pl.pallas_call(functools.partial(kernel_taps_body, tap_count), out_shape=...]
    ppermute x8, waiting for transfers between devices: 3.61 us -> 8.48 us  [from_behind(): return lax.ppermute(block, axis, route)]
    pallas_call x1, Pallas kernels: 117 us -> 113 us  [allreduce(): pl.pallas_call(functools.partial(allreduce_kernel, bits, n_halve), out_sh...]
    slice x3 -> x4, local copies, waits for them, and re-layouts: 3.65 us -> 5.84 us  [depthwise(): term = conv_kernel[tap_index] * extended[first_row:first_row + row_count]]
  transfers between devices with their start and end apart: 8 -> 8, of which waited for: 2 -> 2; matrix products, arithmetic and copies ran while one was open for 23% -> 9% of each run, Pallas kernels for 45% -> 53%
where the time goes in v4:
time: 227 us; the launch traced here: 226 us
  Pallas kernels  119 us (52%)
  local copies, waits for them, and re-layouts  31 us (14%)
  starting transfers between devices  29.5 us (13%)
  other arithmetic  19.8 us (9%)
  matrix products  16.4 us (7%)
  waiting for transfers between devices  8.48 us (4%)
    pallas_call x1, Pallas kernels, allreduce(): pl.pallas_call(functools.partial(allreduce_kernel, bits, n_halve), out_sh...  113 us
    ppermute x8, starting transfers between devices, from_behind(): return lax.ppermute(block, axis, route)  29.5 us
    ppermute x8, waiting for transfers between devices, from_behind(): return lax.ppermute(block, axis, route)  8.48 us
    unnamed x102, local copies, waits for them, and re-layouts  8.4 us
    pallas_call x1, Pallas kernels, kernel_taps(): pl.pallas_call(functools.partial(kernel_taps_body, tap_count), out_shape=...  6.65 us
    slice x4, local copies, waits for them, and re-layouts, depthwise(): term = conv_kernel[tap_index] * extended[first_row:first_row + row_count]  5.84 us
    dot_general x1, matrix products, per_device(): jnp.einsum('hqk,qhd->khd', probs.astype(jnp.bfloat16), dout_heads, prefer...  5.18 us
  transfers between devices with their start and end apart: 8, of which 2 were waited for; matrix products, arithmetic and copies ran while one was open for 9% of the time, Pallas kernels for 53%

profile of v4, /device:TPU:1, one launch (start us, length us, event | category | flops | bytes accessed | tf_op | source)
XLA Modules:
  0.0 225.8 jit_solution(2800204739014624722)
XLA Ops:
  1.8 5.5 %collective-permute-start.2 = (bf16[192,1024]{1,0:T(8,128)(2,1)S(1)}, bf16[192,1024]{1,0:T(8,128)(2,1)S(1)}, u32[]{:S(2)}, u32[]{:S(2)}) collective-permute-start(bf16[192,1024]{1,0:T(8,128)(2,1)S(1)} %pad_maximum_fusion.1), channel_id=1, source_target_pairs={{0,1},{1,2},{2,3},{3,4},{4,5},{5,6},{6,7},{7,8},{8,9},{9,10},{10,1... | collective-permute-start | bytes 1179656 | tf_op jit(solution)/shard_map/ppermute | solution.py:117
  7.3 4.0 %collective-permute-start.1 = (bf16[192,1024]{1,0:T(8,128)(2,1)S(1)}, bf16[192,1024]{1,0:T(8,128)(2,1)S(1)}, u32[]{:S(2)}, u32[]{:S(2)}) collective-permute-start(bf16[192,1024]{1,0:T(8,128)(2,1)S(1)} %pad_maximum_fusion.1), channel_id=1, source_target_pairs={{0,2},{1,3},{2,4},{3,5},{4,6},{5,7},{6,8},{7,9},{8,10},{9,11},{10,... | collective-permute-start | bytes 1179656 | tf_op jit(solution)/shard_map/ppermute | solution.py:117
  11.3 5.8 %collective-permute-start = (bf16[192,1024]{1,0:T(8,128)(2,1)S(1)}, bf16[192,1024]{1,0:T(8,128)(2,1)S(1)}, u32[]{:S(2)}, u32[]{:S(2)}) collective-permute-start(bf16[192,1024]{1,0:T(8,128)(2,1)S(1)} %pad_maximum_fusion.1), channel_id=1, source_target_pairs={{0,3},{1,4},{2,5},{3,6},{4,7},{5,8},{6,9},{7,10},{8,11},{9,12},{10... | collective-permute-start | bytes 1179656 | tf_op jit(solution)/shard_map/ppermute | solution.py:117
  17.1 1.7 fusion.103
  18.8 2.0 fusion.102
  23.8 3.3 %collective-permute-done = bf16[192,1024]{1,0:T(8,128)(2,1)S(1)} collective-permute-done((bf16[192,1024]{1,0:T(8,128)(2,1)S(1)}, bf16[192,1024]{1,0:T(8,128)(2,1)S(1)}, u32[]{:S(2)}, u32[]{:S(2)}) %collective-permute-start) | collective-permute-done | bytes 393248 | tf_op jit(solution)/shard_map/ppermute | solution.py:117
  36.8 8.7 %collective-permute-start.3 = (bf16[30,1024]{1,0:T(8,128)(2,1)S(1)}, bf16[30,1024]{1,0:T(8,128)(2,1)S(1)}, u32[]{:S(2)}, u32[]{:S(2)}) collective-permute-start(bf16[30,1024]{1,0:T(8,128)(2,1)S(1)} %get-tuple-element.27), channel_id=1, source_target_pairs={{0,1},{1,2},{2,3},{3,4},{4,5},{5,6},{6,7},{7,8},{8,9},{9,10},{10,1... | collective-permute-start | bytes 184328 | tf_op jit(solution)/shard_map/ppermute | solution.py:117
  47.6 5.1 %collective-permute-done.4 = bf16[30,2048]{1,0:T(8,128)(2,1)S(1)} collective-permute-done((bf16[30,2048]{1,0:T(8,128)(2,1)S(1)}, bf16[30,2048]{1,0:T(8,128)(2,1)S(1)}, u32[]{:S(2)}, u32[]{:S(2)}) %collective-permute-start.4) | collective-permute-done | bytes 122912 | tf_op jit(solution)/shard_map/ppermute | solution.py:117
  54.2 3.9 %add_multiply_fusion = (f32[222,1024]{1,0:T(8,128)S(1)}, f32[222,1024]{1,0:T(8,128)S(1)}) fusion(bf16[30,1024]{1,0:T(8,128)(2,1)S(1)} %get-tuple-element.61, bf16[192,1024]{1,0:T(8,128)(2,1)S(1)} %bitcast.138, f32[252,1024]{1,0:T(8,128)S(1)} %maximum_convert_fusion, f32[1024]{0:T(1024)S(1)} %bitcast.161, f32[1024]{0:T(1024)S(1)} %bitcast.163, ...), kind=kLoop, calls=%fused_computation.87 | loop fusion | flops 16594944 | bytes 30588928 | tf_op jit(solution)/shard_map/mul | solution.py:215
  58.1 3.1 %fusion.57 = bf16[192,1024]{1,0:T(8,128)(2,1)S(1)} fusion(f32[222,1024]{1,0:T(8,128)S(1)} %get-tuple-element.18, f32[1024]{0:T(1024)S(1)} %bitcast.162, f32[1024]{0:T(1024)S(1)} %bitcast.164, f32[1024]{0:T(1024)S(1)} %bitcast.168, f32[1024]{0:T(1024)S(1)} %bitcast.170, f32[1024]{0:T(1024)S(1)} %bitcast.172, f32[1024]{0:T(1024)S(1)} %bitcast.174, ...), kind=kLoop, calls=%fused_computation.98 | loop fusion | flops 12189696 | bytes 24899584 | tf_op jit(solution)/shard_map/convert_element_type | solution.py:218
  63.5 1.8 copy.24
  66.5 5.2 %fusion.5 = f32[8,64,768]{2,1,0:T(8,128)} fusion(bf16[192,8,64]{0,2,1:T(8,128)(2,1)} %bitcast.129, f32[8,768,192]{1,2,0:T(8,128)} %copy-done.1, f32[8,192]{1,0:T(8,128)S(1)} %copy-done.45, pred[192,768]{1,0:T(8,128)(4,1)} %copy-done.10), kind=kOutput, calls=%fused_computation.12 | convolution fusion | flops 156893184 | bytes 6641664 | tf_op jit(solution)/shard_map/hqk,qhd->khd/dot_general | solution.py:231
  71.7 2.1 multiply_convert_fusion
  75.4 1.7 convolution_multiply_fusion
  77.2 1.7 fusion.105
  80.1 1.9 copy.25
  82.0 3.0 %copy.26 = f32[768,512]{1,0:T(8,128)} copy(f32[768,512]{0,1:T(8,128)} %bitcast.128) | data formatting | bytes 3145728 | tf_op jit(solution)/shard_map/reshape | solution.py:246
  85.0 1.6 fusion.3
  91.8 6.7 %shard_map.109 = f32[32,1024]{1,0:T(8,128)} custom-call(f32[192,1024]{1,0:T(8,128)} %slice.529.dmixed_ref, f32[222,1024]{1,0:T(8,128)} %slice.525.extended_ref), custom_call_target="tpu_custom_call" | custom-call | tf_op jit(solution)/shard_map/pallas_call | solution.py:148
  98.5 1.8 maximum_bitcast_fusion
  100.3 1.8 copy.37
  102.1 112.5 %shard_map.110 = f32[544,8,128]{2,1,0:T(8,128)} custom-call(f32[544,8,128]{2,1,0:T(8,128)} %bitcast.118), custom_call_target="tpu_custom_call" | custom-call | tf_op jit(solution)/shard_map/pallas_call | solution.py:104
  214.7 3.1 %slice.486 = f32[512,8,128]{2,1,0:T(8,128)} slice(f32[544,8,128]{2,1,0:T(8,128)} %shard_map.110), slice={[0:512], [0:8], [0:128]} | slice | bytes 4194304 | tf_op jit(solution)/shard_map/slice | solution.py:164
  218.6 3.5 %copy.41 = f32[64,8,8,128]{3,1,2,0:T(8,128)} copy(f32[64,8,8,128]{3,2,1,0:T(8,128)} %bitcast.119) | data formatting | bytes 4194304
  (143 shorter events, 32.6 us)
Async XLA Ops:
  0.6 35.7 %copy-start = (bf16[512,1024]{1,0:T(8,128)(2,1)S(1)}, bf16[512,1024]{1,0:T(8,128)(2,1)}, u32[]{:S(2)}) copy-start(bf16[512,1024]{1,0:T(8,128)(2,1)} %param.9) | copy-start | bytes 3145732
  1.8 22.0 %collective-permute-start.2 = (bf16[192,1024]{1,0:T(8,128)(2,1)S(1)}, bf16[192,1024]{1,0:T(8,128)(2,1)S(1)}, u32[]{:S(2)}, u32[]{:S(2)}) collective-permute-start(bf16[192,1024]{1,0:T(8,128)(2,1)S(1)} %pad_maximum_fusion.1), channel_id=1, source_target_pairs={{0,1},{1,2},{2,3},{3,4},{4,5},{5,6},{6,7},{7,8},{8,9},{9,10},{10,1... | collective-permute-start | bytes 1179656 | tf_op jit(solution)/shard_map/ppermute | solution.py:117
  7.3 16.5 %collective-permute-start.1 = (bf16[192,1024]{1,0:T(8,128)(2,1)S(1)}, bf16[192,1024]{1,0:T(8,128)(2,1)S(1)}, u32[]{:S(2)}, u32[]{:S(2)}) collective-permute-start(bf16[192,1024]{1,0:T(8,128)(2,1)S(1)} %pad_maximum_fusion.1), channel_id=1, source_target_pairs={{0,2},{1,3},{2,4},{3,5},{4,6},{5,7},{6,8},{7,9},{8,10},{9,11},{10,... | collective-permute-start | bytes 1179656 | tf_op jit(solution)/shard_map/ppermute | solution.py:117
  11.3 15.8 %collective-permute-start = (bf16[192,1024]{1,0:T(8,128)(2,1)S(1)}, bf16[192,1024]{1,0:T(8,128)(2,1)S(1)}, u32[]{:S(2)}, u32[]{:S(2)}) collective-permute-start(bf16[192,1024]{1,0:T(8,128)(2,1)S(1)} %pad_maximum_fusion.1), channel_id=1, source_target_pairs={{0,3},{1,4},{2,5},{3,6},{4,7},{5,8},{6,9},{7,10},{8,11},{9,12},{10... | collective-permute-start | bytes 1179656 | tf_op jit(solution)/shard_map/ppermute | solution.py:117
  36.0 17.9 %copy-start.8 = (bf16[192,8,64]{0,2,1:T(8,128)(2,1)}, bf16[192,8,64]{0,2,1:T(8,128)(2,1)S(1)}, u32[]{:S(2)}) copy-start(bf16[192,8,64]{0,2,1:T(8,128)(2,1)S(1)} %fusion.18) | copy-start | bytes 589828
  36.0 17.9 %copy-start.16 = (bf16[1,192,1024]{2,1,0:T(8,128)(2,1)S(1)}, bf16[1,192,1024]{2,1,0:T(8,128)(2,1)}, u32[]{:S(2)}) copy-start(bf16[1,192,1024]{2,1,0:T(8,128)(2,1)} %param.11) | copy-start | bytes 1179652
  36.1 17.9 %copy-start.18 = (f32[1,1024]{1,0:T(1,128)S(1)}, f32[1,1024]{1,0:T(1,128)}, u32[]{:S(2)}) copy-start(f32[1,1024]{1,0:T(1,128)} %get-tuple-element.52) | copy-start | bytes 12292
  36.1 17.9 %copy-start.19 = (f32[1,1024]{1,0:T(1,128)S(1)}, f32[1,1024]{1,0:T(1,128)}, u32[]{:S(2)}) copy-start(f32[1,1024]{1,0:T(1,128)} %get-tuple-element.53) | copy-start | bytes 12292
  36.1 17.9 %copy-start.20 = (f32[1,1024]{1,0:T(1,128)S(1)}, f32[1,1024]{1,0:T(1,128)}, u32[]{:S(2)}) copy-start(f32[1,1024]{1,0:T(1,128)} %get-tuple-element.54) | copy-start | bytes 12292
  36.1 17.9 %copy-start.21 = (f32[1,1024]{1,0:T(1,128)S(1)}, f32[1,1024]{1,0:T(1,128)}, u32[]{:S(2)}) copy-start(f32[1,1024]{1,0:T(1,128)} %get-tuple-element.55) | copy-start | bytes 12292
  36.1 17.9 %copy-start.22 = (f32[1,1024]{1,0:T(1,128)S(1)}, f32[1,1024]{1,0:T(1,128)}, u32[]{:S(2)}) copy-start(f32[1,1024]{1,0:T(1,128)} %get-tuple-element.56) | copy-start | bytes 12292
  36.1 17.9 %copy-start.23 = (f32[1,1024]{1,0:T(1,128)S(1)}, f32[1,1024]{1,0:T(1,128)}, u32[]{:S(2)}) copy-start(f32[1,1024]{1,0:T(1,128)} %get-tuple-element.57) | copy-start | bytes 12292
  36.1 17.9 %copy-start.24 = (f32[1,1024]{1,0:T(1,128)S(1)}, f32[1,1024]{1,0:T(1,128)}, u32[]{:S(2)}) copy-start(f32[1,1024]{1,0:T(1,128)} %get-tuple-element.58) | copy-start | bytes 12292
  36.1 17.9 %copy-start.25 = (f32[1,1024]{1,0:T(1,128)S(1)}, f32[1,1024]{1,0:T(1,128)}, u32[]{:S(2)}) copy-start(f32[1,1024]{1,0:T(1,128)} %get-tuple-element.59) | copy-start | bytes 12292
  36.1 17.9 %copy-start.26 = (f32[1,1024]{1,0:T(1,128)S(1)}, f32[1,1024]{1,0:T(1,128)}, u32[]{:S(2)}) copy-start(f32[1,1024]{1,0:T(1,128)} %get-tuple-element.29) | copy-start | bytes 12292
  36.1 17.9 %copy-start.27 = (f32[1,1024]{1,0:T(1,128)S(1)}, f32[1,1024]{1,0:T(1,128)}, u32[]{:S(2)}) copy-start(f32[1,1024]{1,0:T(1,128)} %get-tuple-element.30) | copy-start | bytes 12292
  36.2 17.9 %copy-start.28 = (f32[1,1024]{1,0:T(1,128)S(1)}, f32[1,1024]{1,0:T(1,128)}, u32[]{:S(2)}) copy-start(f32[1,1024]{1,0:T(1,128)} %get-tuple-element.31) | copy-start | bytes 12292
  36.2 17.9 %copy-start.29 = (f32[1,1024]{1,0:T(1,128)S(1)}, f32[1,1024]{1,0:T(1,128)}, u32[]{:S(2)}) copy-start(f32[1,1024]{1,0:T(1,128)} %get-tuple-element.32) | copy-start | bytes 12292
  36.8 16.0 %collective-permute-start.3 = (bf16[30,1024]{1,0:T(8,128)(2,1)S(1)}, bf16[30,1024]{1,0:T(8,128)(2,1)S(1)}, u32[]{:S(2)}, u32[]{:S(2)}) collective-permute-start(bf16[30,1024]{1,0:T(8,128)(2,1)S(1)} %get-tuple-element.27), channel_id=1, source_target_pairs={{0,1},{1,2},{2,3},{3,4},{4,5},{5,6},{6,7},{7,8},{8,9},{9,10},{10,1... | collective-permute-start | bytes 184328 | tf_op jit(solution)/shard_map/ppermute | solution.py:117
  45.5 7.2 %collective-permute-start.4 = (bf16[30,2048]{1,0:T(8,128)(2,1)S(1)}, bf16[30,2048]{1,0:T(8,128)(2,1)S(1)}, u32[]{:S(2)}, u32[]{:S(2)}) collective-permute-start(bf16[30,2048]{1,0:T(8,128)(2,1)S(1)} %pad_maximum_fusion.2), channel_id=1, source_target_pairs={{1,0},{2,1},{3,2},{4,3},{5,4},{6,5},{7,6},{8,7},{9,8},{10,9},{11,1... | collective-permute-start | bytes 368648 | tf_op jit(solution)/shard_map/ppermute | solution.py:117
  58.1 20.8 %copy-start.3 = (f32[222,1024]{1,0:T(8,128)}, f32[222,1024]{1,0:T(8,128)S(1)}, u32[]{:S(2)}) copy-start(f32[222,1024]{1,0:T(8,128)S(1)} %get-tuple-element.19) | copy-start | bytes 2727940
  87.7 136.0 %collective-permute-start.5 = (bf16[192,1024]{1,0:T(8,128)(2,1)}, bf16[192,1024]{1,0:T(8,128)(2,1)S(1)}, u32[]{:S(2)}, u32[]{:S(2)}) collective-permute-start(bf16[192,1024]{1,0:T(8,128)(2,1)} %get-tuple-element.20), channel_id=1, source_target_pairs={{3,0},{4,1},{5,2},{6,3},{7,4},{8,5},{9,6},{10,7},{11,8},{12,9},{13... | collective-permute-start | bytes 1179656 | tf_op jit(solution)/shard_map/ppermute | solution.py:117
  89.0 134.7 %collective-permute-start.7 = (bf16[192,1024]{1,0:T(8,128)(2,1)}, bf16[192,1024]{1,0:T(8,128)(2,1)}, u32[]{:S(2)}, u32[]{:S(2)}) collective-permute-start(bf16[192,1024]{1,0:T(8,128)(2,1)} %get-tuple-element.21), channel_id=1, source_target_pairs={{1,0},{2,1},{3,2},{4,3},{5,4},{6,5},{7,6},{8,7},{9,8},{10,9},{11,1... | collective-permute-start | bytes 1179656 | tf_op jit(solution)/shard_map/ppermute | solution.py:117
  90.3 133.4 %collective-permute-start.6 = (bf16[192,1024]{1,0:T(8,128)(2,1)}, bf16[192,1024]{1,0:T(8,128)(2,1)}, u32[]{:S(2)}, u32[]{:S(2)}) collective-permute-start(bf16[192,1024]{1,0:T(8,128)(2,1)} %get-tuple-element.22), channel_id=1, source_target_pairs={{2,0},{3,1},{4,2},{5,3},{6,4},{7,5},{8,6},{9,7},{10,8},{11,9},{12,... | collective-permute-start | bytes 1179656 | tf_op jit(solution)/shard_map/ppermute | solution.py:117
  (33 other events, 357.9 us)

commit v5 on v4

--- a/solution.py
+++ b/solution.py
@@ -20,13 +20,16 @@
 
 def reduce_bits(dp_size, blk_size):
     if dp_size == 4 and blk_size == 128:
-        return [("dp", 1), ("dp", 2), ("blk", 16), ("blk", 2), ("blk", 32),
-                ("blk", 4), ("blk", 64), ("blk", 8), ("blk", 1)]
+        core0 = [("dp", 1), ("dp", 2), ("blk", 16), ("blk", 2), ("blk", 32),
+                 ("blk", 4), ("blk", 64), ("blk", 8), ("blk", 1)]
+        core1 = [("dp", 1), ("blk", 16), ("dp", 2), ("blk", 32), ("blk", 2),
+                 ("blk", 64), ("blk", 4), ("blk", 1), ("blk", 8)]
+        return list(zip(core0, core1))
     bits = []
     for axis, size in (("dp", dp_size), ("blk", blk_size)):
         m = 1
         while m < size:
-            bits.append((axis, m))
+            bits.append(((axis, m), (axis, m)))
             m *= 2
     return bits
 
@@ -37,24 +40,32 @@
     acc, send_sem, recv_sem = scratch[len(bits):]
     me = {"dp": lax.axis_index("dp"), "blk": lax.axis_index("blk")}
 
-    def partner(axis, m):
+    core = me["dp"] % 2
+
+    def one_partner(axis, m):
         bit = (me[axis] // m) % 2
         peer = me[axis] + m - 2 * m * bit
         ids = (peer, me["blk"]) if axis == "dp" else (me["dp"], peer)
         return bit, ids
 
+    def partner(specs):
+        bit0, ids0 = one_partner(*specs[0])
+        bit1, ids1 = one_partner(*specs[1])
+        bit = bit0 + (bit1 - bit0) * core
+        ids = tuple(a + (b - a) * core for a, b in zip(ids0, ids1))
+        return bit, ids
+
     barrier = pltpu.get_barrier_semaphore()
-    for axis, m in bits:
-        pl.semaphore_signal(barrier, 1, device_id=partner(axis, m)[1], device_id_type=MESH_ID)
+    for specs in bits:
+        pl.semaphore_signal(barrier, 1, device_id=partner(specs)[1], device_id_type=MESH_ID)
     pl.semaphore_wait(barrier, len(bits))
 
     offset = 0
     length = o_ref.shape[0]
     plan = []
     for step in range(n_halve):
-        axis, m = bits[step]
         half = length // 2
-        bit, ids = partner(axis, m)
+        bit, ids = partner(bits[step])
         keep = offset + bit * half
         give = offset + (1 - bit) * half
         source = x_ref if step == 0 else acc
@@ -67,9 +78,9 @@
         acc[pl.ds(keep, half)] = source[pl.ds(keep, half)] + halves[step][...]
         plan.append((ids, keep, half))
         offset, length = keep, half
-    for slot, (axis, m) in enumerate(bits[n_halve:]):
+    for slot, specs in enumerate(bits[n_halve:]):
         step = n_halve + slot
-        bit, ids = partner(axis, m)
+        bit, ids = partner(specs)
         copy = pltpu.make_async_remote_copy(
             src_ref=acc.at[pl.ds(offset, length)], dst_ref=doubles[slot],
             send_sem=send_sem.at[step], recv_sem=recv_sem.at[step],

time: 227 us -> 224 us (0.987)
  Pallas kernels: 119 us -> 116 us
    pallas_call x1, Pallas kernels: 113 us -> 110 us  [allreduce(): pl.pallas_call(functools.partial(allreduce_kernel, bits, n_halve), out_sh...]
  transfers between devices with their start and end apart: 8 -> 8, of which waited for: 2 -> 2; matrix products, arithmetic and copies ran while one was open for 9% -> 9% of each run, Pallas kernels for 53% -> 52%
where the time goes in v5:
time: 224 us; the launch traced here: 223 us
  Pallas kernels  116 us (52%)
  local copies, waits for them, and re-layouts  31 us (14%)
  starting transfers between devices  29.5 us (13%)
  other arithmetic  19.8 us (9%)
  matrix products  16.4 us (7%)
  waiting for transfers between devices  8.48 us (4%)
    pallas_call x1, Pallas kernels, allreduce(): pl.pallas_call(functools.partial(allreduce_kernel, bits, n_halve), out_sh...  110 us
    ppermute x8, starting transfers between devices, from_behind(): return lax.ppermute(block, axis, route)  29.5 us
    ppermute x8, waiting for transfers between devices, from_behind(): return lax.ppermute(block, axis, route)  8.48 us
    unnamed x102, local copies, waits for them, and re-layouts  8.4 us
    pallas_call x1, Pallas kernels, kernel_taps(): pl.pallas_call(functools.partial(kernel_taps_body, tap_count), out_shape=...  6.65 us
    slice x4, local copies, waits for them, and re-layouts, depthwise(): term = conv_kernel[tap_index] * extended[first_row:first_row + row_count]  5.84 us
    dot_general x1, matrix products, per_device(): jnp.einsum('hqk,qhd->khd', probs.astype(jnp.bfloat16), dout_heads, prefer...  5.18 us
  transfers between devices with their start and end apart: 8, of which 2 were waited for; matrix products, arithmetic and copies ran while one was open for 9% of the time, Pallas kernels for 52%

profile of v5, /device:TPU:1, one launch (start us, length us, event | category | flops | bytes accessed | tf_op | source)
XLA Modules:
  0.0 222.9 jit_solution(15211941731600640283)
XLA Ops:
  1.8 5.5 %collective-permute-start.2 = (bf16[192,1024]{1,0:T(8,128)(2,1)S(1)}, bf16[192,1024]{1,0:T(8,128)(2,1)S(1)}, u32[]{:S(2)}, u32[]{:S(2)}) collective-permute-start(bf16[192,1024]{1,0:T(8,128)(2,1)S(1)} %pad_maximum_fusion.1), channel_id=1, source_target_pairs={{0,1},{1,2},{2,3},{3,4},{4,5},{5,6},{6,7},{7,8},{8,9},{9,10},{10,1... | collective-permute-start | bytes 1179656 | tf_op jit(solution)/shard_map/ppermute | solution.py:128
  7.3 4.0 %collective-permute-start.1 = (bf16[192,1024]{1,0:T(8,128)(2,1)S(1)}, bf16[192,1024]{1,0:T(8,128)(2,1)S(1)}, u32[]{:S(2)}, u32[]{:S(2)}) collective-permute-start(bf16[192,1024]{1,0:T(8,128)(2,1)S(1)} %pad_maximum_fusion.1), channel_id=1, source_target_pairs={{0,2},{1,3},{2,4},{3,5},{4,6},{5,7},{6,8},{7,9},{8,10},{9,11},{10,... | collective-permute-start | bytes 1179656 | tf_op jit(solution)/shard_map/ppermute | solution.py:128
  11.3 5.8 %collective-permute-start = (bf16[192,1024]{1,0:T(8,128)(2,1)S(1)}, bf16[192,1024]{1,0:T(8,128)(2,1)S(1)}, u32[]{:S(2)}, u32[]{:S(2)}) collective-permute-start(bf16[192,1024]{1,0:T(8,128)(2,1)S(1)} %pad_maximum_fusion.1), channel_id=1, source_target_pairs={{0,3},{1,4},{2,5},{3,6},{4,7},{5,8},{6,9},{7,10},{8,11},{9,12},{10... | collective-permute-start | bytes 1179656 | tf_op jit(solution)/shard_map/ppermute | solution.py:128
  17.1 1.7 fusion.103
  18.8 2.0 fusion.102
  23.8 3.3 %collective-permute-done = bf16[192,1024]{1,0:T(8,128)(2,1)S(1)} collective-permute-done((bf16[192,1024]{1,0:T(8,128)(2,1)S(1)}, bf16[192,1024]{1,0:T(8,128)(2,1)S(1)}, u32[]{:S(2)}, u32[]{:S(2)}) %collective-permute-start) | collective-permute-done | bytes 393248 | tf_op jit(solution)/shard_map/ppermute | solution.py:128
  36.8 8.7 %collective-permute-start.3 = (bf16[30,1024]{1,0:T(8,128)(2,1)S(1)}, bf16[30,1024]{1,0:T(8,128)(2,1)S(1)}, u32[]{:S(2)}, u32[]{:S(2)}) collective-permute-start(bf16[30,1024]{1,0:T(8,128)(2,1)S(1)} %get-tuple-element.27), channel_id=1, source_target_pairs={{0,1},{1,2},{2,3},{3,4},{4,5},{5,6},{6,7},{7,8},{8,9},{9,10},{10,1... | collective-permute-start | bytes 184328 | tf_op jit(solution)/shard_map/ppermute | solution.py:128
  47.6 5.1 %collective-permute-done.4 = bf16[30,2048]{1,0:T(8,128)(2,1)S(1)} collective-permute-done((bf16[30,2048]{1,0:T(8,128)(2,1)S(1)}, bf16[30,2048]{1,0:T(8,128)(2,1)S(1)}, u32[]{:S(2)}, u32[]{:S(2)}) %collective-permute-start.4) | collective-permute-done | bytes 122912 | tf_op jit(solution)/shard_map/ppermute | solution.py:128
  54.2 3.9 %add_multiply_fusion = (f32[222,1024]{1,0:T(8,128)S(1)}, f32[222,1024]{1,0:T(8,128)S(1)}) fusion(bf16[30,1024]{1,0:T(8,128)(2,1)S(1)} %get-tuple-element.61, bf16[192,1024]{1,0:T(8,128)(2,1)S(1)} %bitcast.138, f32[252,1024]{1,0:T(8,128)S(1)} %maximum_convert_fusion, f32[1024]{0:T(1024)S(1)} %bitcast.161, f32[1024]{0:T(1024)S(1)} %bitcast.163, ...), kind=kLoop, calls=%fused_computation.87 | loop fusion | flops 16594944 | bytes 30588928 | tf_op jit(solution)/shard_map/mul | solution.py:226
  58.1 3.1 %fusion.57 = bf16[192,1024]{1,0:T(8,128)(2,1)S(1)} fusion(f32[222,1024]{1,0:T(8,128)S(1)} %get-tuple-element.18, f32[1024]{0:T(1024)S(1)} %bitcast.162, f32[1024]{0:T(1024)S(1)} %bitcast.164, f32[1024]{0:T(1024)S(1)} %bitcast.168, f32[1024]{0:T(1024)S(1)} %bitcast.170, f32[1024]{0:T(1024)S(1)} %bitcast.172, f32[1024]{0:T(1024)S(1)} %bitcast.174, ...), kind=kLoop, calls=%fused_computation.98 | loop fusion | flops 12189696 | bytes 24899584 | tf_op jit(solution)/shard_map/convert_element_type | solution.py:229
  63.5 1.8 copy.24
  66.5 5.2 %fusion.5 = f32[8,64,768]{2,1,0:T(8,128)} fusion(bf16[192,8,64]{0,2,1:T(8,128)(2,1)} %bitcast.129, f32[8,768,192]{1,2,0:T(8,128)} %copy-done.1, f32[8,192]{1,0:T(8,128)S(1)} %copy-done.45, pred[192,768]{1,0:T(8,128)(4,1)} %copy-done.10), kind=kOutput, calls=%fused_computation.12 | convolution fusion | flops 156893184 | bytes 6641664 | tf_op jit(solution)/shard_map/hqk,qhd->khd/dot_general | solution.py:242
  71.7 2.1 multiply_convert_fusion
  75.4 1.7 convolution_multiply_fusion
  77.2 1.7 fusion.105
  80.1 1.9 copy.25
  82.0 3.0 %copy.26 = f32[768,512]{1,0:T(8,128)} copy(f32[768,512]{0,1:T(8,128)} %bitcast.128) | data formatting | bytes 3145728 | tf_op jit(solution)/shard_map/reshape | solution.py:257
  85.0 1.6 fusion.3
  91.8 6.7 %shard_map.109 = f32[32,1024]{1,0:T(8,128)} custom-call(f32[192,1024]{1,0:T(8,128)} %slice.529.dmixed_ref, f32[222,1024]{1,0:T(8,128)} %slice.525.extended_ref), custom_call_target="tpu_custom_call" | custom-call | tf_op jit(solution)/shard_map/pallas_call | solution.py:159
  98.5 1.8 maximum_bitcast_fusion
  100.3 1.8 copy.37
  102.1 109.7 %shard_map.110 = f32[544,8,128]{2,1,0:T(8,128)} custom-call(f32[544,8,128]{2,1,0:T(8,128)} %bitcast.118), custom_call_target="tpu_custom_call" | custom-call | tf_op jit(solution)/shard_map/pallas_call | solution.py:115
  211.8 3.1 %slice.486 = f32[512,8,128]{2,1,0:T(8,128)} slice(f32[544,8,128]{2,1,0:T(8,128)} %shard_map.110), slice={[0:512], [0:8], [0:128]} | slice | bytes 4194304 | tf_op jit(solution)/shard_map/slice | solution.py:175
  215.7 3.5 %copy.41 = f32[64,8,8,128]{3,1,2,0:T(8,128)} copy(f32[64,8,8,128]{3,2,1,0:T(8,128)} %bitcast.119) | data formatting | bytes 4194304
  (143 shorter events, 32.6 us)
Async XLA Ops:
  0.6 35.7 %copy-start = (bf16[512,1024]{1,0:T(8,128)(2,1)S(1)}, bf16[512,1024]{1,0:T(8,128)(2,1)}, u32[]{:S(2)}) copy-start(bf16[512,1024]{1,0:T(8,128)(2,1)} %param.9) | copy-start | bytes 3145732
  1.8 22.0 %collective-permute-start.2 = (bf16[192,1024]{1,0:T(8,128)(2,1)S(1)}, bf16[192,1024]{1,0:T(8,128)(2,1)S(1)}, u32[]{:S(2)}, u32[]{:S(2)}) collective-permute-start(bf16[192,1024]{1,0:T(8,128)(2,1)S(1)} %pad_maximum_fusion.1), channel_id=1, source_target_pairs={{0,1},{1,2},{2,3},{3,4},{4,5},{5,6},{6,7},{7,8},{8,9},{9,10},{10,1... | collective-permute-start | bytes 1179656 | tf_op jit(solution)/shard_map/ppermute | solution.py:128
  7.3 16.5 %collective-permute-start.1 = (bf16[192,1024]{1,0:T(8,128)(2,1)S(1)}, bf16[192,1024]{1,0:T(8,128)(2,1)S(1)}, u32[]{:S(2)}, u32[]{:S(2)}) collective-permute-start(bf16[192,1024]{1,0:T(8,128)(2,1)S(1)} %pad_maximum_fusion.1), channel_id=1, source_target_pairs={{0,2},{1,3},{2,4},{3,5},{4,6},{5,7},{6,8},{7,9},{8,10},{9,11},{10,... | collective-permute-start | bytes 1179656 | tf_op jit(solution)/shard_map/ppermute | solution.py:128
  11.3 15.8 %collective-permute-start = (bf16[192,1024]{1,0:T(8,128)(2,1)S(1)}, bf16[192,1024]{1,0:T(8,128)(2,1)S(1)}, u32[]{:S(2)}, u32[]{:S(2)}) collective-permute-start(bf16[192,1024]{1,0:T(8,128)(2,1)S(1)} %pad_maximum_fusion.1), channel_id=1, source_target_pairs={{0,3},{1,4},{2,5},{3,6},{4,7},{5,8},{6,9},{7,10},{8,11},{9,12},{10... | collective-permute-start | bytes 1179656 | tf_op jit(solution)/shard_map/ppermute | solution.py:128
  36.0 17.9 %copy-start.8 = (bf16[192,8,64]{0,2,1:T(8,128)(2,1)}, bf16[192,8,64]{0,2,1:T(8,128)(2,1)S(1)}, u32[]{:S(2)}) copy-start(bf16[192,8,64]{0,2,1:T(8,128)(2,1)S(1)} %fusion.18) | copy-start | bytes 589828
  36.0 17.9 %copy-start.16 = (bf16[1,192,1024]{2,1,0:T(8,128)(2,1)S(1)}, bf16[1,192,1024]{2,1,0:T(8,128)(2,1)}, u32[]{:S(2)}) copy-start(bf16[1,192,1024]{2,1,0:T(8,128)(2,1)} %param.11) | copy-start | bytes 1179652
  36.1 17.9 %copy-start.18 = (f32[1,1024]{1,0:T(1,128)S(1)}, f32[1,1024]{1,0:T(1,128)}, u32[]{:S(2)}) copy-start(f32[1,1024]{1,0:T(1,128)} %get-tuple-element.52) | copy-start | bytes 12292
  36.1 17.9 %copy-start.19 = (f32[1,1024]{1,0:T(1,128)S(1)}, f32[1,1024]{1,0:T(1,128)}, u32[]{:S(2)}) copy-start(f32[1,1024]{1,0:T(1,128)} %get-tuple-element.53) | copy-start | bytes 12292
  36.1 17.9 %copy-start.20 = (f32[1,1024]{1,0:T(1,128)S(1)}, f32[1,1024]{1,0:T(1,128)}, u32[]{:S(2)}) copy-start(f32[1,1024]{1,0:T(1,128)} %get-tuple-element.54) | copy-start | bytes 12292
  36.1 17.9 %copy-start.21 = (f32[1,1024]{1,0:T(1,128)S(1)}, f32[1,1024]{1,0:T(1,128)}, u32[]{:S(2)}) copy-start(f32[1,1024]{1,0:T(1,128)} %get-tuple-element.55) | copy-start | bytes 12292
  36.1 17.9 %copy-start.22 = (f32[1,1024]{1,0:T(1,128)S(1)}, f32[1,1024]{1,0:T(1,128)}, u32[]{:S(2)}) copy-start(f32[1,1024]{1,0:T(1,128)} %get-tuple-element.56) | copy-start | bytes 12292
  36.1 17.9 %copy-start.23 = (f32[1,1024]{1,0:T(1,128)S(1)}, f32[1,1024]{1,0:T(1,128)}, u32[]{:S(2)}) copy-start(f32[1,1024]{1,0:T(1,128)} %get-tuple-element.57) | copy-start | bytes 12292
  36.1 17.9 %copy-start.24 = (f32[1,1024]{1,0:T(1,128)S(1)}, f32[1,1024]{1,0:T(1,128)}, u32[]{:S(2)}) copy-start(f32[1,1024]{1,0:T(1,128)} %get-tuple-element.58) | copy-start | bytes 12292
  36.1 17.9 %copy-start.25 = (f32[1,1024]{1,0:T(1,128)S(1)}, f32[1,1024]{1,0:T(1,128)}, u32[]{:S(2)}) copy-start(f32[1,1024]{1,0:T(1,128)} %get-tuple-element.59) | copy-start | bytes 12292
  36.1 17.9 %copy-start.26 = (f32[1,1024]{1,0:T(1,128)S(1)}, f32[1,1024]{1,0:T(1,128)}, u32[]{:S(2)}) copy-start(f32[1,1024]{1,0:T(1,128)} %get-tuple-element.29) | copy-start | bytes 12292
  36.1 17.9 %copy-start.27 = (f32[1,1024]{1,0:T(1,128)S(1)}, f32[1,1024]{1,0:T(1,128)}, u32[]{:S(2)}) copy-start(f32[1,1024]{1,0:T(1,128)} %get-tuple-element.30) | copy-start | bytes 12292
  36.2 17.9 %copy-start.28 = (f32[1,1024]{1,0:T(1,128)S(1)}, f32[1,1024]{1,0:T(1,128)}, u32[]{:S(2)}) copy-start(f32[1,1024]{1,0:T(1,128)} %get-tuple-element.31) | copy-start | bytes 12292
  36.2 17.9 %copy-start.29 = (f32[1,1024]{1,0:T(1,128)S(1)}, f32[1,1024]{1,0:T(1,128)}, u32[]{:S(2)}) copy-start(f32[1,1024]{1,0:T(1,128)} %get-tuple-element.32) | copy-start | bytes 12292
  36.8 16.0 %collective-permute-start.3 = (bf16[30,1024]{1,0:T(8,128)(2,1)S(1)}, bf16[30,1024]{1,0:T(8,128)(2,1)S(1)}, u32[]{:S(2)}, u32[]{:S(2)}) collective-permute-start(bf16[30,1024]{1,0:T(8,128)(2,1)S(1)} %get-tuple-element.27), channel_id=1, source_target_pairs={{0,1},{1,2},{2,3},{3,4},{4,5},{5,6},{6,7},{7,8},{8,9},{9,10},{10,1... | collective-permute-start | bytes 184328 | tf_op jit(solution)/shard_map/ppermute | solution.py:128
  45.5 7.2 %collective-permute-start.4 = (bf16[30,2048]{1,0:T(8,128)(2,1)S(1)}, bf16[30,2048]{1,0:T(8,128)(2,1)S(1)}, u32[]{:S(2)}, u32[]{:S(2)}) collective-permute-start(bf16[30,2048]{1,0:T(8,128)(2,1)S(1)} %pad_maximum_fusion.2), channel_id=1, source_target_pairs={{1,0},{2,1},{3,2},{4,3},{5,4},{6,5},{7,6},{8,7},{9,8},{10,9},{11,1... | collective-permute-start | bytes 368648 | tf_op jit(solution)/shard_map/ppermute | solution.py:128
  58.1 20.8 %copy-start.3 = (f32[222,1024]{1,0:T(8,128)}, f32[222,1024]{1,0:T(8,128)S(1)}, u32[]{:S(2)}) copy-start(f32[222,1024]{1,0:T(8,128)S(1)} %get-tuple-element.19) | copy-start | bytes 2727940
  87.7 133.1 %collective-permute-start.5 = (bf16[192,1024]{1,0:T(8,128)(2,1)}, bf16[192,1024]{1,0:T(8,128)(2,1)S(1)}, u32[]{:S(2)}, u32[]{:S(2)}) collective-permute-start(bf16[192,1024]{1,0:T(8,128)(2,1)} %get-tuple-element.20), channel_id=1, source_target_pairs={{3,0},{4,1},{5,2},{6,3},{7,4},{8,5},{9,6},{10,7},{11,8},{12,9},{13... | collective-permute-start | bytes 1179656 | tf_op jit(solution)/shard_map/ppermute | solution.py:128
  89.0 131.8 %collective-permute-start.7 = (bf16[192,1024]{1,0:T(8,128)(2,1)}, bf16[192,1024]{1,0:T(8,128)(2,1)}, u32[]{:S(2)}, u32[]{:S(2)}) collective-permute-start(bf16[192,1024]{1,0:T(8,128)(2,1)} %get-tuple-element.21), channel_id=1, source_target_pairs={{1,0},{2,1},{3,2},{4,3},{5,4},{6,5},{7,6},{8,7},{9,8},{10,9},{11,1... | collective-permute-start | bytes 1179656 | tf_op jit(solution)/shard_map/ppermute | solution.py:128
  90.3 130.5 %collective-permute-start.6 = (bf16[192,1024]{1,0:T(8,128)(2,1)}, bf16[192,1024]{1,0:T(8,128)(2,1)}, u32[]{:S(2)}, u32[]{:S(2)}) collective-permute-start(bf16[192,1024]{1,0:T(8,128)(2,1)} %get-tuple-element.22), channel_id=1, source_target_pairs={{2,0},{3,1},{4,2},{5,3},{6,4},{7,5},{8,6},{9,7},{10,8},{11,9},{12,... | collective-permute-start | bytes 1179656 | tf_op jit(solution)/shard_map/ppermute | solution.py:128
  (33 other events, 357.9 us)

commit v6 on v5

--- a/solution.py
+++ b/solution.py
@@ -34,12 +34,19 @@
     return bits
 
 
-def allreduce_kernel(bits, n_halve, x_ref, o_ref, *scratch):
-    halves = scratch[:n_halve]
-    doubles = scratch[n_halve:len(bits)]
-    acc, send_sem, recv_sem = scratch[len(bits):]
+def allreduce_kernel(bits, splits, n_arrays, *refs):
+    x_refs = refs[:n_arrays]
+    o_refs = refs[n_arrays:2 * n_arrays]
+    scratch = refs[2 * n_arrays:]
+    n_halve = len(splits)
+    halves = [scratch[s * n_arrays:(s + 1) * n_arrays] for s in range(n_halve)]
+    base = n_halve * n_arrays
+    n_double = len(bits) - n_halve
+    doubles = [scratch[base + t * n_arrays:base + (t + 1) * n_arrays] for t in range(n_double)]
+    base += n_double * n_arrays
+    accs = scratch[base:base + n_arrays]
+    send_sem, recv_sem = scratch[base + n_arrays:]
     me = {"dp": lax.axis_index("dp"), "blk": lax.axis_index("blk")}
-
     core = me["dp"] % 2
 
     def one_partner(axis, m):
@@ -55,71 +62,90 @@
         ids = tuple(a + (b - a) * core for a, b in zip(ids0, ids1))
         return bit, ids
 
+    def window(ref, region):
+        r0, rl, c0, cl = region
+        return ref.at[pl.ds(pl.multiple_of(r0, 8), rl), pl.ds(pl.multiple_of(c0, 128), cl)]
+
+    def exchange(step, ids, sources, targets, regions):
+        copies = []
+        for i in range(n_arrays):
+            copy = pltpu.make_async_remote_copy(
+                src_ref=window(sources[i], regions[i]), dst_ref=targets[i],
+                send_sem=send_sem.at[step, i], recv_sem=recv_sem.at[step, i],
+                device_id=ids, device_id_type=MESH_ID)
+            copy.start()
+            copies.append(copy)
+        for copy in copies:
+            copy.wait()
+
     barrier = pltpu.get_barrier_semaphore()
     for specs in bits:
         pl.semaphore_signal(barrier, 1, device_id=partner(specs)[1], device_id_type=MESH_ID)
     pl.semaphore_wait(barrier, len(bits))
 
-    offset = 0
-    length = o_ref.shape[0]
+    regions = [(0, x.shape[0], 0, x.shape[1]) for x in x_refs]
     plan = []
-    for step in range(n_halve):
-        half = length // 2
+    for step, dim in enumerate(splits):
         bit, ids = partner(bits[step])
-        keep = offset + bit * half
-        give = offset + (1 - bit) * half
-        source = x_ref if step == 0 else acc
-        copy = pltpu.make_async_remote_copy(
-            src_ref=source.at[pl.ds(give, half)], dst_ref=halves[step],
-            send_sem=send_sem.at[step], recv_sem=recv_sem.at[step],
-            device_id=ids, device_id_type=MESH_ID)
-        copy.start()
-        copy.wait()
-        acc[pl.ds(keep, half)] = source[pl.ds(keep, half)] + halves[step][...]
-        plan.append((ids, keep, half))
-        offset, length = keep, half
-    for slot, specs in enumerate(bits[n_halve:]):
+        keeps, gives = [], []
+        for r0, rl, c0, cl in regions:
+            if dim == 0:
+                half = rl // 2
+                keeps.append((r0 + bit * half, half, c0, cl))
+                gives.append((r0 + (1 - bit) * half, half, c0, cl))
+            else:
+                half = cl // 2
+                keeps.append((r0, rl, c0 + bit * half, half))
+                gives.append((r0, rl, c0 + (1 - bit) * half, half))
+        sources = x_refs if step == 0 else accs
+        exchange(step, ids, sources, [h.at[...] for h in halves[step]], gives)
+        for i in range(n_arrays):
+            window(accs[i], keeps[i])[...] = window(sources[i], keeps[i])[...] + halves[step][i][...]
+        plan.append((ids, keeps))
+        regions = keeps
+    for slot in range(n_double):
         step = n_halve + slot
-        bit, ids = partner(specs)
-        copy = pltpu.make_async_remote_copy(
-            src_ref=acc.at[pl.ds(offset, length)], dst_ref=doubles[slot],
-            send_sem=send_sem.at[step], recv_sem=recv_sem.at[step],
-            device_id=ids, device_id_type=MESH_ID)
-        copy.start()
-        copy.wait()
-        acc[pl.ds(offset, length)] = acc[pl.ds(offset, length)] + doubles[slot][...]
-    o_ref[pl.ds(offset, length)] = acc[pl.ds(offset, length)]
-    for back, (ids, keep, half) in enumerate(reversed(plan)):
+        bit, ids = partner(bits[step])
+        exchange(step, ids, accs, [d.at[...] for d in doubles[slot]], regions)
+        for i in range(n_arrays):
+            window(accs[i], regions[i])[...] = window(accs[i], regions[i])[...] + doubles[slot][i][...]
+    for i in range(n_arrays):
+        window(o_refs[i], regions[i])[...] = window(accs[i], regions[i])[...]
+    for back, (ids, keeps) in enumerate(reversed(plan)):
         step = len(bits) + back
-        copy = pltpu.make_async_remote_copy(
-            src_ref=o_ref.at[pl.ds(keep, half)], dst_ref=o_ref.at[pl.ds(keep, half)],
-            send_sem=send_sem.at[step], recv_sem=recv_sem.at[step],
-            device_id=ids, device_id_type=MESH_ID)
-        copy.start()
-        copy.wait()
-
-
-def allreduce(x, dp_size, blk_size, n_halve_max=5):
+        exchange(step, ids, o_refs, [window(o, k) for o, k in zip(o_refs, keeps)], keeps)
+
+
+def allreduce(arrays, dp_size, blk_size, n_halve_max=5):
     bits = reduce_bits(dp_size, blk_size)
-    rows = x.shape[0]
-    n_halve = 0
-    while n_halve < min(n_halve_max, len(bits)) and rows % (2 ** (n_halve + 1)) == 0:
-        n_halve += 1
-    lengths = [rows // 2 ** (s + 1) for s in range(n_halve)]
-    final = rows // 2 ** n_halve
-    tile = x.shape[1:]
-    scratch = [pltpu.VMEM((n,) + tile, x.dtype) for n in lengths]
-    scratch += [pltpu.VMEM((final,) + tile, x.dtype) for _ in bits[n_halve:]]
-    steps = len(bits) + n_halve
-    scratch += [pltpu.VMEM(x.shape, x.dtype), pltpu.SemaphoreType.DMA((steps,)), pltpu.SemaphoreType.DMA((steps,))]
+    limit = min(n_halve_max, len(bits))
+    splits = []
+    cols = arrays[0].shape[1]
+    rows = [a.shape[0] for a in arrays]
+    while len(splits) < limit and cols % 256 == 0:
+        splits.append(1)
+        cols //= 2
+    while len(splits) < limit and all(r % 16 == 0 for r in rows):
+        splits.append(0)
+        rows = [r // 2 for r in rows]
+    scratch = []
+    shapes = [a.shape for a in arrays]
+    for dim in splits:
+        shapes = [(s[0] // 2, s[1]) if dim == 0 else (s[0], s[1] // 2) for s in shapes]
+        scratch += [pltpu.VMEM(s, jnp.float32) for s in shapes]
+    for _ in bits[len(splits):]:
+        scratch += [pltpu.VMEM(s, jnp.float32) for s in shapes]
+    scratch += [pltpu.VMEM(a.shape, jnp.float32) for a in arrays]
+    steps = len(bits) + len(splits)
+    scratch += [pltpu.SemaphoreType.DMA((steps, len(arrays))), pltpu.SemaphoreType.DMA((steps, len(arrays)))]
     return pl.pallas_call(
-        functools.partial(allreduce_kernel, bits, n_halve),
-        out_shape=jax.ShapeDtypeStruct(x.shape, x.dtype),
-        in_specs=[pl.BlockSpec(memory_space=pltpu.VMEM)],
-        out_specs=pl.BlockSpec(memory_space=pltpu.VMEM),
+        functools.partial(allreduce_kernel, bits, splits, len(arrays)),
+        out_shape=[jax.ShapeDtypeStruct(a.shape, jnp.float32) for a in arrays],
+        in_specs=[pl.BlockSpec(memory_space=pltpu.VMEM)] * len(arrays),
+        out_specs=[pl.BlockSpec(memory_space=pltpu.VMEM)] * len(arrays),
         scratch_shapes=scratch,
         compiler_params=pltpu.CompilerParams(collective_id=0, has_side_effects=True),
-    )(x)
+    )(*arrays)
 
 
 def from_behind(block, axis, distance):
@@ -165,14 +191,10 @@
 
 
 def sum_weights(weight_part, kernel_part, kernel_rows):
-    width = weight_part.shape[1]
-    rows = weight_part.shape[0] + kernel_part.shape[0]
-    packed = jnp.concatenate([weight_part, kernel_part], axis=0)
-    total = allreduce(
-        packed.reshape(rows, 8, width // 8), lax.axis_size("dp"), lax.axis_size("blk")
-    ).reshape(rows, width)
-    start = weight_part.shape[0]
-    return total[:start], total[start:start + kernel_rows]
+    weight_total, kernel_total = allreduce(
+        [weight_part, kernel_part], lax.axis_size("dp"), lax.axis_size("blk")
+    )
+    return weight_total, kernel_total[:kernel_rows]
 
 
 def per_device(queries, key_in, value_in, out_weight, conv_kernel, cotangent):

time: 224 us -> 220 us (0.982)
  local copies, waits for them, and re-layouts: 31 us -> 23.3 us
  matrix products: 16.4 us -> 19.1 us
    slice x3 -> x0, local copies, waits for them, and re-layouts: 3.08 us -> none  [sum_weights(): return (total[:start], total[start:start + kernel_rows])]
    unnamed x102, local copies, waits for them, and re-layouts: 8.4 us -> 5.87 us
  transfers between devices with their start and end apart: 8 -> 8, of which waited for: 2 -> 2; matrix products, arithmetic and copies ran while one was open for 9% -> 7% of each run, Pallas kernels for 52% -> 53%
where the time goes in v6:
time: 220 us; the launch traced here: 219 us
  Pallas kernels  117 us (53%)
  starting transfers between devices  29.5 us (13%)
  local copies, waits for them, and re-layouts  23.3 us (11%)
  other arithmetic  20.7 us (9%)
  matrix products  19.1 us (9%)
  waiting for transfers between devices  7.88 us (4%)
    pallas_call x1, Pallas kernels, allreduce(): pl.pallas_call(functools.partial(allreduce_kernel, bits, splits, len(arra...  110 us
    ppermute x8, starting transfers between devices, from_behind(): return lax.ppermute(block, axis, route)  29.5 us
    ppermute x8, waiting for transfers between devices, from_behind(): return lax.ppermute(block, axis, route)  7.88 us
    pallas_call x1, Pallas kernels, kernel_taps(): pl.pallas_call(functools.partial(kernel_taps_body, tap_count), out_shape=...  6.65 us
    unnamed x102, local copies, waits for them, and re-layouts  5.87 us
    slice x4, local copies, waits for them, and re-layouts, depthwise(): term = conv_kernel[tap_index] * extended[first_row:first_row + row_count]  5.61 us
    dot_general x1, matrix products, per_device(): jnp.einsum('hqk,qhd->khd', probs.astype(jnp.bfloat16), dout_heads, prefer...  5.02 us
    mul x1, other arithmetic, per_device(): dmixed_all = upstream * sigma_all * (1.0 + mixed_all * (1.0 - sigma_all))  4.71 us
  transfers between devices with their start and end apart: 8, of which 2 were waited for; matrix products, arithmetic and copies ran while one was open for 7% of the time, Pallas kernels for 53%

profile of v6, /device:TPU:1, one launch (start us, length us, event | category | flops | bytes accessed | tf_op | source)
XLA Modules:
  0.0 218.7 jit_solution(13009057907440967169)
XLA Ops:
  1.8 5.5 %collective-permute-start.2 = (bf16[192,1024]{1,0:T(8,128)(2,1)S(1)}, bf16[192,1024]{1,0:T(8,128)(2,1)S(1)}, u32[]{:S(2)}, u32[]{:S(2)}) collective-permute-start(bf16[192,1024]{1,0:T(8,128)(2,1)S(1)} %pad_maximum_fusion.1), channel_id=1, source_target_pairs={{0,1},{1,2},{2,3},{3,4},{4,5},{5,6},{6,7},{7,8},{8,9},{9,10},{10,1... | collective-permute-start | bytes 1179656 | tf_op jit(solution)/shard_map/ppermute | solution.py:154
  7.3 4.0 %collective-permute-start.1 = (bf16[192,1024]{1,0:T(8,128)(2,1)S(1)}, bf16[192,1024]{1,0:T(8,128)(2,1)S(1)}, u32[]{:S(2)}, u32[]{:S(2)}) collective-permute-start(bf16[192,1024]{1,0:T(8,128)(2,1)S(1)} %pad_maximum_fusion.1), channel_id=1, source_target_pairs={{0,2},{1,3},{2,4},{3,5},{4,6},{5,7},{6,8},{7,9},{8,10},{9,11},{10,... | collective-permute-start | bytes 1179656 | tf_op jit(solution)/shard_map/ppermute | solution.py:154
  11.3 5.8 %collective-permute-start = (bf16[192,1024]{1,0:T(8,128)(2,1)S(1)}, bf16[192,1024]{1,0:T(8,128)(2,1)S(1)}, u32[]{:S(2)}, u32[]{:S(2)}) collective-permute-start(bf16[192,1024]{1,0:T(8,128)(2,1)S(1)} %pad_maximum_fusion.1), channel_id=1, source_target_pairs={{0,3},{1,4},{2,5},{3,6},{4,7},{5,8},{6,9},{7,10},{8,11},{9,12},{10... | collective-permute-start | bytes 1179656 | tf_op jit(solution)/shard_map/ppermute | solution.py:154
  17.1 1.7 fusion.103
  18.8 1.9 fusion.102
  22.3 1.8 copy.23
  24.4 2.7 %collective-permute-done = bf16[192,1024]{1,0:T(8,128)(2,1)S(1)} collective-permute-done((bf16[192,1024]{1,0:T(8,128)(2,1)S(1)}, bf16[192,1024]{1,0:T(8,128)(2,1)S(1)}, u32[]{:S(2)}, u32[]{:S(2)}) %collective-permute-start) | collective-permute-done | bytes 393248 | tf_op jit(solution)/shard_map/ppermute | solution.py:154
  29.0 2.2 fusion.4
  34.9 8.7 %collective-permute-start.3 = (bf16[30,1024]{1,0:T(8,128)(2,1)S(1)}, bf16[30,1024]{1,0:T(8,128)(2,1)S(1)}, u32[]{:S(2)}, u32[]{:S(2)}) collective-permute-start(bf16[30,1024]{1,0:T(8,128)(2,1)S(1)} %get-tuple-element.31), channel_id=1, source_target_pairs={{0,1},{1,2},{2,3},{3,4},{4,5},{5,6},{6,7},{7,8},{8,9},{9,10},{10,1... | collective-permute-start | bytes 184328 | tf_op jit(solution)/shard_map/ppermute | solution.py:154
  45.7 5.1 %collective-permute-done.4 = bf16[30,2048]{1,0:T(8,128)(2,1)S(1)} collective-permute-done((bf16[30,2048]{1,0:T(8,128)(2,1)S(1)}, bf16[30,2048]{1,0:T(8,128)(2,1)S(1)}, u32[]{:S(2)}, u32[]{:S(2)}) %collective-permute-start.4) | collective-permute-done | bytes 122912 | tf_op jit(solution)/shard_map/ppermute | solution.py:154
  51.3 4.7 %add_multiply_fusion = (f32[222,1024]{1,0:T(8,128)S(1)}, f32[222,1024]{1,0:T(8,128)}) fusion(bf16[30,1024]{1,0:T(8,128)(2,1)S(1)} %get-tuple-element.65, bf16[192,1024]{1,0:T(8,128)(2,1)S(1)} %bitcast.124, f32[252,1024]{1,0:T(8,128)S(1)} %maximum_convert_fusion, f32[1024]{0:T(1024)S(1)} %bitcast.146, f32[1024]{0:T(1024)S(1)} %bitcast.148, ...), kind=kLoop, calls=%fused_computation.85 | loop fusion | flops 16594944 | bytes 30588928 | tf_op jit(solution)/shard_map/mul | solution.py:248
  56.0 3.0 %fusion.57 = bf16[192,1024]{1,0:T(8,128)(2,1)S(1)} fusion(f32[222,1024]{1,0:T(8,128)S(1)} %get-tuple-element.22, f32[1024]{0:T(1024)S(1)} %bitcast.147, f32[1024]{0:T(1024)S(1)} %bitcast.149, f32[1024]{0:T(1024)S(1)} %bitcast.153, f32[1024]{0:T(1024)S(1)} %bitcast.155, f32[1024]{0:T(1024)S(1)} %bitcast.157, f32[1024]{0:T(1024)S(1)} %bitcast.159, ...), kind=kLoop, calls=%fused_computation.96 | loop fusion | flops 12189696 | bytes 24899584 | tf_op jit(solution)/shard_map/convert_element_type | solution.py:251
  60.2 1.8 copy.24
  63.2 5.0 %fusion.5 = f32[8,64,768]{2,1,0:T(8,128)} fusion(bf16[192,8,64]{0,2,1:T(8,128)(2,1)} %bitcast.115, f32[8,768,192]{1,2,0:T(8,128)} %copy-done.1, f32[8,192]{1,0:T(8,128)} %log_add_fusion, pred[192,768]{1,0:T(8,128)(4,1)S(1)} %fusion.89), kind=kOutput, calls=%fused_computation.12 | convolution fusion | flops 156893184 | bytes 6641664 | tf_op jit(solution)/shard_map/hqk,qhd->khd/dot_general | solution.py:264
  68.2 3.8 %multiply_convert_fusion = bf16[8,192,768]{2,1,0:T(8,128)(2,1)S(1)} fusion(f32[8,768,192]{1,2,0:T(8,128)} %copy-done.1, f32[8,192]{1,0:T(8,128)S(1)} %fusion.90, f32[8,192]{1,0:T(8,128)S(1)} %copy-done.48, pred[192,768]{1,0:T(8,128)(4,1)S(1)} %fusion.89, bf16[192,8,64]{0,2,1:T(8,128)(2,1)S(1)} %bitcast.116, bf16[768,8,64]{0,2,1:T(8,128)(2,1)S(1)} %bitcast.119), kind=kOutput, calls=%fused_computation.1 | convolution fusion | flops 159252480 | bytes 8220672 | tf_op jit(solution)/shard_map/qhd,khd->hqk/dot_general | solution.py:267
  73.7 1.7 convolution_multiply_fusion
  75.4 1.8 fusion.105.refs_0_
  77.2 3.0 %copy.25 = f32[768,512]{1,0:T(8,128)} copy(f32[768,512]{0,1:T(8,128)} %bitcast.109) | data formatting | bytes 3145728 | tf_op jit(solution)/shard_map/reshape | solution.py:279
  80.2 3.1 %copy.26 = f32[768,512]{1,0:T(8,128)} copy(f32[768,512]{0,1:T(8,128)} %bitcast.114) | data formatting | bytes 3145728 | tf_op jit(solution)/shard_map/reshape | solution.py:279
  83.2 2.2 fusion.3
  93.7 1.9 copy.27
  95.6 6.7 %shard_map.109.refs_1_ = f32[32,1024]{1,0:T(8,128)} custom-call(f32[192,1024]{1,0:T(8,128)} %slice.517.dmixed_ref, f32[222,1024]{1,0:T(8,128)} %slice.513.extended_ref), custom_call_target="tpu_custom_call" | custom-call | tf_op jit(solution)/shard_map/pallas_call | solution.py:185
  102.2 110.0 %shard_map.110 = (f32[512,1024]{1,0:T(8,128)}, f32[32,1024]{1,0:T(8,128)}) custom-call(f32[512,1024]{1,0:T(8,128)} %fusion.105.refs_0_, f32[32,1024]{1,0:T(8,128)} %shard_map.109.refs_1_), custom_call_target="tpu_custom_call" | custom-call | tf_op jit(solution)/shard_map/pallas_call | solution.py:141
  212.2 2.0 fusion.91
  (138 shorter events, 27.1 us)
Async XLA Ops:
  0.6 33.8 %copy-start = (bf16[512,1024]{1,0:T(8,128)(2,1)S(1)}, bf16[512,1024]{1,0:T(8,128)(2,1)}, u32[]{:S(2)}) copy-start(bf16[512,1024]{1,0:T(8,128)(2,1)} %param.9) | copy-start | bytes 3145732
  1.8 22.6 %collective-permute-start.2 = (bf16[192,1024]{1,0:T(8,128)(2,1)S(1)}, bf16[192,1024]{1,0:T(8,128)(2,1)S(1)}, u32[]{:S(2)}, u32[]{:S(2)}) collective-permute-start(bf16[192,1024]{1,0:T(8,128)(2,1)S(1)} %pad_maximum_fusion.1), channel_id=1, source_target_pairs={{0,1},{1,2},{2,3},{3,4},{4,5},{5,6},{6,7},{7,8},{8,9},{9,10},{10,1... | collective-permute-start | bytes 1179656 | tf_op jit(solution)/shard_map/ppermute | solution.py:154
  7.3 17.1 %collective-permute-start.1 = (bf16[192,1024]{1,0:T(8,128)(2,1)S(1)}, bf16[192,1024]{1,0:T(8,128)(2,1)S(1)}, u32[]{:S(2)}, u32[]{:S(2)}) collective-permute-start(bf16[192,1024]{1,0:T(8,128)(2,1)S(1)} %pad_maximum_fusion.1), channel_id=1, source_target_pairs={{0,2},{1,3},{2,4},{3,5},{4,6},{5,7},{6,8},{7,9},{8,10},{9,11},{10,... | collective-permute-start | bytes 1179656 | tf_op jit(solution)/shard_map/ppermute | solution.py:154
  11.3 15.8 %collective-permute-start = (bf16[192,1024]{1,0:T(8,128)(2,1)S(1)}, bf16[192,1024]{1,0:T(8,128)(2,1)S(1)}, u32[]{:S(2)}, u32[]{:S(2)}) collective-permute-start(bf16[192,1024]{1,0:T(8,128)(2,1)S(1)} %pad_maximum_fusion.1), channel_id=1, source_target_pairs={{0,3},{1,4},{2,5},{3,6},{4,7},{5,8},{6,9},{7,10},{8,11},{9,12},{10... | collective-permute-start | bytes 1179656 | tf_op jit(solution)/shard_map/ppermute | solution.py:154
  34.1 16.9 %copy-start.8 = (bf16[192,8,64]{0,2,1:T(8,128)(2,1)}, bf16[192,8,64]{0,2,1:T(8,128)(2,1)S(1)}, u32[]{:S(2)}) copy-start(bf16[192,8,64]{0,2,1:T(8,128)(2,1)S(1)} %fusion.18) | copy-start | bytes 589828
  34.1 16.9 %copy-start.14 = (bf16[1,192,1024]{2,1,0:T(8,128)(2,1)S(1)}, bf16[1,192,1024]{2,1,0:T(8,128)(2,1)}, u32[]{:S(2)}) copy-start(bf16[1,192,1024]{2,1,0:T(8,128)(2,1)} %param.11) | copy-start | bytes 1179652
  34.1 16.9 %copy-start.17 = (f32[1,1024]{1,0:T(1,128)S(1)}, f32[1,1024]{1,0:T(1,128)}, u32[]{:S(2)}) copy-start(f32[1,1024]{1,0:T(1,128)} %get-tuple-element.52) | copy-start | bytes 12292
  34.1 16.9 %copy-start.18 = (f32[1,1024]{1,0:T(1,128)S(1)}, f32[1,1024]{1,0:T(1,128)}, u32[]{:S(2)}) copy-start(f32[1,1024]{1,0:T(1,128)} %get-tuple-element.53) | copy-start | bytes 12292
  34.1 16.9 %copy-start.19 = (f32[1,1024]{1,0:T(1,128)S(1)}, f32[1,1024]{1,0:T(1,128)}, u32[]{:S(2)}) copy-start(f32[1,1024]{1,0:T(1,128)} %get-tuple-element.54) | copy-start | bytes 12292
  34.1 16.9 %copy-start.20 = (f32[1,1024]{1,0:T(1,128)S(1)}, f32[1,1024]{1,0:T(1,128)}, u32[]{:S(2)}) copy-start(f32[1,1024]{1,0:T(1,128)} %get-tuple-element.55) | copy-start | bytes 12292
  34.2 16.9 %copy-start.21 = (f32[1,1024]{1,0:T(1,128)S(1)}, f32[1,1024]{1,0:T(1,128)}, u32[]{:S(2)}) copy-start(f32[1,1024]{1,0:T(1,128)} %get-tuple-element.56) | copy-start | bytes 12292
  34.2 16.9 %copy-start.22 = (f32[1,1024]{1,0:T(1,128)S(1)}, f32[1,1024]{1,0:T(1,128)}, u32[]{:S(2)}) copy-start(f32[1,1024]{1,0:T(1,128)} %get-tuple-element.57) | copy-start | bytes 12292
  34.2 16.9 %copy-start.23 = (f32[1,1024]{1,0:T(1,128)S(1)}, f32[1,1024]{1,0:T(1,128)}, u32[]{:S(2)}) copy-start(f32[1,1024]{1,0:T(1,128)} %get-tuple-element.58) | copy-start | bytes 12292
  34.2 16.9 %copy-start.24 = (f32[1,1024]{1,0:T(1,128)S(1)}, f32[1,1024]{1,0:T(1,128)}, u32[]{:S(2)}) copy-start(f32[1,1024]{1,0:T(1,128)} %get-tuple-element.59) | copy-start | bytes 12292
  34.2 16.9 %copy-start.25 = (f32[1,1024]{1,0:T(1,128)S(1)}, f32[1,1024]{1,0:T(1,128)}, u32[]{:S(2)}) copy-start(f32[1,1024]{1,0:T(1,128)} %get-tuple-element.60) | copy-start | bytes 12292
  34.2 16.9 %copy-start.26 = (f32[1,1024]{1,0:T(1,128)S(1)}, f32[1,1024]{1,0:T(1,128)}, u32[]{:S(2)}) copy-start(f32[1,1024]{1,0:T(1,128)} %get-tuple-element.61) | copy-start | bytes 12292
  34.2 16.9 %copy-start.27 = (f32[1,1024]{1,0:T(1,128)S(1)}, f32[1,1024]{1,0:T(1,128)}, u32[]{:S(2)}) copy-start(f32[1,1024]{1,0:T(1,128)} %get-tuple-element.62) | copy-start | bytes 12292
  34.9 16.0 %collective-permute-start.3 = (bf16[30,1024]{1,0:T(8,128)(2,1)S(1)}, bf16[30,1024]{1,0:T(8,128)(2,1)S(1)}, u32[]{:S(2)}, u32[]{:S(2)}) collective-permute-start(bf16[30,1024]{1,0:T(8,128)(2,1)S(1)} %get-tuple-element.31), channel_id=1, source_target_pairs={{0,1},{1,2},{2,3},{3,4},{4,5},{5,6},{6,7},{7,8},{8,9},{9,10},{10,1... | collective-permute-start | bytes 184328 | tf_op jit(solution)/shard_map/ppermute | solution.py:154
  43.6 7.2 %collective-permute-start.4 = (bf16[30,2048]{1,0:T(8,128)(2,1)S(1)}, bf16[30,2048]{1,0:T(8,128)(2,1)S(1)}, u32[]{:S(2)}, u32[]{:S(2)}) collective-permute-start(bf16[30,2048]{1,0:T(8,128)(2,1)S(1)} %pad_maximum_fusion.2), channel_id=1, source_target_pairs={{1,0},{2,1},{3,2},{4,3},{5,4},{6,5},{7,6},{8,7},{9,8},{10,9},{11,1... | collective-permute-start | bytes 368648 | tf_op jit(solution)/shard_map/ppermute | solution.py:154
  86.5 127.7 %collective-permute-start.5 = (bf16[192,1024]{1,0:T(8,128)(2,1)}, bf16[192,1024]{1,0:T(8,128)(2,1)}, u32[]{:S(2)}, u32[]{:S(2)}) collective-permute-start(bf16[192,1024]{1,0:T(8,128)(2,1)} %get-tuple-element.24), channel_id=1, source_target_pairs={{3,0},{4,1},{5,2},{6,3},{7,4},{8,5},{9,6},{10,7},{11,8},{12,9},{13... | collective-permute-start | bytes 1179656 | tf_op jit(solution)/shard_map/ppermute | solution.py:154
  87.7 126.5 %collective-permute-start.7 = (bf16[192,1024]{1,0:T(8,128)(2,1)}, bf16[192,1024]{1,0:T(8,128)(2,1)}, u32[]{:S(2)}, u32[]{:S(2)}) collective-permute-start(bf16[192,1024]{1,0:T(8,128)(2,1)} %get-tuple-element.25), channel_id=1, source_target_pairs={{1,0},{2,1},{3,2},{4,3},{5,4},{6,5},{7,6},{8,7},{9,8},{10,9},{11,1... | collective-permute-start | bytes 1179656 | tf_op jit(solution)/shard_map/ppermute | solution.py:154
  89.0 125.2 %collective-permute-start.6 = (bf16[192,1024]{1,0:T(8,128)(2,1)}, bf16[192,1024]{1,0:T(8,128)(2,1)}, u32[]{:S(2)}, u32[]{:S(2)}) collective-permute-start(bf16[192,1024]{1,0:T(8,128)(2,1)} %get-tuple-element.26), channel_id=1, source_target_pairs={{2,0},{3,1},{4,2},{5,3},{6,4},{7,5},{8,6},{9,7},{10,8},{11,9},{12,... | collective-permute-start | bytes 1179656 | tf_op jit(solution)/shard_map/ppermute | solution.py:154
  93.7 118.5 %copy-start.4 = (f32[222,1024]{1,0:T(8,128)S(1)}, f32[222,1024]{1,0:T(8,128)}, u32[]{:S(2)}) copy-start(f32[222,1024]{1,0:T(8,128)} %get-tuple-element.23) | copy-start | bytes 2727940
  93.7 120.5 %copy-start.2 = (f32[768,512]{1,0:T(8,128)S(1)}, f32[768,512]{1,0:T(8,128)}, u32[]{:S(2)}) copy-start(f32[768,512]{1,0:T(8,128)} %copy.25) | copy-start | bytes 4718596
  (33 other events, 394.1 us)

commit v7 on v6

--- a/solution.py
+++ b/solution.py
@@ -16,6 +16,7 @@
 
 NEGATIVE = -1e30
 MESH_ID = pl.DeviceIdType.MESH
+FIRST_PIECES = 4
 
 
 def reduce_bits(dp_size, blk_size):
@@ -66,15 +67,20 @@
         r0, rl, c0, cl = region
         return ref.at[pl.ds(pl.multiple_of(r0, 8), rl), pl.ds(pl.multiple_of(c0, 128), cl)]
 
-    def exchange(step, ids, sources, targets, regions):
+    def exchange(step, ids, sources, targets, regions, pieces=1):
         copies = []
         for i in range(n_arrays):
-            copy = pltpu.make_async_remote_copy(
-                src_ref=window(sources[i], regions[i]), dst_ref=targets[i],
-                send_sem=send_sem.at[step, i], recv_sem=recv_sem.at[step, i],
-                device_id=ids, device_id_type=MESH_ID)
-            copy.start()
-            copies.append(copy)
+            r0, rl, c0, cl = regions[i]
+            part = rl // pieces
+            for p in range(pieces):
+                piece = (r0 + p * part, part, c0, cl)
+                copy = pltpu.make_async_remote_copy(
+                    src_ref=window(sources[i], piece),
+                    dst_ref=targets[i].at[pl.ds(p * part, part), :],
+                    send_sem=send_sem.at[step, i, p], recv_sem=recv_sem.at[step, i, p],
+                    device_id=ids, device_id_type=MESH_ID)
+                copy.start()
+                copies.append(copy)
         for copy in copies:
             copy.wait()
 
@@ -98,7 +104,7 @@
                 keeps.append((r0, rl, c0 + bit * half, half))
                 gives.append((r0, rl, c0 + (1 - bit) * half, half))
         sources = x_refs if step == 0 else accs
-        exchange(step, ids, sources, [h.at[...] for h in halves[step]], gives)
+        exchange(step, ids, sources, [h.at[...] for h in halves[step]], gives, FIRST_PIECES if step == 0 else 1)
         for i in range(n_arrays):
             window(accs[i], keeps[i])[...] = window(sources[i], keeps[i])[...] + halves[step][i][...]
         plan.append((ids, keeps))
@@ -113,7 +119,9 @@
         window(o_refs[i], regions[i])[...] = window(accs[i], regions[i])[...]
     for back, (ids, keeps) in enumerate(reversed(plan)):
         step = len(bits) + back
-        exchange(step, ids, o_refs, [window(o, k) for o, k in zip(o_refs, keeps)], keeps)
+        targets = [window(o, (k[0], k[1], k[2], k[3])) for o, k in zip(o_refs, keeps)]
+        pieces = FIRST_PIECES if back == len(plan) - 1 else 1
+        exchange(step, ids, o_refs, targets, keeps, pieces)
 
 
 def allreduce(arrays, dp_size, blk_size, n_halve_max=5):
@@ -137,7 +145,8 @@
         scratch += [pltpu.VMEM(s, jnp.float32) for s in shapes]
     scratch += [pltpu.VMEM(a.shape, jnp.float32) for a in arrays]
     steps = len(bits) + len(splits)
-    scratch += [pltpu.SemaphoreType.DMA((steps, len(arrays))), pltpu.SemaphoreType.DMA((steps, len(arrays)))]
+    sems = (steps, len(arrays), FIRST_PIECES)
+    scratch += [pltpu.SemaphoreType.DMA(sems), pltpu.SemaphoreType.DMA(sems)]
     return pl.pallas_call(
         functools.partial(allreduce_kernel, bits, splits, len(arrays)),
         out_shape=[jax.ShapeDtypeStruct(a.shape, jnp.float32) for a in arrays],

time: 220 us -> 221 us (level)
  transfers between devices with their start and end apart: 8 -> 8, of which waited for: 2 -> 2; matrix products, arithmetic and copies ran while one was open for 7% -> 7% of each run, Pallas kernels for 53% -> 54%
where the time goes in v7:
time: 221 us; the launch traced here: 220 us
  Pallas kernels  118 us (53%)
  starting transfers between devices  29.5 us (13%)
  local copies, waits for them, and re-layouts  23.3 us (11%)
  other arithmetic  20.7 us (9%)
  matrix products  19.1 us (9%)
  waiting for transfers between devices  7.88 us (4%)
    pallas_call x1, Pallas kernels, allreduce(): pl.pallas_call(functools.partial(allreduce_kernel, bits, splits, len(arra...  111 us
    ppermute x8, starting transfers between devices, from_behind(): return lax.ppermute(block, axis, route)  29.5 us
    ppermute x8, waiting for transfers between devices, from_behind(): return lax.ppermute(block, axis, route)  7.88 us
    pallas_call x1, Pallas kernels, kernel_taps(): pl.pallas_call(functools.partial(kernel_taps_body, tap_count), out_shape=...  6.65 us
    unnamed x102, local copies, waits for them, and re-layouts  5.87 us
    slice x4, local copies, waits for them, and re-layouts, depthwise(): term = conv_kernel[tap_index] * extended[first_row:first_row + row_count]  5.61 us
    dot_general x1, matrix products, per_device(): jnp.einsum('hqk,qhd->khd', probs.astype(jnp.bfloat16), dout_heads, prefer...  5.02 us
    mul x1, other arithmetic, per_device(): dmixed_all = upstream * sigma_all * (1.0 + mixed_all * (1.0 - sigma_all))  4.71 us
  transfers between devices with their start and end apart: 8, of which 2 were waited for; matrix products, arithmetic and copies ran while one was open for 7% of the time, Pallas kernels for 54%

profile of v7, /device:TPU:1, one launch (start us, length us, event | category | flops | bytes accessed | tf_op | source)
XLA Modules:
  0.0 220.2 jit_solution(3248958369791663815)
XLA Ops:
  1.8 5.5 %collective-permute-start.2 = (bf16[192,1024]{1,0:T(8,128)(2,1)S(1)}, bf16[192,1024]{1,0:T(8,128)(2,1)S(1)}, u32[]{:S(2)}, u32[]{:S(2)}) collective-permute-start(bf16[192,1024]{1,0:T(8,128)(2,1)S(1)} %pad_maximum_fusion.1), channel_id=1, source_target_pairs={{0,1},{1,2},{2,3},{3,4},{4,5},{5,6},{6,7},{7,8},{8,9},{9,10},{10,1... | collective-permute-start | bytes 1179656 | tf_op jit(solution)/shard_map/ppermute | solution.py:163
  7.3 4.0 %collective-permute-start.1 = (bf16[192,1024]{1,0:T(8,128)(2,1)S(1)}, bf16[192,1024]{1,0:T(8,128)(2,1)S(1)}, u32[]{:S(2)}, u32[]{:S(2)}) collective-permute-start(bf16[192,1024]{1,0:T(8,128)(2,1)S(1)} %pad_maximum_fusion.1), channel_id=1, source_target_pairs={{0,2},{1,3},{2,4},{3,5},{4,6},{5,7},{6,8},{7,9},{8,10},{9,11},{10,... | collective-permute-start | bytes 1179656 | tf_op jit(solution)/shard_map/ppermute | solution.py:163
  11.3 5.8 %collective-permute-start = (bf16[192,1024]{1,0:T(8,128)(2,1)S(1)}, bf16[192,1024]{1,0:T(8,128)(2,1)S(1)}, u32[]{:S(2)}, u32[]{:S(2)}) collective-permute-start(bf16[192,1024]{1,0:T(8,128)(2,1)S(1)} %pad_maximum_fusion.1), channel_id=1, source_target_pairs={{0,3},{1,4},{2,5},{3,6},{4,7},{5,8},{6,9},{7,10},{8,11},{9,12},{10... | collective-permute-start | bytes 1179656 | tf_op jit(solution)/shard_map/ppermute | solution.py:163
  17.1 1.7 fusion.103
  18.8 1.9 fusion.102
  22.3 1.8 copy.23
  24.4 2.7 %collective-permute-done = bf16[192,1024]{1,0:T(8,128)(2,1)S(1)} collective-permute-done((bf16[192,1024]{1,0:T(8,128)(2,1)S(1)}, bf16[192,1024]{1,0:T(8,128)(2,1)S(1)}, u32[]{:S(2)}, u32[]{:S(2)}) %collective-permute-start) | collective-permute-done | bytes 393248 | tf_op jit(solution)/shard_map/ppermute | solution.py:163
  29.0 2.2 fusion.4
  34.9 8.7 %collective-permute-start.3 = (bf16[30,1024]{1,0:T(8,128)(2,1)S(1)}, bf16[30,1024]{1,0:T(8,128)(2,1)S(1)}, u32[]{:S(2)}, u32[]{:S(2)}) collective-permute-start(bf16[30,1024]{1,0:T(8,128)(2,1)S(1)} %get-tuple-element.31), channel_id=1, source_target_pairs={{0,1},{1,2},{2,3},{3,4},{4,5},{5,6},{6,7},{7,8},{8,9},{9,10},{10,1... | collective-permute-start | bytes 184328 | tf_op jit(solution)/shard_map/ppermute | solution.py:163
  45.7 5.1 %collective-permute-done.4 = bf16[30,2048]{1,0:T(8,128)(2,1)S(1)} collective-permute-done((bf16[30,2048]{1,0:T(8,128)(2,1)S(1)}, bf16[30,2048]{1,0:T(8,128)(2,1)S(1)}, u32[]{:S(2)}, u32[]{:S(2)}) %collective-permute-start.4) | collective-permute-done | bytes 122912 | tf_op jit(solution)/shard_map/ppermute | solution.py:163
  51.3 4.7 %add_multiply_fusion = (f32[222,1024]{1,0:T(8,128)S(1)}, f32[222,1024]{1,0:T(8,128)}) fusion(bf16[30,1024]{1,0:T(8,128)(2,1)S(1)} %get-tuple-element.65, bf16[192,1024]{1,0:T(8,128)(2,1)S(1)} %bitcast.124, f32[252,1024]{1,0:T(8,128)S(1)} %maximum_convert_fusion, f32[1024]{0:T(1024)S(1)} %bitcast.146, f32[1024]{0:T(1024)S(1)} %bitcast.148, ...), kind=kLoop, calls=%fused_computation.85 | loop fusion | flops 16594944 | bytes 30588928 | tf_op jit(solution)/shard_map/mul | solution.py:257
  56.0 3.0 %fusion.57 = bf16[192,1024]{1,0:T(8,128)(2,1)S(1)} fusion(f32[222,1024]{1,0:T(8,128)S(1)} %get-tuple-element.22, f32[1024]{0:T(1024)S(1)} %bitcast.147, f32[1024]{0:T(1024)S(1)} %bitcast.149, f32[1024]{0:T(1024)S(1)} %bitcast.153, f32[1024]{0:T(1024)S(1)} %bitcast.155, f32[1024]{0:T(1024)S(1)} %bitcast.157, f32[1024]{0:T(1024)S(1)} %bitcast.159, ...), kind=kLoop, calls=%fused_computation.96 | loop fusion | flops 12189696 | bytes 24899584 | tf_op jit(solution)/shard_map/convert_element_type | solution.py:260
  60.2 1.8 copy.24
  63.2 5.0 %fusion.5 = f32[8,64,768]{2,1,0:T(8,128)} fusion(bf16[192,8,64]{0,2,1:T(8,128)(2,1)} %bitcast.115, f32[8,768,192]{1,2,0:T(8,128)} %copy-done.1, f32[8,192]{1,0:T(8,128)} %log_add_fusion, pred[192,768]{1,0:T(8,128)(4,1)S(1)} %fusion.89), kind=kOutput, calls=%fused_computation.12 | convolution fusion | flops 156893184 | bytes 6641664 | tf_op jit(solution)/shard_map/hqk,qhd->khd/dot_general | solution.py:273
  68.2 3.8 %multiply_convert_fusion = bf16[8,192,768]{2,1,0:T(8,128)(2,1)S(1)} fusion(f32[8,768,192]{1,2,0:T(8,128)} %copy-done.1, f32[8,192]{1,0:T(8,128)S(1)} %fusion.90, f32[8,192]{1,0:T(8,128)S(1)} %copy-done.48, pred[192,768]{1,0:T(8,128)(4,1)S(1)} %fusion.89, bf16[192,8,64]{0,2,1:T(8,128)(2,1)S(1)} %bitcast.116, bf16[768,8,64]{0,2,1:T(8,128)(2,1)S(1)} %bitcast.119), kind=kOutput, calls=%fused_computation.1 | convolution fusion | flops 159252480 | bytes 8220672 | tf_op jit(solution)/shard_map/qhd,khd->hqk/dot_general | solution.py:276
  73.7 1.7 convolution_multiply_fusion
  75.4 1.8 fusion.105.refs_0_
  77.2 3.0 %copy.25 = f32[768,512]{1,0:T(8,128)} copy(f32[768,512]{0,1:T(8,128)} %bitcast.109) | data formatting | bytes 3145728 | tf_op jit(solution)/shard_map/reshape | solution.py:288
  80.2 3.1 %copy.26 = f32[768,512]{1,0:T(8,128)} copy(f32[768,512]{0,1:T(8,128)} %bitcast.114) | data formatting | bytes 3145728 | tf_op jit(solution)/shard_map/reshape | solution.py:288
  83.2 2.2 fusion.3
  93.7 1.9 copy.27
  95.6 6.7 %shard_map.109.refs_1_ = f32[32,1024]{1,0:T(8,128)} custom-call(f32[192,1024]{1,0:T(8,128)} %slice.517.dmixed_ref, f32[222,1024]{1,0:T(8,128)} %slice.513.extended_ref), custom_call_target="tpu_custom_call" | custom-call | tf_op jit(solution)/shard_map/pallas_call | solution.py:194
  102.2 111.5 %shard_map.110 = (f32[512,1024]{1,0:T(8,128)}, f32[32,1024]{1,0:T(8,128)}) custom-call(f32[512,1024]{1,0:T(8,128)} %fusion.105.refs_0_, f32[32,1024]{1,0:T(8,128)} %shard_map.109.refs_1_), custom_call_target="tpu_custom_call" | custom-call | tf_op jit(solution)/shard_map/pallas_call | solution.py:150
  213.7 2.0 fusion.91
  (138 shorter events, 27.1 us)
Async XLA Ops:
  0.6 33.8 %copy-start = (bf16[512,1024]{1,0:T(8,128)(2,1)S(1)}, bf16[512,1024]{1,0:T(8,128)(2,1)}, u32[]{:S(2)}) copy-start(bf16[512,1024]{1,0:T(8,128)(2,1)} %param.9) | copy-start | bytes 3145732
  1.8 22.6 %collective-permute-start.2 = (bf16[192,1024]{1,0:T(8,128)(2,1)S(1)}, bf16[192,1024]{1,0:T(8,128)(2,1)S(1)}, u32[]{:S(2)}, u32[]{:S(2)}) collective-permute-start(bf16[192,1024]{1,0:T(8,128)(2,1)S(1)} %pad_maximum_fusion.1), channel_id=1, source_target_pairs={{0,1},{1,2},{2,3},{3,4},{4,5},{5,6},{6,7},{7,8},{8,9},{9,10},{10,1... | collective-permute-start | bytes 1179656 | tf_op jit(solution)/shard_map/ppermute | solution.py:163
  7.3 17.1 %collective-permute-start.1 = (bf16[192,1024]{1,0:T(8,128)(2,1)S(1)}, bf16[192,1024]{1,0:T(8,128)(2,1)S(1)}, u32[]{:S(2)}, u32[]{:S(2)}) collective-permute-start(bf16[192,1024]{1,0:T(8,128)(2,1)S(1)} %pad_maximum_fusion.1), channel_id=1, source_target_pairs={{0,2},{1,3},{2,4},{3,5},{4,6},{5,7},{6,8},{7,9},{8,10},{9,11},{10,... | collective-permute-start | bytes 1179656 | tf_op jit(solution)/shard_map/ppermute | solution.py:163
  11.3 15.8 %collective-permute-start = (bf16[192,1024]{1,0:T(8,128)(2,1)S(1)}, bf16[192,1024]{1,0:T(8,128)(2,1)S(1)}, u32[]{:S(2)}, u32[]{:S(2)}) collective-permute-start(bf16[192,1024]{1,0:T(8,128)(2,1)S(1)} %pad_maximum_fusion.1), channel_id=1, source_target_pairs={{0,3},{1,4},{2,5},{3,6},{4,7},{5,8},{6,9},{7,10},{8,11},{9,12},{10... | collective-permute-start | bytes 1179656 | tf_op jit(solution)/shard_map/ppermute | solution.py:163
  34.1 16.9 %copy-start.8 = (bf16[192,8,64]{0,2,1:T(8,128)(2,1)}, bf16[192,8,64]{0,2,1:T(8,128)(2,1)S(1)}, u32[]{:S(2)}) copy-start(bf16[192,8,64]{0,2,1:T(8,128)(2,1)S(1)} %fusion.18) | copy-start | bytes 589828
  34.1 16.9 %copy-start.14 = (bf16[1,192,1024]{2,1,0:T(8,128)(2,1)S(1)}, bf16[1,192,1024]{2,1,0:T(8,128)(2,1)}, u32[]{:S(2)}) copy-start(bf16[1,192,1024]{2,1,0:T(8,128)(2,1)} %param.11) | copy-start | bytes 1179652
  34.1 16.9 %copy-start.17 = (f32[1,1024]{1,0:T(1,128)S(1)}, f32[1,1024]{1,0:T(1,128)}, u32[]{:S(2)}) copy-start(f32[1,1024]{1,0:T(1,128)} %get-tuple-element.52) | copy-start | bytes 12292
  34.1 16.9 %copy-start.18 = (f32[1,1024]{1,0:T(1,128)S(1)}, f32[1,1024]{1,0:T(1,128)}, u32[]{:S(2)}) copy-start(f32[1,1024]{1,0:T(1,128)} %get-tuple-element.53) | copy-start | bytes 12292
  34.1 16.9 %copy-start.19 = (f32[1,1024]{1,0:T(1,128)S(1)}, f32[1,1024]{1,0:T(1,128)}, u32[]{:S(2)}) copy-start(f32[1,1024]{1,0:T(1,128)} %get-tuple-element.54) | copy-start | bytes 12292
  34.1 16.9 %copy-start.20 = (f32[1,1024]{1,0:T(1,128)S(1)}, f32[1,1024]{1,0:T(1,128)}, u32[]{:S(2)}) copy-start(f32[1,1024]{1,0:T(1,128)} %get-tuple-element.55) | copy-start | bytes 12292
  34.2 16.9 %copy-start.21 = (f32[1,1024]{1,0:T(1,128)S(1)}, f32[1,1024]{1,0:T(1,128)}, u32[]{:S(2)}) copy-start(f32[1,1024]{1,0:T(1,128)} %get-tuple-element.56) | copy-start | bytes 12292
  34.2 16.9 %copy-start.22 = (f32[1,1024]{1,0:T(1,128)S(1)}, f32[1,1024]{1,0:T(1,128)}, u32[]{:S(2)}) copy-start(f32[1,1024]{1,0:T(1,128)} %get-tuple-element.57) | copy-start | bytes 12292
  34.2 16.9 %copy-start.23 = (f32[1,1024]{1,0:T(1,128)S(1)}, f32[1,1024]{1,0:T(1,128)}, u32[]{:S(2)}) copy-start(f32[1,1024]{1,0:T(1,128)} %get-tuple-element.58) | copy-start | bytes 12292
  34.2 16.9 %copy-start.24 = (f32[1,1024]{1,0:T(1,128)S(1)}, f32[1,1024]{1,0:T(1,128)}, u32[]{:S(2)}) copy-start(f32[1,1024]{1,0:T(1,128)} %get-tuple-element.59) | copy-start | bytes 12292
  34.2 16.9 %copy-start.25 = (f32[1,1024]{1,0:T(1,128)S(1)}, f32[1,1024]{1,0:T(1,128)}, u32[]{:S(2)}) copy-start(f32[1,1024]{1,0:T(1,128)} %get-tuple-element.60) | copy-start | bytes 12292
  34.2 16.9 %copy-start.26 = (f32[1,1024]{1,0:T(1,128)S(1)}, f32[1,1024]{1,0:T(1,128)}, u32[]{:S(2)}) copy-start(f32[1,1024]{1,0:T(1,128)} %get-tuple-element.61) | copy-start | bytes 12292
  34.2 16.9 %copy-start.27 = (f32[1,1024]{1,0:T(1,128)S(1)}, f32[1,1024]{1,0:T(1,128)}, u32[]{:S(2)}) copy-start(f32[1,1024]{1,0:T(1,128)} %get-tuple-element.62) | copy-start | bytes 12292
  34.9 16.0 %collective-permute-start.3 = (bf16[30,1024]{1,0:T(8,128)(2,1)S(1)}, bf16[30,1024]{1,0:T(8,128)(2,1)S(1)}, u32[]{:S(2)}, u32[]{:S(2)}) collective-permute-start(bf16[30,1024]{1,0:T(8,128)(2,1)S(1)} %get-tuple-element.31), channel_id=1, source_target_pairs={{0,1},{1,2},{2,3},{3,4},{4,5},{5,6},{6,7},{7,8},{8,9},{9,10},{10,1... | collective-permute-start | bytes 184328 | tf_op jit(solution)/shard_map/ppermute | solution.py:163
  43.6 7.2 %collective-permute-start.4 = (bf16[30,2048]{1,0:T(8,128)(2,1)S(1)}, bf16[30,2048]{1,0:T(8,128)(2,1)S(1)}, u32[]{:S(2)}, u32[]{:S(2)}) collective-permute-start(bf16[30,2048]{1,0:T(8,128)(2,1)S(1)} %pad_maximum_fusion.2), channel_id=1, source_target_pairs={{1,0},{2,1},{3,2},{4,3},{5,4},{6,5},{7,6},{8,7},{9,8},{10,9},{11,1... | collective-permute-start | bytes 368648 | tf_op jit(solution)/shard_map/ppermute | solution.py:163
  86.5 129.2 %collective-permute-start.5 = (bf16[192,1024]{1,0:T(8,128)(2,1)}, bf16[192,1024]{1,0:T(8,128)(2,1)}, u32[]{:S(2)}, u32[]{:S(2)}) collective-permute-start(bf16[192,1024]{1,0:T(8,128)(2,1)} %get-tuple-element.24), channel_id=1, source_target_pairs={{3,0},{4,1},{5,2},{6,3},{7,4},{8,5},{9,6},{10,7},{11,8},{12,9},{13... | collective-permute-start | bytes 1179656 | tf_op jit(solution)/shard_map/ppermute | solution.py:163
  87.7 128.0 %collective-permute-start.7 = (bf16[192,1024]{1,0:T(8,128)(2,1)}, bf16[192,1024]{1,0:T(8,128)(2,1)}, u32[]{:S(2)}, u32[]{:S(2)}) collective-permute-start(bf16[192,1024]{1,0:T(8,128)(2,1)} %get-tuple-element.25), channel_id=1, source_target_pairs={{1,0},{2,1},{3,2},{4,3},{5,4},{6,5},{7,6},{8,7},{9,8},{10,9},{11,1... | collective-permute-start | bytes 1179656 | tf_op jit(solution)/shard_map/ppermute | solution.py:163
  89.0 126.7 %collective-permute-start.6 = (bf16[192,1024]{1,0:T(8,128)(2,1)}, bf16[192,1024]{1,0:T(8,128)(2,1)}, u32[]{:S(2)}, u32[]{:S(2)}) collective-permute-start(bf16[192,1024]{1,0:T(8,128)(2,1)} %get-tuple-element.26), channel_id=1, source_target_pairs={{2,0},{3,1},{4,2},{5,3},{6,4},{7,5},{8,6},{9,7},{10,8},{11,9},{12,... | collective-permute-start | bytes 1179656 | tf_op jit(solution)/shard_map/ppermute | solution.py:163
  93.7 120.0 %copy-start.4 = (f32[222,1024]{1,0:T(8,128)S(1)}, f32[222,1024]{1,0:T(8,128)}, u32[]{:S(2)}) copy-start(f32[222,1024]{1,0:T(8,128)} %get-tuple-element.23) | copy-start | bytes 2727940
  93.7 122.0 %copy-start.2 = (f32[768,512]{1,0:T(8,128)S(1)}, f32[768,512]{1,0:T(8,128)}, u32[]{:S(2)}) copy-start(f32[768,512]{1,0:T(8,128)} %copy.25) | copy-start | bytes 4718596
  (33 other events, 394.1 us)

commit v8 on v6

--- a/solution.py
+++ b/solution.py
@@ -172,8 +172,13 @@
     rows = dmixed_ref.shape[0]
     first = tap_count - 1
     grads = dmixed_ref[...]
+    shifted = []
+    for shift in range(8):
+        span = (first - shift) // 8 * 8 + rows if shift <= first else 0
+        shifted.append(extended_ref[pl.ds(shift, span), :] if span else None)
     for tap in range(tap_count):
-        window = extended_ref[pl.ds(first - tap, rows), :]
+        block, shift = divmod(first - tap, 8)
+        window = shifted[shift][block * 8:block * 8 + rows]
         out_ref[pl.ds(tap, 1), :] = jnp.sum(grads * window, axis=0, keepdims=True)
     out_ref[pl.ds(tap_count, out_ref.shape[0] - tap_count), :] = jnp.zeros(
         (out_ref.shape[0] - tap_count, out_ref.shape[1]), jnp.float32

time: 220 us -> 219 us (level)
  no operation moved by 1% of the time
where the time goes in v8:
time: 219 us; the launch traced here: 218 us
  Pallas kernels  116 us (53%)
  starting transfers between devices  29.5 us (13%)
  local copies, waits for them, and re-layouts  23.3 us (11%)
  other arithmetic  20.7 us (9%)
  matrix products  19.1 us (9%)
  waiting for transfers between devices  7.88 us (4%)
    pallas_call x1, Pallas kernels, allreduce(): pl.pallas_call(functools.partial(allreduce_kernel, bits, splits, len(arra...  110 us
    ppermute x8, starting transfers between devices, from_behind(): return lax.ppermute(block, axis, route)  29.5 us
    ppermute x8, waiting for transfers between devices, from_behind(): return lax.ppermute(block, axis, route)  7.88 us
    pallas_call x1, Pallas kernels, kernel_taps(): pl.pallas_call(functools.partial(kernel_taps_body, tap_count), out_shape=...  6.36 us
    unnamed x102, local copies, waits for them, and re-layouts  5.87 us
    slice x4, local copies, waits for them, and re-layouts, depthwise(): term = conv_kernel[tap_index] * extended[first_row:first_row + row_count]  5.61 us
    dot_general x1, matrix products, per_device(): jnp.einsum('hqk,qhd->khd', probs.astype(jnp.bfloat16), dout_heads, prefer...  5.02 us
    mul x1, other arithmetic, per_device(): dmixed_all = upstream * sigma_all * (1.0 + mixed_all * (1.0 - sigma_all))  4.71 us
  transfers between devices with their start and end apart: 8, of which 2 were waited for; matrix products, arithmetic and copies ran while one was open for 7% of the time, Pallas kernels for 53%

profile of v8, /device:TPU:1, one launch (start us, length us, event | category | flops | bytes accessed | tf_op | source)
XLA Modules:
  0.0 218.0 jit_solution(11662756794070185452)
XLA Ops:
  1.8 5.5 %collective-permute-start.2 = (bf16[192,1024]{1,0:T(8,128)(2,1)S(1)}, bf16[192,1024]{1,0:T(8,128)(2,1)S(1)}, u32[]{:S(2)}, u32[]{:S(2)}) collective-permute-start(bf16[192,1024]{1,0:T(8,128)(2,1)S(1)} %pad_maximum_fusion.1), channel_id=1, source_target_pairs={{0,1},{1,2},{2,3},{3,4},{4,5},{5,6},{6,7},{7,8},{8,9},{9,10},{10,1... | collective-permute-start | bytes 1179656 | tf_op jit(solution)/shard_map/ppermute | solution.py:154
  7.3 4.0 %collective-permute-start.1 = (bf16[192,1024]{1,0:T(8,128)(2,1)S(1)}, bf16[192,1024]{1,0:T(8,128)(2,1)S(1)}, u32[]{:S(2)}, u32[]{:S(2)}) collective-permute-start(bf16[192,1024]{1,0:T(8,128)(2,1)S(1)} %pad_maximum_fusion.1), channel_id=1, source_target_pairs={{0,2},{1,3},{2,4},{3,5},{4,6},{5,7},{6,8},{7,9},{8,10},{9,11},{10,... | collective-permute-start | bytes 1179656 | tf_op jit(solution)/shard_map/ppermute | solution.py:154
  11.3 5.8 %collective-permute-start = (bf16[192,1024]{1,0:T(8,128)(2,1)S(1)}, bf16[192,1024]{1,0:T(8,128)(2,1)S(1)}, u32[]{:S(2)}, u32[]{:S(2)}) collective-permute-start(bf16[192,1024]{1,0:T(8,128)(2,1)S(1)} %pad_maximum_fusion.1), channel_id=1, source_target_pairs={{0,3},{1,4},{2,5},{3,6},{4,7},{5,8},{6,9},{7,10},{8,11},{9,12},{10... | collective-permute-start | bytes 1179656 | tf_op jit(solution)/shard_map/ppermute | solution.py:154
  17.1 1.7 fusion.103
  18.8 1.9 fusion.102
  22.3 1.8 copy.23
  24.4 2.7 %collective-permute-done = bf16[192,1024]{1,0:T(8,128)(2,1)S(1)} collective-permute-done((bf16[192,1024]{1,0:T(8,128)(2,1)S(1)}, bf16[192,1024]{1,0:T(8,128)(2,1)S(1)}, u32[]{:S(2)}, u32[]{:S(2)}) %collective-permute-start) | collective-permute-done | bytes 393248 | tf_op jit(solution)/shard_map/ppermute | solution.py:154
  29.0 2.2 %fusion.4 = (f32[8,192]{1,0:T(8,128)S(1)}, f32[8,768,192]{1,2,0:T(8,128)S(1)}) fusion(pred[192,768]{1,0:T(8,128)(4,1)S(1)} %fusion.89, bf16[768,8,64]{0,2,1:T(8,128)(2,1)S(1)} %bitcast.107, bf16[192,8,64]{0,2,1:T(8,128)(2,1)} %bitcast.110), kind=kOutput, calls=%fused_computation.11 | convolution fusion | flops 154532352 | bytes 5855232 | tf_op jit(solution)/shard_map/qhd,khd->hqk/dot_general | solution.py:229
  34.9 8.7 %collective-permute-start.3 = (bf16[30,1024]{1,0:T(8,128)(2,1)S(1)}, bf16[30,1024]{1,0:T(8,128)(2,1)S(1)}, u32[]{:S(2)}, u32[]{:S(2)}) collective-permute-start(bf16[30,1024]{1,0:T(8,128)(2,1)S(1)} %get-tuple-element.31), channel_id=1, source_target_pairs={{0,1},{1,2},{2,3},{3,4},{4,5},{5,6},{6,7},{7,8},{8,9},{9,10},{10,1... | collective-permute-start | bytes 184328 | tf_op jit(solution)/shard_map/ppermute | solution.py:154
  45.7 5.1 %collective-permute-done.4 = bf16[30,2048]{1,0:T(8,128)(2,1)S(1)} collective-permute-done((bf16[30,2048]{1,0:T(8,128)(2,1)S(1)}, bf16[30,2048]{1,0:T(8,128)(2,1)S(1)}, u32[]{:S(2)}, u32[]{:S(2)}) %collective-permute-start.4) | collective-permute-done | bytes 122912 | tf_op jit(solution)/shard_map/ppermute | solution.py:154
  51.3 4.7 %add_multiply_fusion = (f32[222,1024]{1,0:T(8,128)S(1)}, f32[222,1024]{1,0:T(8,128)}) fusion(bf16[30,1024]{1,0:T(8,128)(2,1)S(1)} %get-tuple-element.65, bf16[192,1024]{1,0:T(8,128)(2,1)S(1)} %bitcast.124, f32[252,1024]{1,0:T(8,128)S(1)} %maximum_convert_fusion, f32[1024]{0:T(1024)S(1)} %bitcast.146, f32[1024]{0:T(1024)S(1)} %bitcast.148, ...), kind=kLoop, calls=%fused_computation.85 | loop fusion | flops 16594944 | bytes 30588928 | tf_op jit(solution)/shard_map/mul | solution.py:253
  56.0 3.0 %fusion.57 = bf16[192,1024]{1,0:T(8,128)(2,1)S(1)} fusion(f32[222,1024]{1,0:T(8,128)S(1)} %get-tuple-element.22, f32[1024]{0:T(1024)S(1)} %bitcast.147, f32[1024]{0:T(1024)S(1)} %bitcast.149, f32[1024]{0:T(1024)S(1)} %bitcast.153, f32[1024]{0:T(1024)S(1)} %bitcast.155, f32[1024]{0:T(1024)S(1)} %bitcast.157, f32[1024]{0:T(1024)S(1)} %bitcast.159, ...), kind=kLoop, calls=%fused_computation.96 | loop fusion | flops 12189696 | bytes 24899584 | tf_op jit(solution)/shard_map/convert_element_type | solution.py:256
  60.2 1.8 copy.24
  63.2 5.0 %fusion.5 = f32[8,64,768]{2,1,0:T(8,128)} fusion(bf16[192,8,64]{0,2,1:T(8,128)(2,1)} %bitcast.115, f32[8,768,192]{1,2,0:T(8,128)} %copy-done.1, f32[8,192]{1,0:T(8,128)} %log_add_fusion, pred[192,768]{1,0:T(8,128)(4,1)S(1)} %fusion.89), kind=kOutput, calls=%fused_computation.12 | convolution fusion | flops 156893184 | bytes 6641664 | tf_op jit(solution)/shard_map/hqk,qhd->khd/dot_general | solution.py:269
  68.2 3.8 %multiply_convert_fusion = bf16[8,192,768]{2,1,0:T(8,128)(2,1)S(1)} fusion(f32[8,768,192]{1,2,0:T(8,128)} %copy-done.1, f32[8,192]{1,0:T(8,128)S(1)} %fusion.90, f32[8,192]{1,0:T(8,128)S(1)} %copy-done.48, pred[192,768]{1,0:T(8,128)(4,1)S(1)} %fusion.89, bf16[192,8,64]{0,2,1:T(8,128)(2,1)S(1)} %bitcast.116, bf16[768,8,64]{0,2,1:T(8,128)(2,1)S(1)} %bitcast.119), kind=kOutput, calls=%fused_computation.1 | convolution fusion | flops 159252480 | bytes 8220672 | tf_op jit(solution)/shard_map/qhd,khd->hqk/dot_general | solution.py:272
  73.7 1.7 convolution_multiply_fusion
  75.4 1.8 fusion.105.refs_0_
  77.2 3.0 %copy.25 = f32[768,512]{1,0:T(8,128)} copy(f32[768,512]{0,1:T(8,128)} %bitcast.109) | data formatting | bytes 3145728 | tf_op jit(solution)/shard_map/reshape | solution.py:284
  80.2 3.1 %copy.26 = f32[768,512]{1,0:T(8,128)} copy(f32[768,512]{0,1:T(8,128)} %bitcast.114) | data formatting | bytes 3145728 | tf_op jit(solution)/shard_map/reshape | solution.py:284
  83.2 2.2 fusion.3
  93.7 1.9 copy.27
  95.6 6.4 %shard_map.109.refs_1_ = f32[32,1024]{1,0:T(8,128)} custom-call(f32[192,1024]{1,0:T(8,128)} %slice.517.dmixed_ref, f32[222,1024]{1,0:T(8,128)} %slice.513.extended_ref), custom_call_target="tpu_custom_call" | custom-call | tf_op jit(solution)/shard_map/pallas_call | solution.py:190
  101.9 109.6 %shard_map.110 = (f32[512,1024]{1,0:T(8,128)}, f32[32,1024]{1,0:T(8,128)}) custom-call(f32[512,1024]{1,0:T(8,128)} %fusion.105.refs_0_, f32[32,1024]{1,0:T(8,128)} %shard_map.109.refs_1_), custom_call_target="tpu_custom_call" | custom-call | tf_op jit(solution)/shard_map/pallas_call | solution.py:141
  211.5 2.0 fusion.91
  (138 shorter events, 27.1 us)
Async XLA Ops:
  0.6 33.8 %copy-start = (bf16[512,1024]{1,0:T(8,128)(2,1)S(1)}, bf16[512,1024]{1,0:T(8,128)(2,1)}, u32[]{:S(2)}) copy-start(bf16[512,1024]{1,0:T(8,128)(2,1)} %param.9) | copy-start | bytes 3145732
  1.8 22.6 %collective-permute-start.2 = (bf16[192,1024]{1,0:T(8,128)(2,1)S(1)}, bf16[192,1024]{1,0:T(8,128)(2,1)S(1)}, u32[]{:S(2)}, u32[]{:S(2)}) collective-permute-start(bf16[192,1024]{1,0:T(8,128)(2,1)S(1)} %pad_maximum_fusion.1), channel_id=1, source_target_pairs={{0,1},{1,2},{2,3},{3,4},{4,5},{5,6},{6,7},{7,8},{8,9},{9,10},{10,1... | collective-permute-start | bytes 1179656 | tf_op jit(solution)/shard_map/ppermute | solution.py:154
  7.3 17.1 %collective-permute-start.1 = (bf16[192,1024]{1,0:T(8,128)(2,1)S(1)}, bf16[192,1024]{1,0:T(8,128)(2,1)S(1)}, u32[]{:S(2)}, u32[]{:S(2)}) collective-permute-start(bf16[192,1024]{1,0:T(8,128)(2,1)S(1)} %pad_maximum_fusion.1), channel_id=1, source_target_pairs={{0,2},{1,3},{2,4},{3,5},{4,6},{5,7},{6,8},{7,9},{8,10},{9,11},{10,... | collective-permute-start | bytes 1179656 | tf_op jit(solution)/shard_map/ppermute | solution.py:154
  11.3 15.8 %collective-permute-start = (bf16[192,1024]{1,0:T(8,128)(2,1)S(1)}, bf16[192,1024]{1,0:T(8,128)(2,1)S(1)}, u32[]{:S(2)}, u32[]{:S(2)}) collective-permute-start(bf16[192,1024]{1,0:T(8,128)(2,1)S(1)} %pad_maximum_fusion.1), channel_id=1, source_target_pairs={{0,3},{1,4},{2,5},{3,6},{4,7},{5,8},{6,9},{7,10},{8,11},{9,12},{10... | collective-permute-start | bytes 1179656 | tf_op jit(solution)/shard_map/ppermute | solution.py:154
  34.1 16.9 %copy-start.8 = (bf16[192,8,64]{0,2,1:T(8,128)(2,1)}, bf16[192,8,64]{0,2,1:T(8,128)(2,1)S(1)}, u32[]{:S(2)}) copy-start(bf16[192,8,64]{0,2,1:T(8,128)(2,1)S(1)} %fusion.18) | copy-start | bytes 589828
  34.1 16.9 %copy-start.14 = (bf16[1,192,1024]{2,1,0:T(8,128)(2,1)S(1)}, bf16[1,192,1024]{2,1,0:T(8,128)(2,1)}, u32[]{:S(2)}) copy-start(bf16[1,192,1024]{2,1,0:T(8,128)(2,1)} %param.11) | copy-start | bytes 1179652
  34.1 16.9 %copy-start.17 = (f32[1,1024]{1,0:T(1,128)S(1)}, f32[1,1024]{1,0:T(1,128)}, u32[]{:S(2)}) copy-start(f32[1,1024]{1,0:T(1,128)} %get-tuple-element.52) | copy-start | bytes 12292
  34.1 16.9 %copy-start.18 = (f32[1,1024]{1,0:T(1,128)S(1)}, f32[1,1024]{1,0:T(1,128)}, u32[]{:S(2)}) copy-start(f32[1,1024]{1,0:T(1,128)} %get-tuple-element.53) | copy-start | bytes 12292
  34.1 16.9 %copy-start.19 = (f32[1,1024]{1,0:T(1,128)S(1)}, f32[1,1024]{1,0:T(1,128)}, u32[]{:S(2)}) copy-start(f32[1,1024]{1,0:T(1,128)} %get-tuple-element.54) | copy-start | bytes 12292
  34.1 16.9 %copy-start.20 = (f32[1,1024]{1,0:T(1,128)S(1)}, f32[1,1024]{1,0:T(1,128)}, u32[]{:S(2)}) copy-start(f32[1,1024]{1,0:T(1,128)} %get-tuple-element.55) | copy-start | bytes 12292
  34.2 16.9 %copy-start.21 = (f32[1,1024]{1,0:T(1,128)S(1)}, f32[1,1024]{1,0:T(1,128)}, u32[]{:S(2)}) copy-start(f32[1,1024]{1,0:T(1,128)} %get-tuple-element.56) | copy-start | bytes 12292
  34.2 16.9 %copy-start.22 = (f32[1,1024]{1,0:T(1,128)S(1)}, f32[1,1024]{1,0:T(1,128)}, u32[]{:S(2)}) copy-start(f32[1,1024]{1,0:T(1,128)} %get-tuple-element.57) | copy-start | bytes 12292
  34.2 16.9 %copy-start.23 = (f32[1,1024]{1,0:T(1,128)S(1)}, f32[1,1024]{1,0:T(1,128)}, u32[]{:S(2)}) copy-start(f32[1,1024]{1,0:T(1,128)} %get-tuple-element.58) | copy-start | bytes 12292
  34.2 16.9 %copy-start.24 = (f32[1,1024]{1,0:T(1,128)S(1)}, f32[1,1024]{1,0:T(1,128)}, u32[]{:S(2)}) copy-start(f32[1,1024]{1,0:T(1,128)} %get-tuple-element.59) | copy-start | bytes 12292
  34.2 16.9 %copy-start.25 = (f32[1,1024]{1,0:T(1,128)S(1)}, f32[1,1024]{1,0:T(1,128)}, u32[]{:S(2)}) copy-start(f32[1,1024]{1,0:T(1,128)} %get-tuple-element.60) | copy-start | bytes 12292
  34.2 16.9 %copy-start.26 = (f32[1,1024]{1,0:T(1,128)S(1)}, f32[1,1024]{1,0:T(1,128)}, u32[]{:S(2)}) copy-start(f32[1,1024]{1,0:T(1,128)} %get-tuple-element.61) | copy-start | bytes 12292
  34.2 16.9 %copy-start.27 = (f32[1,1024]{1,0:T(1,128)S(1)}, f32[1,1024]{1,0:T(1,128)}, u32[]{:S(2)}) copy-start(f32[1,1024]{1,0:T(1,128)} %get-tuple-element.62) | copy-start | bytes 12292
  34.9 16.0 %collective-permute-start.3 = (bf16[30,1024]{1,0:T(8,128)(2,1)S(1)}, bf16[30,1024]{1,0:T(8,128)(2,1)S(1)}, u32[]{:S(2)}, u32[]{:S(2)}) collective-permute-start(bf16[30,1024]{1,0:T(8,128)(2,1)S(1)} %get-tuple-element.31), channel_id=1, source_target_pairs={{0,1},{1,2},{2,3},{3,4},{4,5},{5,6},{6,7},{7,8},{8,9},{9,10},{10,1... | collective-permute-start | bytes 184328 | tf_op jit(solution)/shard_map/ppermute | solution.py:154
  43.6 7.2 %collective-permute-start.4 = (bf16[30,2048]{1,0:T(8,128)(2,1)S(1)}, bf16[30,2048]{1,0:T(8,128)(2,1)S(1)}, u32[]{:S(2)}, u32[]{:S(2)}) collective-permute-start(bf16[30,2048]{1,0:T(8,128)(2,1)S(1)} %pad_maximum_fusion.2), channel_id=1, source_target_pairs={{1,0},{2,1},{3,2},{4,3},{5,4},{6,5},{7,6},{8,7},{9,8},{10,9},{11,1... | collective-permute-start | bytes 368648 | tf_op jit(solution)/shard_map/ppermute | solution.py:154
  86.5 127.1 %collective-permute-start.5 = (bf16[192,1024]{1,0:T(8,128)(2,1)}, bf16[192,1024]{1,0:T(8,128)(2,1)}, u32[]{:S(2)}, u32[]{:S(2)}) collective-permute-start(bf16[192,1024]{1,0:T(8,128)(2,1)} %get-tuple-element.24), channel_id=1, source_target_pairs={{3,0},{4,1},{5,2},{6,3},{7,4},{8,5},{9,6},{10,7},{11,8},{12,9},{13... | collective-permute-start | bytes 1179656 | tf_op jit(solution)/shard_map/ppermute | solution.py:154
  87.7 125.8 %collective-permute-start.7 = (bf16[192,1024]{1,0:T(8,128)(2,1)}, bf16[192,1024]{1,0:T(8,128)(2,1)}, u32[]{:S(2)}, u32[]{:S(2)}) collective-permute-start(bf16[192,1024]{1,0:T(8,128)(2,1)} %get-tuple-element.25), channel_id=1, source_target_pairs={{1,0},{2,1},{3,2},{4,3},{5,4},{6,5},{7,6},{8,7},{9,8},{10,9},{11,1... | collective-permute-start | bytes 1179656 | tf_op jit(solution)/shard_map/ppermute | solution.py:154
  89.0 124.5 %collective-permute-start.6 = (bf16[192,1024]{1,0:T(8,128)(2,1)}, bf16[192,1024]{1,0:T(8,128)(2,1)}, u32[]{:S(2)}, u32[]{:S(2)}) collective-permute-start(bf16[192,1024]{1,0:T(8,128)(2,1)} %get-tuple-element.26), channel_id=1, source_target_pairs={{2,0},{3,1},{4,2},{5,3},{6,4},{7,5},{8,6},{9,7},{10,8},{11,9},{12,... | collective-permute-start | bytes 1179656 | tf_op jit(solution)/shard_map/ppermute | solution.py:154
  93.7 117.8 %copy-start.4 = (f32[222,1024]{1,0:T(8,128)S(1)}, f32[222,1024]{1,0:T(8,128)}, u32[]{:S(2)}) copy-start(f32[222,1024]{1,0:T(8,128)} %get-tuple-element.23) | copy-start | bytes 2727940
  93.7 119.8 %copy-start.2 = (f32[768,512]{1,0:T(8,128)S(1)}, f32[768,512]{1,0:T(8,128)}, u32[]{:S(2)}) copy-start(f32[768,512]{1,0:T(8,128)} %copy.25) | copy-start | bytes 4718596
  (33 other events, 394.1 us)

commit v9 on v8

--- a/solution.py
+++ b/solution.py
@@ -148,6 +148,71 @@
     )(*arrays)
 
 
+def halo_body(edge_right_ref, edge_left_ref, before_ref, following_ref, send_sem, recv_sem):
+    count = lax.axis_size("blk")
+    me = lax.axis_index("blk")
+    dp = lax.axis_index("dp")
+    has_left = (me + count - 1) // count
+    has_right = (2 * count - 2 - me) // count
+    left = (dp, (me + count - 1) % count)
+    right = (dp, (me + 1) % count)
+    barrier = pltpu.get_barrier_semaphore()
+
+    @pl.when(has_left == 1)
+    def _():
+        pl.semaphore_signal(barrier, 1, device_id=left, device_id_type=MESH_ID)
+
+    @pl.when(has_right == 1)
+    def _():
+        pl.semaphore_signal(barrier, 1, device_id=right, device_id_type=MESH_ID)
+
+    pl.semaphore_wait(barrier, has_left + has_right)
+    to_right = pltpu.make_async_remote_copy(
+        src_ref=edge_right_ref, dst_ref=before_ref, send_sem=send_sem.at[0],
+        recv_sem=recv_sem.at[0], device_id=right, device_id_type=MESH_ID)
+    to_left = pltpu.make_async_remote_copy(
+        src_ref=edge_left_ref, dst_ref=following_ref, send_sem=send_sem.at[1],
+        recv_sem=recv_sem.at[1], device_id=left, device_id_type=MESH_ID)
+
+    @pl.when(has_right == 1)
+    def _():
+        to_right.start()
+
+    @pl.when(has_left == 1)
+    def _():
+        to_left.start()
+
+    @pl.when(has_left == 0)
+    def _():
+        before_ref[...] = jnp.zeros(before_ref.shape, before_ref.dtype)
+
+    @pl.when(has_right == 0)
+    def _():
+        following_ref[...] = jnp.zeros(following_ref.shape, following_ref.dtype)
+
+    @pl.when(has_right == 1)
+    def _():
+        to_right.wait_send()
+        to_left.wait_recv()
+
+    @pl.when(has_left == 1)
+    def _():
+        to_left.wait_send()
+        to_right.wait_recv()
+
+
+def halo_exchange(edge_right, edge_left):
+    return pl.pallas_call(
+        halo_body,
+        out_shape=[jax.ShapeDtypeStruct(edge_right.shape, edge_right.dtype),
+                   jax.ShapeDtypeStruct(edge_left.shape, edge_left.dtype)],
+        in_specs=[pl.BlockSpec(memory_space=pltpu.VMEM)] * 2,
+        out_specs=[pl.BlockSpec(memory_space=pltpu.VMEM)] * 2,
+        scratch_shapes=[pltpu.SemaphoreType.DMA((2,)), pltpu.SemaphoreType.DMA((2,))],
+        compiler_params=pltpu.CompilerParams(collective_id=1, has_side_effects=True),
+    )(edge_right, edge_left)
+
+
 def from_behind(block, axis, distance):
     devices = range(lax.axis_size(axis))
     route = [(i - distance, i) for i in devices if i - distance in devices]
@@ -241,9 +306,9 @@
     flat = attended.reshape(row_count, ATT)
 
     hidden = jnp.dot(flat, out_weight, preferred_element_type=jnp.float32).astype(jnp.bfloat16)
-    before = from_behind(hidden[-edge_rows:], "blk", 1)
-    following = from_behind(
-        jnp.concatenate([hidden[:edge_rows], cotangent[0][:edge_rows]], axis=1), "blk", -1
+    before, following = halo_exchange(
+        hidden[-edge_rows:],
+        jnp.concatenate([hidden[:edge_rows], cotangent[0][:edge_rows]], axis=1),
     )
     width = hidden.shape[1]
     extended = jnp.concatenate([before, hidden, following[:, :width]], axis=0).astype(jnp.float32)

time: 219 us -> 222 us (1.014)
  Pallas kernels: 116 us -> 129 us
  starting transfers between devices: 29.5 us -> 19.3 us
  waiting for transfers between devices: 7.88 us -> 2.74 us
  other arithmetic: 20.7 us -> 23.3 us
  local copies, waits for them, and re-layouts: 23.3 us -> 25.6 us
    pallas_call x0 -> x1, Pallas kernels: none -> 11.5 us  [halo_exchange(): pl.pallas_call(halo_body, out_shape=[jax.ShapeDtypeStruct(edge_right.shap...]
    ppermute x8 -> x6, starting transfers between devices: 29.5 us -> 19.3 us  [from_behind(): return lax.ppermute(block, axis, route)]
    ppermute x8 -> x6, waiting for transfers between devices: 7.88 us -> 2.74 us  [from_behind(): return lax.ppermute(block, axis, route)]
  transfers between devices with their start and end apart: 8 -> 6, of which waited for: 2 -> 1; matrix products, arithmetic and copies ran while one was open for 7% -> 7% of each run, Pallas kernels for 53% -> 53%
where the time goes in v9:
time: 222 us; the launch traced here: 221 us
  Pallas kernels  129 us (58%)
  local copies, waits for them, and re-layouts  25.6 us (12%)
  other arithmetic  23.3 us (10%)
  starting transfers between devices  19.3 us (9%)
  matrix products  19.1 us (9%)
  waiting for transfers between devices  2.74 us (1%)
    pallas_call x1, Pallas kernels, allreduce(): pl.pallas_call(functools.partial(allreduce_kernel, bits, splits, len(arra...  111 us
    ppermute x6, starting transfers between devices, from_behind(): return lax.ppermute(block, axis, route)  19.3 us
    pallas_call x1, Pallas kernels, halo_exchange(): pl.pallas_call(halo_body, out_shape=[jax.ShapeDtypeStruct(edge_right.shap...  11.5 us
    unnamed x102, local copies, waits for them, and re-layouts  6.55 us
    pallas_call x1, Pallas kernels, kernel_taps(): pl.pallas_call(functools.partial(kernel_taps_body, tap_count), out_shape=...  6.36 us
    slice x4, local copies, waits for them, and re-layouts, depthwise(): term = conv_kernel[tap_index] * extended[first_row:first_row + row_count]  5.72 us
    mul x1, other arithmetic, per_device(): dmixed_all = upstream * sigma_all * (1.0 + mixed_all * (1.0 - sigma_all))  5.63 us
    dot_general x1, matrix products, per_device(): jnp.einsum('hqk,qhd->khd', probs.astype(jnp.bfloat16), dout_heads, prefer...  5.1 us
  transfers between devices with their start and end apart: 6, of which 1 were waited for; matrix products, arithmetic and copies ran while one was open for 7% of the time, Pallas kernels for 53%

profile of v9, /device:TPU:1, one launch (start us, length us, event | category | flops | bytes accessed | tf_op | source)
XLA Modules:
  0.0 220.9 jit_solution(11921233096299562929)
XLA Ops:
  1.8 5.5 %collective-permute-start.2 = (bf16[192,1024]{1,0:T(8,128)(2,1)S(1)}, bf16[192,1024]{1,0:T(8,128)(2,1)S(1)}, u32[]{:S(2)}, u32[]{:S(2)}) collective-permute-start(bf16[192,1024]{1,0:T(8,128)(2,1)S(1)} %pad_maximum_fusion.1), channel_id=1, source_target_pairs={{0,1},{1,2},{2,3},{3,4},{4,5},{5,6},{6,7},{7,8},{8,9},{9,10},{10,1... | collective-permute-start | bytes 1179656 | tf_op jit(solution)/shard_map/ppermute | solution.py:219
  7.3 4.0 %collective-permute-start.1 = (bf16[192,1024]{1,0:T(8,128)(2,1)S(1)}, bf16[192,1024]{1,0:T(8,128)(2,1)S(1)}, u32[]{:S(2)}, u32[]{:S(2)}) collective-permute-start(bf16[192,1024]{1,0:T(8,128)(2,1)S(1)} %pad_maximum_fusion.1), channel_id=1, source_target_pairs={{0,2},{1,3},{2,4},{3,5},{4,6},{5,7},{6,8},{7,9},{8,10},{9,11},{10,... | collective-permute-start | bytes 1179656 | tf_op jit(solution)/shard_map/ppermute | solution.py:219
  11.3 5.8 %collective-permute-start = (bf16[192,1024]{1,0:T(8,128)(2,1)S(1)}, bf16[192,1024]{1,0:T(8,128)(2,1)S(1)}, u32[]{:S(2)}, u32[]{:S(2)}) collective-permute-start(bf16[192,1024]{1,0:T(8,128)(2,1)S(1)} %pad_maximum_fusion.1), channel_id=1, source_target_pairs={{0,3},{1,4},{2,5},{3,6},{4,7},{5,8},{6,9},{7,10},{8,11},{9,12},{10... | collective-permute-start | bytes 1179656 | tf_op jit(solution)/shard_map/ppermute | solution.py:219
  17.1 1.7 fusion.103
  18.8 1.9 fusion.102
  22.3 1.8 copy.23
  24.4 2.7 %collective-permute-done = bf16[192,1024]{1,0:T(8,128)(2,1)S(1)} collective-permute-done((bf16[192,1024]{1,0:T(8,128)(2,1)S(1)}, bf16[192,1024]{1,0:T(8,128)(2,1)S(1)}, u32[]{:S(2)}, u32[]{:S(2)}) %collective-permute-start) | collective-permute-done | bytes 393248 | tf_op jit(solution)/shard_map/ppermute | solution.py:219
  29.0 2.2 fusion.4
  37.2 11.5 %shard_map.109 = (bf16[30,1024]{1,0:T(8,128)(2,1)}, bf16[30,2048]{1,0:T(8,128)(2,1)}) custom-call(bf16[30,1024]{1,0:T(8,128)(2,1)} %get-tuple-element.36.edge_right_ref, bf16[30,2048]{1,0:T(8,128)(2,1)} %pad_maximum_fusion.2.edge_left_ref), custom_call_target="tpu_custom_call" | custom-call | tf_op jit(solution)/shard_map/pallas_call | solution.py:205
  50.9 5.6 %add_multiply_fusion = (f32[222,1024]{1,0:T(8,128)S(1)}, f32[222,1024]{1,0:T(8,128)}) fusion(bf16[30,1024]{1,0:T(8,128)(2,1)S(1)} %get-tuple-element.69, bf16[192,1024]{1,0:T(8,128)(2,1)S(1)} %bitcast.124, f32[252,1024]{1,0:T(8,128)S(1)} %maximum_convert_fusion, f32[1024]{0:T(1024)} %bitcast.146, f32[1024]{0:T(1024)} %bitcast.148, f32[1024]{0:T(1024)} %bitcast.152, ...), kind=kLoop, calls=%fused_computation.85 | loop fusion | flops 16594944 | bytes 30588928 | tf_op jit(solution)/shard_map/mul | solution.py:318
  56.9 3.1 %fusion.57 = bf16[192,1024]{1,0:T(8,128)(2,1)S(1)} fusion(f32[222,1024]{1,0:T(8,128)S(1)} %get-tuple-element.26, f32[1024]{0:T(1024)S(1)} %bitcast.147, f32[1024]{0:T(1024)S(1)} %bitcast.149, f32[1024]{0:T(1024)S(1)} %bitcast.153, f32[1024]{0:T(1024)S(1)} %bitcast.155, f32[1024]{0:T(1024)S(1)} %bitcast.157, f32[1024]{0:T(1024)S(1)} %bitcast.159, ...), kind=kLoop, calls=%fused_computation.96 | loop fusion | flops 12189696 | bytes 24899584 | tf_op jit(solution)/shard_map/convert_element_type | solution.py:321
  61.1 1.8 copy.24
  64.1 5.1 %fusion.5 = f32[8,64,768]{2,1,0:T(8,128)} fusion(bf16[192,8,64]{0,2,1:T(8,128)(2,1)} %bitcast.115, f32[8,768,192]{1,2,0:T(8,128)} %copy-done.1, f32[8,192]{1,0:T(8,128)} %log_add_fusion, pred[192,768]{1,0:T(8,128)(4,1)S(1)} %fusion.89), kind=kOutput, calls=%fused_computation.12 | convolution fusion | flops 156893184 | bytes 6641664 | tf_op jit(solution)/shard_map/hqk,qhd->khd/dot_general | solution.py:334
  69.2 3.8 %multiply_convert_fusion = bf16[8,192,768]{2,1,0:T(8,128)(2,1)S(1)} fusion(f32[8,768,192]{1,2,0:T(8,128)} %copy-done.1, f32[8,192]{1,0:T(8,128)S(1)} %fusion.90, f32[8,192]{1,0:T(8,128)S(1)} %copy-done.48, pred[192,768]{1,0:T(8,128)(4,1)S(1)} %fusion.89, bf16[192,8,64]{0,2,1:T(8,128)(2,1)S(1)} %bitcast.116, bf16[768,8,64]{0,2,1:T(8,128)(2,1)S(1)} %bitcast.119), kind=kOutput, calls=%fused_computation.1 | convolution fusion | flops 159252480 | bytes 8220672 | tf_op jit(solution)/shard_map/qhd,khd->hqk/dot_general | solution.py:337
  74.6 1.7 convolution_multiply_fusion
  76.3 1.8 fusion.105.refs_0_
  78.1 3.0 %copy.25 = f32[768,512]{1,0:T(8,128)} copy(f32[768,512]{0,1:T(8,128)} %bitcast.109) | data formatting | bytes 3145728 | tf_op jit(solution)/shard_map/reshape | solution.py:349
  81.1 3.0 %copy.26 = f32[768,512]{1,0:T(8,128)} copy(f32[768,512]{0,1:T(8,128)} %bitcast.114) | data formatting | bytes 3145728 | tf_op jit(solution)/shard_map/reshape | solution.py:349
  84.1 2.2 fusion.3
  94.7 1.9 copy.27
  96.6 6.4 %shard_map.110.refs_1_ = f32[32,1024]{1,0:T(8,128)} custom-call(f32[192,1024]{1,0:T(8,128)} %slice.515.dmixed_ref, f32[222,1024]{1,0:T(8,128)} %slice.512.extended_ref), custom_call_target="tpu_custom_call" | custom-call | tf_op jit(solution)/shard_map/pallas_call | solution.py:255
  103.0 111.4 %shard_map.111 = (f32[512,1024]{1,0:T(8,128)}, f32[32,1024]{1,0:T(8,128)}) custom-call(f32[512,1024]{1,0:T(8,128)} %fusion.105.refs_0_, f32[32,1024]{1,0:T(8,128)} %shard_map.110.refs_1_), custom_call_target="tpu_custom_call" | custom-call | tf_op jit(solution)/shard_map/pallas_call | solution.py:141
  214.4 2.0 fusion.91
  216.4 1.7 fusion.55
  (135 shorter events, 27.8 us)
Async XLA Ops:
  0.6 34.8 %copy-start = (bf16[512,1024]{1,0:T(8,128)(2,1)S(1)}, bf16[512,1024]{1,0:T(8,128)(2,1)}, u32[]{:S(2)}) copy-start(bf16[512,1024]{1,0:T(8,128)(2,1)} %param.9) | copy-start | bytes 3145732
  1.8 22.6 %collective-permute-start.2 = (bf16[192,1024]{1,0:T(8,128)(2,1)S(1)}, bf16[192,1024]{1,0:T(8,128)(2,1)S(1)}, u32[]{:S(2)}, u32[]{:S(2)}) collective-permute-start(bf16[192,1024]{1,0:T(8,128)(2,1)S(1)} %pad_maximum_fusion.1), channel_id=1, source_target_pairs={{0,1},{1,2},{2,3},{3,4},{4,5},{5,6},{6,7},{7,8},{8,9},{9,10},{10,1... | collective-permute-start | bytes 1179656 | tf_op jit(solution)/shard_map/ppermute | solution.py:219
  7.3 17.1 %collective-permute-start.1 = (bf16[192,1024]{1,0:T(8,128)(2,1)S(1)}, bf16[192,1024]{1,0:T(8,128)(2,1)S(1)}, u32[]{:S(2)}, u32[]{:S(2)}) collective-permute-start(bf16[192,1024]{1,0:T(8,128)(2,1)S(1)} %pad_maximum_fusion.1), channel_id=1, source_target_pairs={{0,2},{1,3},{2,4},{3,5},{4,6},{5,7},{6,8},{7,9},{8,10},{9,11},{10,... | collective-permute-start | bytes 1179656 | tf_op jit(solution)/shard_map/ppermute | solution.py:219
  11.3 15.8 %collective-permute-start = (bf16[192,1024]{1,0:T(8,128)(2,1)S(1)}, bf16[192,1024]{1,0:T(8,128)(2,1)S(1)}, u32[]{:S(2)}, u32[]{:S(2)}) collective-permute-start(bf16[192,1024]{1,0:T(8,128)(2,1)S(1)} %pad_maximum_fusion.1), channel_id=1, source_target_pairs={{0,3},{1,4},{2,5},{3,6},{4,7},{5,8},{6,9},{7,10},{8,11},{9,12},{10... | collective-permute-start | bytes 1179656 | tf_op jit(solution)/shard_map/ppermute | solution.py:219
  34.8 15.8 %copy-start.14 = (bf16[1,192,1024]{2,1,0:T(8,128)(2,1)S(1)}, bf16[1,192,1024]{2,1,0:T(8,128)(2,1)}, u32[]{:S(2)}) copy-start(bf16[1,192,1024]{2,1,0:T(8,128)(2,1)} %param.11) | copy-start | bytes 1179652
  50.6 6.0 %copy-start.17 = (f32[1,1024]{1,0:T(1,128)S(1)}, f32[1,1024]{1,0:T(1,128)}, u32[]{:S(2)}) copy-start(f32[1,1024]{1,0:T(1,128)} %get-tuple-element.56) | copy-start | bytes 12292
  50.6 5.9 %copy-start.18 = (f32[1,1024]{1,0:T(1,128)S(1)}, f32[1,1024]{1,0:T(1,128)}, u32[]{:S(2)}) copy-start(f32[1,1024]{1,0:T(1,128)} %get-tuple-element.57) | copy-start | bytes 12292
  50.6 5.9 %copy-start.19 = (f32[1,1024]{1,0:T(1,128)S(1)}, f32[1,1024]{1,0:T(1,128)}, u32[]{:S(2)}) copy-start(f32[1,1024]{1,0:T(1,128)} %get-tuple-element.58) | copy-start | bytes 12292
  50.6 5.9 %copy-start.20 = (f32[1,1024]{1,0:T(1,128)S(1)}, f32[1,1024]{1,0:T(1,128)}, u32[]{:S(2)}) copy-start(f32[1,1024]{1,0:T(1,128)} %get-tuple-element.59) | copy-start | bytes 12292
  50.6 5.9 %copy-start.21 = (f32[1,1024]{1,0:T(1,128)S(1)}, f32[1,1024]{1,0:T(1,128)}, u32[]{:S(2)}) copy-start(f32[1,1024]{1,0:T(1,128)} %get-tuple-element.60) | copy-start | bytes 12292
  50.7 5.9 %copy-start.22 = (f32[1,1024]{1,0:T(1,128)S(1)}, f32[1,1024]{1,0:T(1,128)}, u32[]{:S(2)}) copy-start(f32[1,1024]{1,0:T(1,128)} %get-tuple-element.61) | copy-start | bytes 12292
  50.7 5.9 %copy-start.23 = (f32[1,1024]{1,0:T(1,128)S(1)}, f32[1,1024]{1,0:T(1,128)}, u32[]{:S(2)}) copy-start(f32[1,1024]{1,0:T(1,128)} %get-tuple-element.62) | copy-start | bytes 12292
  50.7 5.9 %copy-start.24 = (f32[1,1024]{1,0:T(1,128)S(1)}, f32[1,1024]{1,0:T(1,128)}, u32[]{:S(2)}) copy-start(f32[1,1024]{1,0:T(1,128)} %get-tuple-element.63) | copy-start | bytes 12292
  50.7 5.9 %copy-start.25 = (f32[1,1024]{1,0:T(1,128)S(1)}, f32[1,1024]{1,0:T(1,128)}, u32[]{:S(2)}) copy-start(f32[1,1024]{1,0:T(1,128)} %get-tuple-element.64) | copy-start | bytes 12292
  50.7 5.9 %copy-start.26 = (f32[1,1024]{1,0:T(1,128)S(1)}, f32[1,1024]{1,0:T(1,128)}, u32[]{:S(2)}) copy-start(f32[1,1024]{1,0:T(1,128)} %get-tuple-element.65) | copy-start | bytes 12292
  50.7 5.9 %copy-start.27 = (f32[1,1024]{1,0:T(1,128)S(1)}, f32[1,1024]{1,0:T(1,128)}, u32[]{:S(2)}) copy-start(f32[1,1024]{1,0:T(1,128)} %get-tuple-element.66) | copy-start | bytes 12292
  50.7 5.9 %copy-start.28 = (f32[1,1024]{1,0:T(1,128)S(1)}, f32[1,1024]{1,0:T(1,128)}, u32[]{:S(2)}) copy-start(f32[1,1024]{1,0:T(1,128)} %get-tuple-element.67) | copy-start | bytes 12292
  50.7 5.9 %copy-start.29 = (f32[1,1024]{1,0:T(1,128)S(1)}, f32[1,1024]{1,0:T(1,128)}, u32[]{:S(2)}) copy-start(f32[1,1024]{1,0:T(1,128)} %get-tuple-element.37) | copy-start | bytes 12292
  84.1 7.3 %copy-start.3 = (f32[222,1024]{1,0:T(8,128)S(1)}, f32[222,1024]{1,0:T(8,128)}, u32[]{:S(2)}) copy-start(f32[222,1024]{1,0:T(8,128)} %get-tuple-element.27) | copy-start | bytes 2727940
  87.4 129.0 %collective-permute-start.3 = (bf16[192,1024]{1,0:T(8,128)(2,1)}, bf16[192,1024]{1,0:T(8,128)(2,1)}, u32[]{:S(2)}, u32[]{:S(2)}) collective-permute-start(bf16[192,1024]{1,0:T(8,128)(2,1)} %get-tuple-element.28), channel_id=1, source_target_pairs={{3,0},{4,1},{5,2},{6,3},{7,4},{8,5},{9,6},{10,7},{11,8},{12,9},{13... | collective-permute-start | bytes 1179656 | tf_op jit(solution)/shard_map/ppermute | solution.py:219
  88.7 127.7 %collective-permute-start.5 = (bf16[192,1024]{1,0:T(8,128)(2,1)}, bf16[192,1024]{1,0:T(8,128)(2,1)}, u32[]{:S(2)}, u32[]{:S(2)}) collective-permute-start(bf16[192,1024]{1,0:T(8,128)(2,1)} %get-tuple-element.29), channel_id=1, source_target_pairs={{1,0},{2,1},{3,2},{4,3},{5,4},{6,5},{7,6},{8,7},{9,8},{10,9},{11,1... | collective-permute-start | bytes 1179656 | tf_op jit(solution)/shard_map/ppermute | solution.py:219
  90.0 126.4 %collective-permute-start.4 = (bf16[192,1024]{1,0:T(8,128)(2,1)}, bf16[192,1024]{1,0:T(8,128)(2,1)}, u32[]{:S(2)}, u32[]{:S(2)}) collective-permute-start(bf16[192,1024]{1,0:T(8,128)(2,1)} %get-tuple-element.30), channel_id=1, source_target_pairs={{2,0},{3,1},{4,2},{5,3},{6,4},{7,5},{8,6},{9,7},{10,8},{11,9},{12,... | collective-permute-start | bytes 1179656 | tf_op jit(solution)/shard_map/ppermute | solution.py:219
  94.7 119.7 %copy-start.4 = (f32[222,1024]{1,0:T(8,128)S(1)}, f32[222,1024]{1,0:T(8,128)}, u32[]{:S(2)}) copy-start(f32[222,1024]{1,0:T(8,128)} %get-tuple-element.27) | copy-start | bytes 2727940
  94.7 121.7 %copy-start.2 = (f32[768,512]{1,0:T(8,128)S(1)}, f32[768,512]{1,0:T(8,128)}, u32[]{:S(2)}) copy-start(f32[768,512]{1,0:T(8,128)} %copy.25) | copy-start | bytes 4718596
  (31 other events, 150.1 us)

commit v10 on v8

--- a/solution.py
+++ b/solution.py
@@ -42,8 +42,8 @@
     halves = [scratch[s * n_arrays:(s + 1) * n_arrays] for s in range(n_halve)]
     base = n_halve * n_arrays
     n_double = len(bits) - n_halve
-    doubles = [scratch[base + t * n_arrays:base + (t + 1) * n_arrays] for t in range(n_double)]
-    base += n_double * n_arrays
+    doubles = [scratch[base + t * n_arrays:base + (t + 1) * n_arrays] for t in range(n_double // 2)]
+    base += n_double // 2 * n_arrays
     accs = scratch[base:base + n_arrays]
     send_sem, recv_sem = scratch[base + n_arrays:]
     me = {"dp": lax.axis_index("dp"), "blk": lax.axis_index("blk")}
@@ -71,17 +71,25 @@
         for i in range(n_arrays):
             copy = pltpu.make_async_remote_copy(
                 src_ref=window(sources[i], regions[i]), dst_ref=targets[i],
-                send_sem=send_sem.at[step, i], recv_sem=recv_sem.at[step, i],
+                send_sem=send_sem.at[step, i, 0], recv_sem=recv_sem.at[step, i, 0],
                 device_id=ids, device_id_type=MESH_ID)
             copy.start()
             copies.append(copy)
         for copy in copies:
             copy.wait()
 
+    def diagonal_of(step):
+        ids_a = partner(bits[step])[1]
+        ids_b = partner(bits[step + 1])[1]
+        return tuple(a + b - m for a, b, m in zip(ids_a, ids_b, (me["dp"], me["blk"])))
+
+    n_groups = (len(bits) - n_halve) // 2
     barrier = pltpu.get_barrier_semaphore()
     for specs in bits:
         pl.semaphore_signal(barrier, 1, device_id=partner(specs)[1], device_id_type=MESH_ID)
-    pl.semaphore_wait(barrier, len(bits))
+    for pair in range(n_groups):
+        pl.semaphore_signal(barrier, 1, device_id=diagonal_of(n_halve + 2 * pair), device_id_type=MESH_ID)
+    pl.semaphore_wait(barrier, len(bits) + n_groups)
 
     regions = [(0, x.shape[0], 0, x.shape[1]) for x in x_refs]
     plan = []
@@ -103,12 +111,36 @@
             window(accs[i], keeps[i])[...] = window(sources[i], keeps[i])[...] + halves[step][i][...]
         plan.append((ids, keeps))
         regions = keeps
-    for slot in range(n_double):
-        step = n_halve + slot
-        bit, ids = partner(bits[step])
-        exchange(step, ids, accs, [d.at[...] for d in doubles[slot]], regions)
-        for i in range(n_arrays):
-            window(accs[i], regions[i])[...] = window(accs[i], regions[i])[...] + doubles[slot][i][...]
+    for pair in range(n_double // 2):
+        step = n_halve + 2 * pair
+        bit_a, ids_a = partner(bits[step])
+        bit_b, ids_b = partner(bits[step + 1])
+        place = bit_a + 2 * bit_b
+        diagonal = diagonal_of(step)
+        slots = doubles[pair]
+        for i in range(n_arrays):
+            own = pltpu.make_async_copy(
+                window(accs[i], regions[i]), slots[i].at[place], recv_sem.at[step, i, place])
+            own.start()
+            for k, ids in enumerate((ids_a, ids_b, diagonal)):
+                copy = pltpu.make_async_remote_copy(
+                    src_ref=window(accs[i], regions[i]), dst_ref=slots[i].at[place],
+                    send_sem=send_sem.at[step, i, k], recv_sem=recv_sem.at[step, i, place],
+                    device_id=ids, device_id_type=MESH_ID)
+                copy.start()
+        for i in range(n_arrays):
+            for k in range(3):
+                pltpu.make_async_remote_copy(
+                    src_ref=window(accs[i], regions[i]), dst_ref=slots[i].at[0],
+                    send_sem=send_sem.at[step, i, k], recv_sem=recv_sem.at[step, i, 0],
+                    device_id=ids_a, device_id_type=MESH_ID).wait_send()
+            for g in range(4):
+                pltpu.make_async_copy(
+                    window(accs[i], regions[i]), slots[i].at[g], recv_sem.at[step, i, g]).wait()
+        for i in range(n_arrays):
+            total = slots[i][0] + slots[i][1]
+            total = total + slots[i][2]
+            window(accs[i], regions[i])[...] = total + slots[i][3]
     for i in range(n_arrays):
         window(o_refs[i], regions[i])[...] = window(accs[i], regions[i])[...]
     for back, (ids, keeps) in enumerate(reversed(plan)):
@@ -133,11 +165,12 @@
     for dim in splits:
         shapes = [(s[0] // 2, s[1]) if dim == 0 else (s[0], s[1] // 2) for s in shapes]
         scratch += [pltpu.VMEM(s, jnp.float32) for s in shapes]
-    for _ in bits[len(splits):]:
-        scratch += [pltpu.VMEM(s, jnp.float32) for s in shapes]
+    for _ in range((len(bits) - len(splits)) // 2):
+        scratch += [pltpu.VMEM((4,) + s, jnp.float32) for s in shapes]
     scratch += [pltpu.VMEM(a.shape, jnp.float32) for a in arrays]
     steps = len(bits) + len(splits)
-    scratch += [pltpu.SemaphoreType.DMA((steps, len(arrays))), pltpu.SemaphoreType.DMA((steps, len(arrays)))]
+    sems = (steps, len(arrays), 4)
+    scratch += [pltpu.SemaphoreType.DMA(sems), pltpu.SemaphoreType.DMA(sems)]
     return pl.pallas_call(
         functools.partial(allreduce_kernel, bits, splits, len(arrays)),
         out_shape=[jax.ShapeDtypeStruct(a.shape, jnp.float32) for a in arrays],

time: 219 us -> 223 us (1.018)
  Pallas kernels: 116 us -> 120 us
    pallas_call x1, Pallas kernels: 110 us -> 114 us  [allreduce(): pl.pallas_call(functools.partial(allreduce_kernel, bits, splits, len(arra...]
  transfers between devices with their start and end apart: 8 -> 8, of which waited for: 2 -> 2; matrix products, arithmetic and copies ran while one was open for 7% -> 7% of each run, Pallas kernels for 53% -> 54%
where the time goes in v10:
time: 223 us; the launch traced here: 222 us
  Pallas kernels  120 us (54%)
  starting transfers between devices  29.5 us (13%)
  local copies, waits for them, and re-layouts  23.3 us (10%)
  other arithmetic  20.7 us (9%)
  matrix products  19.1 us (9%)
  waiting for transfers between devices  7.88 us (4%)
    pallas_call x1, Pallas kernels, allreduce(): pl.pallas_call(functools.partial(allreduce_kernel, bits, splits, len(arra...  114 us
    ppermute x8, starting transfers between devices, from_behind(): return lax.ppermute(block, axis, route)  29.5 us
    ppermute x8, waiting for transfers between devices, from_behind(): return lax.ppermute(block, axis, route)  7.88 us
    pallas_call x1, Pallas kernels, kernel_taps(): pl.pallas_call(functools.partial(kernel_taps_body, tap_count), out_shape=...  6.36 us
    unnamed x102, local copies, waits for them, and re-layouts  5.87 us
    slice x4, local copies, waits for them, and re-layouts, depthwise(): term = conv_kernel[tap_index] * extended[first_row:first_row + row_count]  5.61 us
    dot_general x1, matrix products, per_device(): jnp.einsum('hqk,qhd->khd', probs.astype(jnp.bfloat16), dout_heads, prefer...  5.02 us
    mul x1, other arithmetic, per_device(): dmixed_all = upstream * sigma_all * (1.0 + mixed_all * (1.0 - sigma_all))  4.71 us
  transfers between devices with their start and end apart: 8, of which 2 were waited for; matrix products, arithmetic and copies ran while one was open for 7% of the time, Pallas kernels for 54%

profile of v10, /device:TPU:1, one launch (start us, length us, event | category | flops | bytes accessed | tf_op | source)
XLA Modules:
  0.0 222.0 jit_solution(10453763142776461041)
XLA Ops:
  1.8 5.5 %collective-permute-start.2 = (bf16[192,1024]{1,0:T(8,128)(2,1)S(1)}, bf16[192,1024]{1,0:T(8,128)(2,1)S(1)}, u32[]{:S(2)}, u32[]{:S(2)}) collective-permute-start(bf16[192,1024]{1,0:T(8,128)(2,1)S(1)} %pad_maximum_fusion.1), channel_id=1, source_target_pairs={{0,1},{1,2},{2,3},{3,4},{4,5},{5,6},{6,7},{7,8},{8,9},{9,10},{10,1... | collective-permute-start | bytes 1179656 | tf_op jit(solution)/shard_map/ppermute | solution.py:187
  7.3 4.0 %collective-permute-start.1 = (bf16[192,1024]{1,0:T(8,128)(2,1)S(1)}, bf16[192,1024]{1,0:T(8,128)(2,1)S(1)}, u32[]{:S(2)}, u32[]{:S(2)}) collective-permute-start(bf16[192,1024]{1,0:T(8,128)(2,1)S(1)} %pad_maximum_fusion.1), channel_id=1, source_target_pairs={{0,2},{1,3},{2,4},{3,5},{4,6},{5,7},{6,8},{7,9},{8,10},{9,11},{10,... | collective-permute-start | bytes 1179656 | tf_op jit(solution)/shard_map/ppermute | solution.py:187
  11.3 5.8 %collective-permute-start = (bf16[192,1024]{1,0:T(8,128)(2,1)S(1)}, bf16[192,1024]{1,0:T(8,128)(2,1)S(1)}, u32[]{:S(2)}, u32[]{:S(2)}) collective-permute-start(bf16[192,1024]{1,0:T(8,128)(2,1)S(1)} %pad_maximum_fusion.1), channel_id=1, source_target_pairs={{0,3},{1,4},{2,5},{3,6},{4,7},{5,8},{6,9},{7,10},{8,11},{9,12},{10... | collective-permute-start | bytes 1179656 | tf_op jit(solution)/shard_map/ppermute | solution.py:187
  17.1 1.7 fusion.103
  18.8 1.9 fusion.102
  22.3 1.8 copy.23
  24.4 2.7 %collective-permute-done = bf16[192,1024]{1,0:T(8,128)(2,1)S(1)} collective-permute-done((bf16[192,1024]{1,0:T(8,128)(2,1)S(1)}, bf16[192,1024]{1,0:T(8,128)(2,1)S(1)}, u32[]{:S(2)}, u32[]{:S(2)}) %collective-permute-start) | collective-permute-done | bytes 393248 | tf_op jit(solution)/shard_map/ppermute | solution.py:187
  29.0 2.2 fusion.4
  34.9 8.7 %collective-permute-start.3 = (bf16[30,1024]{1,0:T(8,128)(2,1)S(1)}, bf16[30,1024]{1,0:T(8,128)(2,1)S(1)}, u32[]{:S(2)}, u32[]{:S(2)}) collective-permute-start(bf16[30,1024]{1,0:T(8,128)(2,1)S(1)} %get-tuple-element.31), channel_id=1, source_target_pairs={{0,1},{1,2},{2,3},{3,4},{4,5},{5,6},{6,7},{7,8},{8,9},{9,10},{10,1... | collective-permute-start | bytes 184328 | tf_op jit(solution)/shard_map/ppermute | solution.py:187
  45.7 5.1 %collective-permute-done.4 = bf16[30,2048]{1,0:T(8,128)(2,1)S(1)} collective-permute-done((bf16[30,2048]{1,0:T(8,128)(2,1)S(1)}, bf16[30,2048]{1,0:T(8,128)(2,1)S(1)}, u32[]{:S(2)}, u32[]{:S(2)}) %collective-permute-start.4) | collective-permute-done | bytes 122912 | tf_op jit(solution)/shard_map/ppermute | solution.py:187
  51.3 4.7 %add_multiply_fusion = (f32[222,1024]{1,0:T(8,128)S(1)}, f32[222,1024]{1,0:T(8,128)}) fusion(bf16[30,1024]{1,0:T(8,128)(2,1)S(1)} %get-tuple-element.65, bf16[192,1024]{1,0:T(8,128)(2,1)S(1)} %bitcast.124, f32[252,1024]{1,0:T(8,128)S(1)} %maximum_convert_fusion, f32[1024]{0:T(1024)S(1)} %bitcast.146, f32[1024]{0:T(1024)S(1)} %bitcast.148, ...), kind=kLoop, calls=%fused_computation.85 | loop fusion | flops 16594944 | bytes 30588928 | tf_op jit(solution)/shard_map/mul | solution.py:286
  56.0 3.0 %fusion.57 = bf16[192,1024]{1,0:T(8,128)(2,1)S(1)} fusion(f32[222,1024]{1,0:T(8,128)S(1)} %get-tuple-element.22, f32[1024]{0:T(1024)S(1)} %bitcast.147, f32[1024]{0:T(1024)S(1)} %bitcast.149, f32[1024]{0:T(1024)S(1)} %bitcast.153, f32[1024]{0:T(1024)S(1)} %bitcast.155, f32[1024]{0:T(1024)S(1)} %bitcast.157, f32[1024]{0:T(1024)S(1)} %bitcast.159, ...), kind=kLoop, calls=%fused_computation.96 | loop fusion | flops 12189696 | bytes 24899584 | tf_op jit(solution)/shard_map/convert_element_type | solution.py:289
  60.2 1.8 copy.24
  63.2 5.0 %fusion.5 = f32[8,64,768]{2,1,0:T(8,128)} fusion(bf16[192,8,64]{0,2,1:T(8,128)(2,1)} %bitcast.115, f32[8,768,192]{1,2,0:T(8,128)} %copy-done.1, f32[8,192]{1,0:T(8,128)} %log_add_fusion, pred[192,768]{1,0:T(8,128)(4,1)S(1)} %fusion.89), kind=kOutput, calls=%fused_computation.12 | convolution fusion | flops 156893184 | bytes 6641664 | tf_op jit(solution)/shard_map/hqk,qhd->khd/dot_general | solution.py:302
  68.2 3.8 %multiply_convert_fusion = bf16[8,192,768]{2,1,0:T(8,128)(2,1)S(1)} fusion(f32[8,768,192]{1,2,0:T(8,128)} %copy-done.1, f32[8,192]{1,0:T(8,128)S(1)} %fusion.90, f32[8,192]{1,0:T(8,128)S(1)} %copy-done.48, pred[192,768]{1,0:T(8,128)(4,1)S(1)} %fusion.89, bf16[192,8,64]{0,2,1:T(8,128)(2,1)S(1)} %bitcast.116, bf16[768,8,64]{0,2,1:T(8,128)(2,1)S(1)} %bitcast.119), kind=kOutput, calls=%fused_computation.1 | convolution fusion | flops 159252480 | bytes 8220672 | tf_op jit(solution)/shard_map/qhd,khd->hqk/dot_general | solution.py:305
  73.7 1.7 convolution_multiply_fusion
  75.4 1.8 fusion.105.refs_0_
  77.2 3.0 %copy.25 = f32[768,512]{1,0:T(8,128)} copy(f32[768,512]{0,1:T(8,128)} %bitcast.109) | data formatting | bytes 3145728 | tf_op jit(solution)/shard_map/reshape | solution.py:317
  80.2 3.1 %copy.26 = f32[768,512]{1,0:T(8,128)} copy(f32[768,512]{0,1:T(8,128)} %bitcast.114) | data formatting | bytes 3145728 | tf_op jit(solution)/shard_map/reshape | solution.py:317
  83.2 2.2 fusion.3
  93.7 1.9 copy.27
  95.6 6.4 %shard_map.109.refs_1_ = f32[32,1024]{1,0:T(8,128)} custom-call(f32[192,1024]{1,0:T(8,128)} %slice.517.dmixed_ref, f32[222,1024]{1,0:T(8,128)} %slice.513.extended_ref), custom_call_target="tpu_custom_call" | custom-call | tf_op jit(solution)/shard_map/pallas_call | solution.py:223
  101.9 113.5 %shard_map.110 = (f32[512,1024]{1,0:T(8,128)}, f32[32,1024]{1,0:T(8,128)}) custom-call(f32[512,1024]{1,0:T(8,128)} %fusion.105.refs_0_, f32[32,1024]{1,0:T(8,128)} %shard_map.109.refs_1_), custom_call_target="tpu_custom_call" | custom-call | tf_op jit(solution)/shard_map/pallas_call | solution.py:174
  215.5 2.0 fusion.91
  (138 shorter events, 27.1 us)
Async XLA Ops:
  0.6 33.8 %copy-start = (bf16[512,1024]{1,0:T(8,128)(2,1)S(1)}, bf16[512,1024]{1,0:T(8,128)(2,1)}, u32[]{:S(2)}) copy-start(bf16[512,1024]{1,0:T(8,128)(2,1)} %param.9) | copy-start | bytes 3145732
  1.8 22.6 %collective-permute-start.2 = (bf16[192,1024]{1,0:T(8,128)(2,1)S(1)}, bf16[192,1024]{1,0:T(8,128)(2,1)S(1)}, u32[]{:S(2)}, u32[]{:S(2)}) collective-permute-start(bf16[192,1024]{1,0:T(8,128)(2,1)S(1)} %pad_maximum_fusion.1), channel_id=1, source_target_pairs={{0,1},{1,2},{2,3},{3,4},{4,5},{5,6},{6,7},{7,8},{8,9},{9,10},{10,1... | collective-permute-start | bytes 1179656 | tf_op jit(solution)/shard_map/ppermute | solution.py:187
  7.3 17.1 %collective-permute-start.1 = (bf16[192,1024]{1,0:T(8,128)(2,1)S(1)}, bf16[192,1024]{1,0:T(8,128)(2,1)S(1)}, u32[]{:S(2)}, u32[]{:S(2)}) collective-permute-start(bf16[192,1024]{1,0:T(8,128)(2,1)S(1)} %pad_maximum_fusion.1), channel_id=1, source_target_pairs={{0,2},{1,3},{2,4},{3,5},{4,6},{5,7},{6,8},{7,9},{8,10},{9,11},{10,... | collective-permute-start | bytes 1179656 | tf_op jit(solution)/shard_map/ppermute | solution.py:187
  11.3 15.8 %collective-permute-start = (bf16[192,1024]{1,0:T(8,128)(2,1)S(1)}, bf16[192,1024]{1,0:T(8,128)(2,1)S(1)}, u32[]{:S(2)}, u32[]{:S(2)}) collective-permute-start(bf16[192,1024]{1,0:T(8,128)(2,1)S(1)} %pad_maximum_fusion.1), channel_id=1, source_target_pairs={{0,3},{1,4},{2,5},{3,6},{4,7},{5,8},{6,9},{7,10},{8,11},{9,12},{10... | collective-permute-start | bytes 1179656 | tf_op jit(solution)/shard_map/ppermute | solution.py:187
  34.1 16.9 %copy-start.8 = (bf16[192,8,64]{0,2,1:T(8,128)(2,1)}, bf16[192,8,64]{0,2,1:T(8,128)(2,1)S(1)}, u32[]{:S(2)}) copy-start(bf16[192,8,64]{0,2,1:T(8,128)(2,1)S(1)} %fusion.18) | copy-start | bytes 589828
  34.1 16.9 %copy-start.14 = (bf16[1,192,1024]{2,1,0:T(8,128)(2,1)S(1)}, bf16[1,192,1024]{2,1,0:T(8,128)(2,1)}, u32[]{:S(2)}) copy-start(bf16[1,192,1024]{2,1,0:T(8,128)(2,1)} %param.11) | copy-start | bytes 1179652
  34.1 16.9 %copy-start.17 = (f32[1,1024]{1,0:T(1,128)S(1)}, f32[1,1024]{1,0:T(1,128)}, u32[]{:S(2)}) copy-start(f32[1,1024]{1,0:T(1,128)} %get-tuple-element.52) | copy-start | bytes 12292
  34.1 16.9 %copy-start.18 = (f32[1,1024]{1,0:T(1,128)S(1)}, f32[1,1024]{1,0:T(1,128)}, u32[]{:S(2)}) copy-start(f32[1,1024]{1,0:T(1,128)} %get-tuple-element.53) | copy-start | bytes 12292
  34.1 16.9 %copy-start.19 = (f32[1,1024]{1,0:T(1,128)S(1)}, f32[1,1024]{1,0:T(1,128)}, u32[]{:S(2)}) copy-start(f32[1,1024]{1,0:T(1,128)} %get-tuple-element.54) | copy-start | bytes 12292
  34.1 16.9 %copy-start.20 = (f32[1,1024]{1,0:T(1,128)S(1)}, f32[1,1024]{1,0:T(1,128)}, u32[]{:S(2)}) copy-start(f32[1,1024]{1,0:T(1,128)} %get-tuple-element.55) | copy-start | bytes 12292
  34.2 16.9 %copy-start.21 = (f32[1,1024]{1,0:T(1,128)S(1)}, f32[1,1024]{1,0:T(1,128)}, u32[]{:S(2)}) copy-start(f32[1,1024]{1,0:T(1,128)} %get-tuple-element.56) | copy-start | bytes 12292
  34.2 16.9 %copy-start.22 = (f32[1,1024]{1,0:T(1,128)S(1)}, f32[1,1024]{1,0:T(1,128)}, u32[]{:S(2)}) copy-start(f32[1,1024]{1,0:T(1,128)} %get-tuple-element.57) | copy-start | bytes 12292
  34.2 16.9 %copy-start.23 = (f32[1,1024]{1,0:T(1,128)S(1)}, f32[1,1024]{1,0:T(1,128)}, u32[]{:S(2)}) copy-start(f32[1,1024]{1,0:T(1,128)} %get-tuple-element.58) | copy-start | bytes 12292
  34.2 16.9 %copy-start.24 = (f32[1,1024]{1,0:T(1,128)S(1)}, f32[1,1024]{1,0:T(1,128)}, u32[]{:S(2)}) copy-start(f32[1,1024]{1,0:T(1,128)} %get-tuple-element.59) | copy-start | bytes 12292
  34.2 16.9 %copy-start.25 = (f32[1,1024]{1,0:T(1,128)S(1)}, f32[1,1024]{1,0:T(1,128)}, u32[]{:S(2)}) copy-start(f32[1,1024]{1,0:T(1,128)} %get-tuple-element.60) | copy-start | bytes 12292
  34.2 16.9 %copy-start.26 = (f32[1,1024]{1,0:T(1,128)S(1)}, f32[1,1024]{1,0:T(1,128)}, u32[]{:S(2)}) copy-start(f32[1,1024]{1,0:T(1,128)} %get-tuple-element.61) | copy-start | bytes 12292
  34.2 16.9 %copy-start.27 = (f32[1,1024]{1,0:T(1,128)S(1)}, f32[1,1024]{1,0:T(1,128)}, u32[]{:S(2)}) copy-start(f32[1,1024]{1,0:T(1,128)} %get-tuple-element.62) | copy-start | bytes 12292
  34.9 16.0 %collective-permute-start.3 = (bf16[30,1024]{1,0:T(8,128)(2,1)S(1)}, bf16[30,1024]{1,0:T(8,128)(2,1)S(1)}, u32[]{:S(2)}, u32[]{:S(2)}) collective-permute-start(bf16[30,1024]{1,0:T(8,128)(2,1)S(1)} %get-tuple-element.31), channel_id=1, source_target_pairs={{0,1},{1,2},{2,3},{3,4},{4,5},{5,6},{6,7},{7,8},{8,9},{9,10},{10,1... | collective-permute-start | bytes 184328 | tf_op jit(solution)/shard_map/ppermute | solution.py:187
  43.6 7.2 %collective-permute-start.4 = (bf16[30,2048]{1,0:T(8,128)(2,1)S(1)}, bf16[30,2048]{1,0:T(8,128)(2,1)S(1)}, u32[]{:S(2)}, u32[]{:S(2)}) collective-permute-start(bf16[30,2048]{1,0:T(8,128)(2,1)S(1)} %pad_maximum_fusion.2), channel_id=1, source_target_pairs={{1,0},{2,1},{3,2},{4,3},{5,4},{6,5},{7,6},{8,7},{9,8},{10,9},{11,1... | collective-permute-start | bytes 368648 | tf_op jit(solution)/shard_map/ppermute | solution.py:187
  86.5 131.0 %collective-permute-start.5 = (bf16[192,1024]{1,0:T(8,128)(2,1)}, bf16[192,1024]{1,0:T(8,128)(2,1)}, u32[]{:S(2)}, u32[]{:S(2)}) collective-permute-start(bf16[192,1024]{1,0:T(8,128)(2,1)} %get-tuple-element.24), channel_id=1, source_target_pairs={{3,0},{4,1},{5,2},{6,3},{7,4},{8,5},{9,6},{10,7},{11,8},{12,9},{13... | collective-permute-start | bytes 1179656 | tf_op jit(solution)/shard_map/ppermute | solution.py:187
  87.7 129.7 %collective-permute-start.7 = (bf16[192,1024]{1,0:T(8,128)(2,1)}, bf16[192,1024]{1,0:T(8,128)(2,1)}, u32[]{:S(2)}, u32[]{:S(2)}) collective-permute-start(bf16[192,1024]{1,0:T(8,128)(2,1)} %get-tuple-element.25), channel_id=1, source_target_pairs={{1,0},{2,1},{3,2},{4,3},{5,4},{6,5},{7,6},{8,7},{9,8},{10,9},{11,1... | collective-permute-start | bytes 1179656 | tf_op jit(solution)/shard_map/ppermute | solution.py:187
  89.0 128.4 %collective-permute-start.6 = (bf16[192,1024]{1,0:T(8,128)(2,1)}, bf16[192,1024]{1,0:T(8,128)(2,1)}, u32[]{:S(2)}, u32[]{:S(2)}) collective-permute-start(bf16[192,1024]{1,0:T(8,128)(2,1)} %get-tuple-element.26), channel_id=1, source_target_pairs={{2,0},{3,1},{4,2},{5,3},{6,4},{7,5},{8,6},{9,7},{10,8},{11,9},{12,... | collective-permute-start | bytes 1179656 | tf_op jit(solution)/shard_map/ppermute | solution.py:187
  93.7 121.8 %copy-start.4 = (f32[222,1024]{1,0:T(8,128)S(1)}, f32[222,1024]{1,0:T(8,128)}, u32[]{:S(2)}) copy-start(f32[222,1024]{1,0:T(8,128)} %get-tuple-element.23) | copy-start | bytes 2727940
  93.7 123.8 %copy-start.2 = (f32[768,512]{1,0:T(8,128)S(1)}, f32[768,512]{1,0:T(8,128)}, u32[]{:S(2)}) copy-start(f32[768,512]{1,0:T(8,128)} %copy.25) | copy-start | bytes 4718596
  (33 other events, 394.1 us)

commit v11 on v8

--- a/solution.py
+++ b/solution.py
@@ -281,11 +281,15 @@
     )
     window_rows = window.shape[0]
     dkv = jnp.concatenate(
-        [dkey_heads.reshape(window_rows, ATT), dvalue_heads.reshape(window_rows, ATT)], axis=1
-    )
-    dkv_total = dkv[context * row_count:]
+        [
+            dkey_heads.astype(jnp.bfloat16).reshape(window_rows, ATT),
+            dvalue_heads.astype(jnp.bfloat16).reshape(window_rows, ATT),
+        ],
+        axis=1,
+    )
+    dkv_total = dkv[context * row_count:].astype(jnp.float32)
     for slot, offset in enumerate(offsets):
-        part = dkv[slot * row_count:(slot + 1) * row_count].astype(jnp.bfloat16)
+        part = dkv[slot * row_count:(slot + 1) * row_count]
         dkv_total = dkv_total + from_behind(part, "blk", -offset).astype(jnp.float32)
 
     query_grad = dquery.reshape(row_count, ATT).astype(jnp.bfloat16)[None]

time: 219 us -> 218 us (level)
  matrix products: 19.1 us -> 16.1 us
    concatenate x0 -> x1, other arithmetic: none -> 2.46 us  [per_device(): jnp.concatenate([dkey_heads.astype(jnp.bfloat16).reshape(window_rows, ATT...]
    another operation x2 -> x1, other arithmetic: 3.89 us -> 1.53 us
    unnamed x102 -> x106, local copies, waits for them, and re-layouts: 5.87 us -> 4.06 us
  transfers between devices with their start and end apart: 8 -> 8, of which waited for: 2 -> 2; matrix products, arithmetic and copies ran while one was open for 7% -> 6% of each run, Pallas kernels for 53% -> 54%
where the time goes in v11:
time: 218 us; the launch traced here: 216 us
  Pallas kernels  116 us (53%)
  starting transfers between devices  29.5 us (14%)
  other arithmetic  22.3 us (10%)
  local copies, waits for them, and re-layouts  21.4 us (10%)
  matrix products  16.1 us (7%)
  waiting for transfers between devices  9.2 us (4%)
    pallas_call x1, Pallas kernels, allreduce(): pl.pallas_call(functools.partial(allreduce_kernel, bits, splits, len(arra...  110 us
    ppermute x8, starting transfers between devices, from_behind(): return lax.ppermute(block, axis, route)  29.5 us
    ppermute x8, waiting for transfers between devices, from_behind(): return lax.ppermute(block, axis, route)  9.2 us
    pallas_call x1, Pallas kernels, kernel_taps(): pl.pallas_call(functools.partial(kernel_taps_body, tap_count), out_shape=...  6.36 us
    slice x4, local copies, waits for them, and re-layouts, depthwise(): term = conv_kernel[tap_index] * extended[first_row:first_row + row_count]  5.67 us
    dot_general x1, matrix products, per_device(): jnp.einsum('hqk,qhd->khd', probs.astype(jnp.bfloat16), dout_heads, prefer...  5.18 us
    mul x1, other arithmetic, per_device(): dmixed_all = upstream * sigma_all * (1.0 + mixed_all * (1.0 - sigma_all))  4.66 us
  transfers between devices with their start and end apart: 8, of which 2 were waited for; matrix products, arithmetic and copies ran while one was open for 6% of the time, Pallas kernels for 54%

profile of v11, /device:TPU:1, one launch (start us, length us, event | category | flops | bytes accessed | tf_op | source)
XLA Modules:
  0.0 216.4 jit_solution(796733769692410508)
XLA Ops:
  1.8 5.5 %collective-permute-start.2 = (bf16[192,1024]{1,0:T(8,128)(2,1)S(1)}, bf16[192,1024]{1,0:T(8,128)(2,1)S(1)}, u32[]{:S(2)}, u32[]{:S(2)}) collective-permute-start(bf16[192,1024]{1,0:T(8,128)(2,1)S(1)} %pad_maximum_fusion.1), channel_id=1, source_target_pairs={{0,1},{1,2},{2,3},{3,4},{4,5},{5,6},{6,7},{7,8},{8,9},{9,10},{10,1... | collective-permute-start | bytes 1179656 | tf_op jit(solution)/shard_map/ppermute | solution.py:154
  7.3 4.0 %collective-permute-start.1 = (bf16[192,1024]{1,0:T(8,128)(2,1)S(1)}, bf16[192,1024]{1,0:T(8,128)(2,1)S(1)}, u32[]{:S(2)}, u32[]{:S(2)}) collective-permute-start(bf16[192,1024]{1,0:T(8,128)(2,1)S(1)} %pad_maximum_fusion.1), channel_id=1, source_target_pairs={{0,2},{1,3},{2,4},{3,5},{4,6},{5,7},{6,8},{7,9},{8,10},{9,11},{10,... | collective-permute-start | bytes 1179656 | tf_op jit(solution)/shard_map/ppermute | solution.py:154
  11.3 5.8 %collective-permute-start = (bf16[192,1024]{1,0:T(8,128)(2,1)S(1)}, bf16[192,1024]{1,0:T(8,128)(2,1)S(1)}, u32[]{:S(2)}, u32[]{:S(2)}) collective-permute-start(bf16[192,1024]{1,0:T(8,128)(2,1)S(1)} %pad_maximum_fusion.1), channel_id=1, source_target_pairs={{0,3},{1,4},{2,5},{3,6},{4,7},{5,8},{6,9},{7,10},{8,11},{9,12},{10... | collective-permute-start | bytes 1179656 | tf_op jit(solution)/shard_map/ppermute | solution.py:154
  17.1 1.7 fusion.102
  18.8 1.9 fusion.101
  23.1 4.1 %collective-permute-done = bf16[192,1024]{1,0:T(8,128)(2,1)S(1)} collective-permute-done((bf16[192,1024]{1,0:T(8,128)(2,1)S(1)}, bf16[192,1024]{1,0:T(8,128)(2,1)S(1)}, u32[]{:S(2)}, u32[]{:S(2)}) %collective-permute-start) | collective-permute-done | bytes 393248 | tf_op jit(solution)/shard_map/ppermute | solution.py:154
  36.6 8.7 %collective-permute-start.3 = (bf16[30,1024]{1,0:T(8,128)(2,1)S(1)}, bf16[30,1024]{1,0:T(8,128)(2,1)S(1)}, u32[]{:S(2)}, u32[]{:S(2)}) collective-permute-start(bf16[30,1024]{1,0:T(8,128)(2,1)S(1)} %get-tuple-element.31), channel_id=1, source_target_pairs={{0,1},{1,2},{2,3},{3,4},{4,5},{5,6},{6,7},{7,8},{8,9},{9,10},{10,1... | collective-permute-start | bytes 184328 | tf_op jit(solution)/shard_map/ppermute | solution.py:154
  47.4 5.1 %collective-permute-done.4 = bf16[30,2048]{1,0:T(8,128)(2,1)S(1)} collective-permute-done((bf16[30,2048]{1,0:T(8,128)(2,1)S(1)}, bf16[30,2048]{1,0:T(8,128)(2,1)S(1)}, u32[]{:S(2)}, u32[]{:S(2)}) %collective-permute-start.4) | collective-permute-done | bytes 122912 | tf_op jit(solution)/shard_map/ppermute | solution.py:154
  53.0 4.7 %add_multiply_fusion = (f32[222,1024]{1,0:T(8,128)S(1)}, f32[222,1024]{1,0:T(8,128)}) fusion(bf16[30,1024]{1,0:T(8,128)(2,1)S(1)} %get-tuple-element.65, bf16[192,1024]{1,0:T(8,128)(2,1)S(1)} %bitcast.128, f32[252,1024]{1,0:T(8,128)S(1)} %maximum_convert_fusion, f32[1024]{0:T(1024)S(1)} %bitcast.150, f32[1024]{0:T(1024)S(1)} %bitcast.152, ...), kind=kLoop, calls=%fused_computation.88 | loop fusion | flops 16594944 | bytes 30588928 | tf_op jit(solution)/shard_map/mul | solution.py:253
  57.7 3.0 %fusion.54 = bf16[192,1024]{1,0:T(8,128)(2,1)S(1)} fusion(f32[222,1024]{1,0:T(8,128)S(1)} %get-tuple-element.22, f32[1024]{0:T(1024)S(1)} %bitcast.151, f32[1024]{0:T(1024)S(1)} %bitcast.153, f32[1024]{0:T(1024)S(1)} %bitcast.157, f32[1024]{0:T(1024)S(1)} %bitcast.159, f32[1024]{0:T(1024)S(1)} %bitcast.161, f32[1024]{0:T(1024)S(1)} %bitcast.163, ...), kind=kLoop, calls=%fused_computation.94 | loop fusion | flops 12189696 | bytes 24899584 | tf_op jit(solution)/shard_map/convert_element_type | solution.py:256
  61.9 1.8 copy.24
  65.0 5.2 %fusion.10 = bf16[8,64,768]{2,1,0:T(8,128)(2,1)} fusion(bf16[192,8,64]{0,2,1:T(8,128)(2,1)} %bitcast.118, f32[8,768,192]{1,2,0:T(8,128)} %copy-done.1, f32[8,192]{1,0:T(8,128)} %log_add_fusion, pred[192,768]{1,0:T(8,128)(4,1)S(1)} %fusion.86), kind=kOutput, calls=%fused_computation.20 | convolution fusion | flops 157286400 | bytes 5855232 | tf_op jit(solution)/shard_map/hqk,qhd->khd/dot_general | solution.py:269
  70.2 2.1 multiply_convert_fusion
  72.3 1.6 fusion.16
  75.4 1.8 fusion.104.refs_0_
  77.1 2.3 %copy.25 = bf16[768,512]{1,0:T(8,128)(2,1)} copy(bf16[768,512]{0,1:T(8,128)(2,1)} %bitcast.113) | data formatting | bytes 1572864 | tf_op jit(solution)/shard_map/reshape | solution.py:285
  79.4 2.4 %copy.26 = bf16[768,512]{1,0:T(8,128)(2,1)} copy(bf16[768,512]{0,1:T(8,128)(2,1)} %bitcast.123) | data formatting | bytes 1572864 | tf_op jit(solution)/shard_map/reshape | solution.py:286
  81.8 2.5 %fusion.91 = (bf16[192,1024]{1,0:T(8,128)(2,1)}, bf16[192,1024]{1,0:T(8,128)(2,1)}, bf16[192,1024]{1,0:T(8,128)(2,1)}) fusion(bf16[768,512]{1,0:T(8,128)(2,1)} %copy.25, bf16[768,512]{1,0:T(8,128)(2,1)} %copy.26), kind=kLoop, calls=%fused_computation.164 | loop fusion | flops 2359296 | bytes 2752512 | tf_op jit(solution)/shard_map/concatenate | solution.py:283
  86.8 1.5 collective-permute-start.6
  88.4 2.4 %add_divide_fusion = f32[222,1024]{1,0:T(8,128)} fusion(f32[222,1024]{1,0:T(8,128)} %get-tuple-element.23), kind=kLoop, calls=%fused_computation.89 | loop fusion | flops 681984 | bytes 1818624 | tf_op jit(solution)/shard_map/div | solution.py:251
  93.5 6.4 %shard_map.109.refs_1_ = f32[32,1024]{1,0:T(8,128)} custom-call(f32[192,1024]{1,0:T(8,128)} %slice.514.dmixed_ref, f32[222,1024]{1,0:T(8,128)} %slice.510.extended_ref), custom_call_target="tpu_custom_call" | custom-call | tf_op jit(solution)/shard_map/pallas_call | solution.py:190
  99.9 110.0 %shard_map.110 = (f32[512,1024]{1,0:T(8,128)}, f32[32,1024]{1,0:T(8,128)}) custom-call(f32[512,1024]{1,0:T(8,128)} %fusion.104.refs_0_, f32[32,1024]{1,0:T(8,128)} %shard_map.109.refs_1_), custom_call_target="tpu_custom_call" | custom-call | tf_op jit(solution)/shard_map/pallas_call | solution.py:141
  210.0 2.1 fusion.88
  212.1 1.5 add_convert_fusion
  (142 shorter events, 26.9 us)
Async XLA Ops:
  0.6 35.5 %copy-start = (bf16[512,1024]{1,0:T(8,128)(2,1)S(1)}, bf16[512,1024]{1,0:T(8,128)(2,1)}, u32[]{:S(2)}) copy-start(bf16[512,1024]{1,0:T(8,128)(2,1)} %param.9) | copy-start | bytes 3145732
  1.8 21.3 %collective-permute-start.2 = (bf16[192,1024]{1,0:T(8,128)(2,1)S(1)}, bf16[192,1024]{1,0:T(8,128)(2,1)S(1)}, u32[]{:S(2)}, u32[]{:S(2)}) collective-permute-start(bf16[192,1024]{1,0:T(8,128)(2,1)S(1)} %pad_maximum_fusion.1), channel_id=1, source_target_pairs={{0,1},{1,2},{2,3},{3,4},{4,5},{5,6},{6,7},{7,8},{8,9},{9,10},{10,1... | collective-permute-start | bytes 1179656 | tf_op jit(solution)/shard_map/ppermute | solution.py:154
  7.3 15.8 %collective-permute-start.1 = (bf16[192,1024]{1,0:T(8,128)(2,1)S(1)}, bf16[192,1024]{1,0:T(8,128)(2,1)S(1)}, u32[]{:S(2)}, u32[]{:S(2)}) collective-permute-start(bf16[192,1024]{1,0:T(8,128)(2,1)S(1)} %pad_maximum_fusion.1), channel_id=1, source_target_pairs={{0,2},{1,3},{2,4},{3,5},{4,6},{5,7},{6,8},{7,9},{8,10},{9,11},{10,... | collective-permute-start | bytes 1179656 | tf_op jit(solution)/shard_map/ppermute | solution.py:154
  11.3 15.8 %collective-permute-start = (bf16[192,1024]{1,0:T(8,128)(2,1)S(1)}, bf16[192,1024]{1,0:T(8,128)(2,1)S(1)}, u32[]{:S(2)}, u32[]{:S(2)}) collective-permute-start(bf16[192,1024]{1,0:T(8,128)(2,1)S(1)} %pad_maximum_fusion.1), channel_id=1, source_target_pairs={{0,3},{1,4},{2,5},{3,6},{4,7},{5,8},{6,9},{7,10},{8,11},{9,12},{10... | collective-permute-start | bytes 1179656 | tf_op jit(solution)/shard_map/ppermute | solution.py:154
  34.4 18.3 %copy-start.15 = (bf16[1,192,1024]{2,1,0:T(8,128)(2,1)S(1)}, bf16[1,192,1024]{2,1,0:T(8,128)(2,1)}, u32[]{:S(2)}) copy-start(bf16[1,192,1024]{2,1,0:T(8,128)(2,1)} %param.11) | copy-start | bytes 1179652
  34.4 18.3 %copy-start.17 = (f32[1,1024]{1,0:T(1,128)S(1)}, f32[1,1024]{1,0:T(1,128)}, u32[]{:S(2)}) copy-start(f32[1,1024]{1,0:T(1,128)} %get-tuple-element.52) | copy-start | bytes 12292
  34.4 18.3 %copy-start.18 = (f32[1,1024]{1,0:T(1,128)S(1)}, f32[1,1024]{1,0:T(1,128)}, u32[]{:S(2)}) copy-start(f32[1,1024]{1,0:T(1,128)} %get-tuple-element.53) | copy-start | bytes 12292
  34.4 18.3 %copy-start.19 = (f32[1,1024]{1,0:T(1,128)S(1)}, f32[1,1024]{1,0:T(1,128)}, u32[]{:S(2)}) copy-start(f32[1,1024]{1,0:T(1,128)} %get-tuple-element.54) | copy-start | bytes 12292
  34.4 18.3 %copy-start.20 = (f32[1,1024]{1,0:T(1,128)S(1)}, f32[1,1024]{1,0:T(1,128)}, u32[]{:S(2)}) copy-start(f32[1,1024]{1,0:T(1,128)} %get-tuple-element.55) | copy-start | bytes 12292
  34.5 18.3 %copy-start.21 = (f32[1,1024]{1,0:T(1,128)S(1)}, f32[1,1024]{1,0:T(1,128)}, u32[]{:S(2)}) copy-start(f32[1,1024]{1,0:T(1,128)} %get-tuple-element.56) | copy-start | bytes 12292
  34.5 18.3 %copy-start.22 = (f32[1,1024]{1,0:T(1,128)S(1)}, f32[1,1024]{1,0:T(1,128)}, u32[]{:S(2)}) copy-start(f32[1,1024]{1,0:T(1,128)} %get-tuple-element.57) | copy-start | bytes 12292
  34.5 18.3 %copy-start.23 = (f32[1,1024]{1,0:T(1,128)S(1)}, f32[1,1024]{1,0:T(1,128)}, u32[]{:S(2)}) copy-start(f32[1,1024]{1,0:T(1,128)} %get-tuple-element.58) | copy-start | bytes 12292
  34.5 18.3 %copy-start.24 = (f32[1,1024]{1,0:T(1,128)S(1)}, f32[1,1024]{1,0:T(1,128)}, u32[]{:S(2)}) copy-start(f32[1,1024]{1,0:T(1,128)} %get-tuple-element.59) | copy-start | bytes 12292
  34.5 18.3 %copy-start.25 = (f32[1,1024]{1,0:T(1,128)S(1)}, f32[1,1024]{1,0:T(1,128)}, u32[]{:S(2)}) copy-start(f32[1,1024]{1,0:T(1,128)} %get-tuple-element.60) | copy-start | bytes 12292
  34.5 18.3 %copy-start.26 = (f32[1,1024]{1,0:T(1,128)S(1)}, f32[1,1024]{1,0:T(1,128)}, u32[]{:S(2)}) copy-start(f32[1,1024]{1,0:T(1,128)} %get-tuple-element.61) | copy-start | bytes 12292
  34.5 18.3 %copy-start.27 = (f32[1,1024]{1,0:T(1,128)S(1)}, f32[1,1024]{1,0:T(1,128)}, u32[]{:S(2)}) copy-start(f32[1,1024]{1,0:T(1,128)} %get-tuple-element.62) | copy-start | bytes 12292
  34.5 18.3 %copy-start.28 = (f32[1,1024]{1,0:T(1,128)S(1)}, f32[1,1024]{1,0:T(1,128)}, u32[]{:S(2)}) copy-start(f32[1,1024]{1,0:T(1,128)} %get-tuple-element.63) | copy-start | bytes 12292
  36.6 16.0 %collective-permute-start.3 = (bf16[30,1024]{1,0:T(8,128)(2,1)S(1)}, bf16[30,1024]{1,0:T(8,128)(2,1)S(1)}, u32[]{:S(2)}, u32[]{:S(2)}) collective-permute-start(bf16[30,1024]{1,0:T(8,128)(2,1)S(1)} %get-tuple-element.31), channel_id=1, source_target_pairs={{0,1},{1,2},{2,3},{3,4},{4,5},{5,6},{6,7},{7,8},{8,9},{9,10},{10,1... | collective-permute-start | bytes 184328 | tf_op jit(solution)/shard_map/ppermute | solution.py:154
  45.3 7.2 %collective-permute-start.4 = (bf16[30,2048]{1,0:T(8,128)(2,1)S(1)}, bf16[30,2048]{1,0:T(8,128)(2,1)S(1)}, u32[]{:S(2)}, u32[]{:S(2)}) collective-permute-start(bf16[30,2048]{1,0:T(8,128)(2,1)S(1)} %pad_maximum_fusion.2), channel_id=1, source_target_pairs={{1,0},{2,1},{3,2},{4,3},{5,4},{6,5},{7,6},{8,7},{9,8},{10,9},{11,1... | collective-permute-start | bytes 368648 | tf_op jit(solution)/shard_map/ppermute | solution.py:154
  84.2 127.8 %collective-permute-start.5 = (bf16[192,1024]{1,0:T(8,128)(2,1)}, bf16[192,1024]{1,0:T(8,128)(2,1)}, u32[]{:S(2)}, u32[]{:S(2)}) collective-permute-start(bf16[192,1024]{1,0:T(8,128)(2,1)} %get-tuple-element.24), channel_id=1, source_target_pairs={{3,0},{4,1},{5,2},{6,3},{7,4},{8,5},{9,6},{10,7},{11,8},{12,9},{13... | collective-permute-start | bytes 1179656 | tf_op jit(solution)/shard_map/ppermute | solution.py:154
  85.5 126.6 %collective-permute-start.7 = (bf16[192,1024]{1,0:T(8,128)(2,1)}, bf16[192,1024]{1,0:T(8,128)(2,1)}, u32[]{:S(2)}, u32[]{:S(2)}) collective-permute-start(bf16[192,1024]{1,0:T(8,128)(2,1)} %get-tuple-element.25), channel_id=1, source_target_pairs={{1,0},{2,1},{3,2},{4,3},{5,4},{6,5},{7,6},{8,7},{9,8},{10,9},{11,1... | collective-permute-start | bytes 1179656 | tf_op jit(solution)/shard_map/ppermute | solution.py:154
  86.8 125.3 %collective-permute-start.6 = (bf16[192,1024]{1,0:T(8,128)(2,1)}, bf16[192,1024]{1,0:T(8,128)(2,1)}, u32[]{:S(2)}, u32[]{:S(2)}) collective-permute-start(bf16[192,1024]{1,0:T(8,128)(2,1)} %get-tuple-element.26), channel_id=1, source_target_pairs={{2,0},{3,1},{4,2},{5,3},{6,4},{7,5},{8,6},{9,7},{10,8},{11,9},{12,... | collective-permute-start | bytes 1179656 | tf_op jit(solution)/shard_map/ppermute | solution.py:154
  91.7 120.3 %copy-start.2 = (bf16[768,512]{1,0:T(8,128)(2,1)S(1)}, bf16[768,512]{1,0:T(8,128)(2,1)}, u32[]{:S(2)}) copy-start(bf16[768,512]{1,0:T(8,128)(2,1)} %copy.25) | copy-start | bytes 2359300
  92.7 117.2 %copy-start.5 = (f32[222,1024]{1,0:T(8,128)S(1)}, f32[222,1024]{1,0:T(8,128)}, u32[]{:S(2)}) copy-start(f32[222,1024]{1,0:T(8,128)} %add_divide_fusion) | copy-start | bytes 2727940
  (35 other events, 446.5 us)

commit v12 on v11

--- a/solution.py
+++ b/solution.py
@@ -168,18 +168,29 @@
     return total
 
 
-def kernel_taps_body(tap_count, dmixed_ref, extended_ref, out_ref):
-    rows = dmixed_ref.shape[0]
+def kernel_taps_body(tap_count, dmixed_ref, extended_ref, out_ref, shifted_ref):
+    rows, cols = dmixed_ref.shape
     first = tap_count - 1
-    grads = dmixed_ref[...]
-    shifted = []
     for shift in range(8):
-        span = (first - shift) // 8 * 8 + rows if shift <= first else 0
-        shifted.append(extended_ref[pl.ds(shift, span), :] if span else None)
-    for tap in range(tap_count):
-        block, shift = divmod(first - tap, 8)
-        window = shifted[shift][block * 8:block * 8 + rows]
-        out_ref[pl.ds(tap, 1), :] = jnp.sum(grads * window, axis=0, keepdims=True)
+        span = (first - shift) // 8 * 8 + rows
+        shifted_ref[shift, pl.ds(0, span), :] = extended_ref[pl.ds(shift, span), :]
+    for column in range(cols // 128):
+        lanes = pl.ds(column * 128, 128)
+
+        def body(block, sums):
+            start = pl.multiple_of(block * 8, 8)
+            grads = dmixed_ref[pl.ds(start, 8), lanes]
+            updated = []
+            for tap in range(tap_count):
+                offset, shift = divmod(first - tap, 8)
+                window = shifted_ref[shift, pl.ds(pl.multiple_of(start + offset * 8, 8), 8), lanes]
+                updated.append(sums[tap] + grads * window)
+            return tuple(updated)
+
+        zero = jnp.zeros((8, 128), jnp.float32)
+        sums = lax.fori_loop(0, rows // 8, body, tuple(zero for _ in range(tap_count)))
+        for tap in range(tap_count):
+            out_ref[pl.ds(tap, 1), lanes] = jnp.sum(sums[tap], axis=0, keepdims=True)
     out_ref[pl.ds(tap_count, out_ref.shape[0] - tap_count), :] = jnp.zeros(
         (out_ref.shape[0] - tap_count, out_ref.shape[1]), jnp.float32
     )
@@ -192,6 +203,7 @@
         out_shape=jax.ShapeDtypeStruct((padded, dmixed.shape[1]), jnp.float32),
         in_specs=[pl.BlockSpec(memory_space=pltpu.VMEM)] * 2,
         out_specs=pl.BlockSpec(memory_space=pltpu.VMEM),
+        scratch_shapes=[pltpu.VMEM((8, dmixed.shape[0] + (tap_count - 1) // 8 * 8, dmixed.shape[1]), jnp.float32)],
     )(dmixed, extended)
 
 

time: 218 us -> 219 us (level)
  no operation moved by 1% of the time
where the time goes in v12:
time: 219 us; the launch traced here: 218 us
  Pallas kernels  118 us (54%)
  starting transfers between devices  29.3 us (13%)
  other arithmetic  22.3 us (10%)
  local copies, waits for them, and re-layouts  21.3 us (10%)
  matrix products  16.1 us (7%)
  waiting for transfers between devices  9.31 us (4%)
    pallas_call x1, Pallas kernels, allreduce(): pl.pallas_call(functools.partial(allreduce_kernel, bits, splits, len(arra...  110 us
    ppermute x8, starting transfers between devices, from_behind(): return lax.ppermute(block, axis, route)  29.3 us
    ppermute x8, waiting for transfers between devices, from_behind(): return lax.ppermute(block, axis, route)  9.31 us
    pallas_call x1, Pallas kernels, kernel_taps(): pl.pallas_call(functools.partial(kernel_taps_body, tap_count), out_shape=...  7.42 us
    slice x4, local copies, waits for them, and re-layouts, depthwise(): term = conv_kernel[tap_index] * extended[first_row:first_row + row_count]  5.56 us
    dot_general x1, matrix products, per_device(): jnp.einsum('hqk,qhd->khd', probs.astype(jnp.bfloat16), dout_heads, prefer...  5.18 us
    mul x1, other arithmetic, per_device(): dmixed_all = upstream * sigma_all * (1.0 + mixed_all * (1.0 - sigma_all))  4.66 us
  transfers between devices with their start and end apart: 8, of which 2 were waited for; matrix products, arithmetic and copies ran while one was open for 6% of the time, Pallas kernels for 54%

profile of v12, /device:TPU:1, one launch (start us, length us, event | category | flops | bytes accessed | tf_op | source)
XLA Modules:
  0.0 217.6 jit_solution(7167610132244973931)
XLA Ops:
  1.8 5.5 %collective-permute-start.2 = (bf16[192,1024]{1,0:T(8,128)(2,1)S(1)}, bf16[192,1024]{1,0:T(8,128)(2,1)S(1)}, u32[]{:S(2)}, u32[]{:S(2)}) collective-permute-start(bf16[192,1024]{1,0:T(8,128)(2,1)S(1)} %pad_maximum_fusion.1), channel_id=1, source_target_pairs={{0,1},{1,2},{2,3},{3,4},{4,5},{5,6},{6,7},{7,8},{8,9},{9,10},{10,1... | collective-permute-start | bytes 1179656 | tf_op jit(solution)/shard_map/ppermute | solution.py:154
  7.3 4.0 %collective-permute-start.1 = (bf16[192,1024]{1,0:T(8,128)(2,1)S(1)}, bf16[192,1024]{1,0:T(8,128)(2,1)S(1)}, u32[]{:S(2)}, u32[]{:S(2)}) collective-permute-start(bf16[192,1024]{1,0:T(8,128)(2,1)S(1)} %pad_maximum_fusion.1), channel_id=1, source_target_pairs={{0,2},{1,3},{2,4},{3,5},{4,6},{5,7},{6,8},{7,9},{8,10},{9,11},{10,... | collective-permute-start | bytes 1179656 | tf_op jit(solution)/shard_map/ppermute | solution.py:154
  11.3 5.8 %collective-permute-start = (bf16[192,1024]{1,0:T(8,128)(2,1)S(1)}, bf16[192,1024]{1,0:T(8,128)(2,1)S(1)}, u32[]{:S(2)}, u32[]{:S(2)}) collective-permute-start(bf16[192,1024]{1,0:T(8,128)(2,1)S(1)} %pad_maximum_fusion.1), channel_id=1, source_target_pairs={{0,3},{1,4},{2,5},{3,6},{4,7},{5,8},{6,9},{7,10},{8,11},{9,12},{10... | collective-permute-start | bytes 1179656 | tf_op jit(solution)/shard_map/ppermute | solution.py:154
  17.1 1.7 fusion.102
  18.8 1.8 fusion.101
  23.0 4.2 %collective-permute-done = bf16[192,1024]{1,0:T(8,128)(2,1)S(1)} collective-permute-done((bf16[192,1024]{1,0:T(8,128)(2,1)S(1)}, bf16[192,1024]{1,0:T(8,128)(2,1)S(1)}, u32[]{:S(2)}, u32[]{:S(2)}) %collective-permute-start) | collective-permute-done | bytes 393248 | tf_op jit(solution)/shard_map/ppermute | solution.py:154
  36.6 8.7 %collective-permute-start.3 = (bf16[30,1024]{1,0:T(8,128)(2,1)S(1)}, bf16[30,1024]{1,0:T(8,128)(2,1)S(1)}, u32[]{:S(2)}, u32[]{:S(2)}) collective-permute-start(bf16[30,1024]{1,0:T(8,128)(2,1)S(1)} %get-tuple-element.31), channel_id=1, source_target_pairs={{0,1},{1,2},{2,3},{3,4},{4,5},{5,6},{6,7},{7,8},{8,9},{9,10},{10,1... | collective-permute-start | bytes 184328 | tf_op jit(solution)/shard_map/ppermute | solution.py:154
  45.3 1.5 collective-permute-start.4
  47.4 5.1 %collective-permute-done.4 = bf16[30,2048]{1,0:T(8,128)(2,1)S(1)} collective-permute-done((bf16[30,2048]{1,0:T(8,128)(2,1)S(1)}, bf16[30,2048]{1,0:T(8,128)(2,1)S(1)}, u32[]{:S(2)}, u32[]{:S(2)}) %collective-permute-start.4) | collective-permute-done | bytes 122912 | tf_op jit(solution)/shard_map/ppermute | solution.py:154
  53.0 4.7 %add_multiply_fusion = (f32[222,1024]{1,0:T(8,128)S(1)}, f32[222,1024]{1,0:T(8,128)}) fusion(bf16[30,1024]{1,0:T(8,128)(2,1)S(1)} %get-tuple-element.65, bf16[192,1024]{1,0:T(8,128)(2,1)S(1)} %bitcast.128, f32[252,1024]{1,0:T(8,128)S(1)} %maximum_convert_fusion, f32[1024]{0:T(1024)S(1)} %bitcast.150, f32[1024]{0:T(1024)S(1)} %bitcast.152, ...), kind=kLoop, calls=%fused_computation.88 | loop fusion | flops 16594944 | bytes 30588928 | tf_op jit(solution)/shard_map/mul | solution.py:265
  57.7 3.0 %fusion.54 = bf16[192,1024]{1,0:T(8,128)(2,1)S(1)} fusion(f32[222,1024]{1,0:T(8,128)S(1)} %get-tuple-element.22, f32[1024]{0:T(1024)S(1)} %bitcast.151, f32[1024]{0:T(1024)S(1)} %bitcast.153, f32[1024]{0:T(1024)S(1)} %bitcast.157, f32[1024]{0:T(1024)S(1)} %bitcast.159, f32[1024]{0:T(1024)S(1)} %bitcast.161, f32[1024]{0:T(1024)S(1)} %bitcast.163, ...), kind=kLoop, calls=%fused_computation.94 | loop fusion | flops 12189696 | bytes 24899584 | tf_op jit(solution)/shard_map/convert_element_type | solution.py:268
  61.9 1.8 copy.24
  65.0 5.2 %fusion.10 = bf16[8,64,768]{2,1,0:T(8,128)(2,1)} fusion(bf16[192,8,64]{0,2,1:T(8,128)(2,1)} %bitcast.118, f32[8,768,192]{1,2,0:T(8,128)} %copy-done.1, f32[8,192]{1,0:T(8,128)} %log_add_fusion, pred[192,768]{1,0:T(8,128)(4,1)S(1)} %fusion.86), kind=kOutput, calls=%fused_computation.20 | convolution fusion | flops 157286400 | bytes 5855232 | tf_op jit(solution)/shard_map/hqk,qhd->khd/dot_general | solution.py:281
  70.2 2.1 multiply_convert_fusion
  72.3 1.6 fusion.16
  75.4 1.8 fusion.104.refs_0_
  77.1 2.3 %copy.25 = bf16[768,512]{1,0:T(8,128)(2,1)} copy(bf16[768,512]{0,1:T(8,128)(2,1)} %bitcast.113) | data formatting | bytes 1572864 | tf_op jit(solution)/shard_map/reshape | solution.py:297
  79.4 2.4 %copy.26 = bf16[768,512]{1,0:T(8,128)(2,1)} copy(bf16[768,512]{0,1:T(8,128)(2,1)} %bitcast.123) | data formatting | bytes 1572864 | tf_op jit(solution)/shard_map/reshape | solution.py:298
  81.8 2.5 %fusion.91 = (bf16[192,1024]{1,0:T(8,128)(2,1)}, bf16[192,1024]{1,0:T(8,128)(2,1)}, bf16[192,1024]{1,0:T(8,128)(2,1)}) fusion(bf16[768,512]{1,0:T(8,128)(2,1)} %copy.25, bf16[768,512]{1,0:T(8,128)(2,1)} %copy.26), kind=kLoop, calls=%fused_computation.164 | loop fusion | flops 2359296 | bytes 2752512 | tf_op jit(solution)/shard_map/concatenate | solution.py:295
  88.1 2.4 %add_divide_fusion = f32[222,1024]{1,0:T(8,128)} fusion(f32[222,1024]{1,0:T(8,128)} %get-tuple-element.23), kind=kLoop, calls=%fused_computation.89 | loop fusion | flops 681984 | bytes 1818624 | tf_op jit(solution)/shard_map/div | solution.py:263
  93.3 7.4 %shard_map.109.refs_1_ = f32[32,1024]{1,0:T(8,128)} custom-call(f32[192,1024]{1,0:T(8,128)} %slice.514.dmixed_ref, f32[222,1024]{1,0:T(8,128)} %slice.510.extended_ref), custom_call_target="tpu_custom_call" | custom-call | tf_op jit(solution)/shard_map/pallas_call | solution.py:201
  100.7 110.4 %shard_map.110 = (f32[512,1024]{1,0:T(8,128)}, f32[32,1024]{1,0:T(8,128)}) custom-call(f32[512,1024]{1,0:T(8,128)} %fusion.104.refs_0_, f32[32,1024]{1,0:T(8,128)} %shard_map.109.refs_1_), custom_call_target="tpu_custom_call" | custom-call | tf_op jit(solution)/shard_map/pallas_call | solution.py:141
  211.1 2.1 fusion.88
  213.3 1.5 add_convert_fusion
  (142 shorter events, 26.7 us)
Async XLA Ops:
  0.6 35.5 %copy-start = (bf16[512,1024]{1,0:T(8,128)(2,1)S(1)}, bf16[512,1024]{1,0:T(8,128)(2,1)}, u32[]{:S(2)}) copy-start(bf16[512,1024]{1,0:T(8,128)(2,1)} %param.9) | copy-start | bytes 3145732
  1.8 21.2 %collective-permute-start.2 = (bf16[192,1024]{1,0:T(8,128)(2,1)S(1)}, bf16[192,1024]{1,0:T(8,128)(2,1)S(1)}, u32[]{:S(2)}, u32[]{:S(2)}) collective-permute-start(bf16[192,1024]{1,0:T(8,128)(2,1)S(1)} %pad_maximum_fusion.1), channel_id=1, source_target_pairs={{0,1},{1,2},{2,3},{3,4},{4,5},{5,6},{6,7},{7,8},{8,9},{9,10},{10,1... | collective-permute-start | bytes 1179656 | tf_op jit(solution)/shard_map/ppermute | solution.py:154
  7.3 15.7 %collective-permute-start.1 = (bf16[192,1024]{1,0:T(8,128)(2,1)S(1)}, bf16[192,1024]{1,0:T(8,128)(2,1)S(1)}, u32[]{:S(2)}, u32[]{:S(2)}) collective-permute-start(bf16[192,1024]{1,0:T(8,128)(2,1)S(1)} %pad_maximum_fusion.1), channel_id=1, source_target_pairs={{0,2},{1,3},{2,4},{3,5},{4,6},{5,7},{6,8},{7,9},{8,10},{9,11},{10,... | collective-permute-start | bytes 1179656 | tf_op jit(solution)/shard_map/ppermute | solution.py:154
  11.3 15.8 %collective-permute-start = (bf16[192,1024]{1,0:T(8,128)(2,1)S(1)}, bf16[192,1024]{1,0:T(8,128)(2,1)S(1)}, u32[]{:S(2)}, u32[]{:S(2)}) collective-permute-start(bf16[192,1024]{1,0:T(8,128)(2,1)S(1)} %pad_maximum_fusion.1), channel_id=1, source_target_pairs={{0,3},{1,4},{2,5},{3,6},{4,7},{5,8},{6,9},{7,10},{8,11},{9,12},{10... | collective-permute-start | bytes 1179656 | tf_op jit(solution)/shard_map/ppermute | solution.py:154
  34.4 18.3 %copy-start.15 = (bf16[1,192,1024]{2,1,0:T(8,128)(2,1)S(1)}, bf16[1,192,1024]{2,1,0:T(8,128)(2,1)}, u32[]{:S(2)}) copy-start(bf16[1,192,1024]{2,1,0:T(8,128)(2,1)} %param.11) | copy-start | bytes 1179652
  34.4 18.3 %copy-start.17 = (f32[1,1024]{1,0:T(1,128)S(1)}, f32[1,1024]{1,0:T(1,128)}, u32[]{:S(2)}) copy-start(f32[1,1024]{1,0:T(1,128)} %get-tuple-element.52) | copy-start | bytes 12292
  34.4 18.3 %copy-start.18 = (f32[1,1024]{1,0:T(1,128)S(1)}, f32[1,1024]{1,0:T(1,128)}, u32[]{:S(2)}) copy-start(f32[1,1024]{1,0:T(1,128)} %get-tuple-element.53) | copy-start | bytes 12292
  34.4 18.3 %copy-start.19 = (f32[1,1024]{1,0:T(1,128)S(1)}, f32[1,1024]{1,0:T(1,128)}, u32[]{:S(2)}) copy-start(f32[1,1024]{1,0:T(1,128)} %get-tuple-element.54) | copy-start | bytes 12292
  34.4 18.3 %copy-start.20 = (f32[1,1024]{1,0:T(1,128)S(1)}, f32[1,1024]{1,0:T(1,128)}, u32[]{:S(2)}) copy-start(f32[1,1024]{1,0:T(1,128)} %get-tuple-element.55) | copy-start | bytes 12292
  34.5 18.3 %copy-start.21 = (f32[1,1024]{1,0:T(1,128)S(1)}, f32[1,1024]{1,0:T(1,128)}, u32[]{:S(2)}) copy-start(f32[1,1024]{1,0:T(1,128)} %get-tuple-element.56) | copy-start | bytes 12292
  34.5 18.3 %copy-start.22 = (f32[1,1024]{1,0:T(1,128)S(1)}, f32[1,1024]{1,0:T(1,128)}, u32[]{:S(2)}) copy-start(f32[1,1024]{1,0:T(1,128)} %get-tuple-element.57) | copy-start | bytes 12292
  34.5 18.3 %copy-start.23 = (f32[1,1024]{1,0:T(1,128)S(1)}, f32[1,1024]{1,0:T(1,128)}, u32[]{:S(2)}) copy-start(f32[1,1024]{1,0:T(1,128)} %get-tuple-element.58) | copy-start | bytes 12292
  34.5 18.3 %copy-start.24 = (f32[1,1024]{1,0:T(1,128)S(1)}, f32[1,1024]{1,0:T(1,128)}, u32[]{:S(2)}) copy-start(f32[1,1024]{1,0:T(1,128)} %get-tuple-element.59) | copy-start | bytes 12292
  34.5 18.3 %copy-start.25 = (f32[1,1024]{1,0:T(1,128)S(1)}, f32[1,1024]{1,0:T(1,128)}, u32[]{:S(2)}) copy-start(f32[1,1024]{1,0:T(1,128)} %get-tuple-element.60) | copy-start | bytes 12292
  34.5 18.3 %copy-start.26 = (f32[1,1024]{1,0:T(1,128)S(1)}, f32[1,1024]{1,0:T(1,128)}, u32[]{:S(2)}) copy-start(f32[1,1024]{1,0:T(1,128)} %get-tuple-element.61) | copy-start | bytes 12292
  34.5 18.3 %copy-start.27 = (f32[1,1024]{1,0:T(1,128)S(1)}, f32[1,1024]{1,0:T(1,128)}, u32[]{:S(2)}) copy-start(f32[1,1024]{1,0:T(1,128)} %get-tuple-element.62) | copy-start | bytes 12292
  34.5 18.3 %copy-start.28 = (f32[1,1024]{1,0:T(1,128)S(1)}, f32[1,1024]{1,0:T(1,128)}, u32[]{:S(2)}) copy-start(f32[1,1024]{1,0:T(1,128)} %get-tuple-element.63) | copy-start | bytes 12292
  36.6 16.0 %collective-permute-start.3 = (bf16[30,1024]{1,0:T(8,128)(2,1)S(1)}, bf16[30,1024]{1,0:T(8,128)(2,1)S(1)}, u32[]{:S(2)}, u32[]{:S(2)}) collective-permute-start(bf16[30,1024]{1,0:T(8,128)(2,1)S(1)} %get-tuple-element.31), channel_id=1, source_target_pairs={{0,1},{1,2},{2,3},{3,4},{4,5},{5,6},{6,7},{7,8},{8,9},{9,10},{10,1... | collective-permute-start | bytes 184328 | tf_op jit(solution)/shard_map/ppermute | solution.py:154
  45.3 7.2 %collective-permute-start.4 = (bf16[30,2048]{1,0:T(8,128)(2,1)S(1)}, bf16[30,2048]{1,0:T(8,128)(2,1)S(1)}, u32[]{:S(2)}, u32[]{:S(2)}) collective-permute-start(bf16[30,2048]{1,0:T(8,128)(2,1)S(1)} %pad_maximum_fusion.2), channel_id=1, source_target_pairs={{1,0},{2,1},{3,2},{4,3},{5,4},{6,5},{7,6},{8,7},{9,8},{10,9},{11,1... | collective-permute-start | bytes 368648 | tf_op jit(solution)/shard_map/ppermute | solution.py:154
  84.2 129.0 %collective-permute-start.5 = (bf16[192,1024]{1,0:T(8,128)(2,1)}, bf16[192,1024]{1,0:T(8,128)(2,1)}, u32[]{:S(2)}, u32[]{:S(2)}) collective-permute-start(bf16[192,1024]{1,0:T(8,128)(2,1)} %get-tuple-element.24), channel_id=1, source_target_pairs={{3,0},{4,1},{5,2},{6,3},{7,4},{8,5},{9,6},{10,7},{11,8},{12,9},{13... | collective-permute-start | bytes 1179656 | tf_op jit(solution)/shard_map/ppermute | solution.py:154
  85.5 127.7 %collective-permute-start.7 = (bf16[192,1024]{1,0:T(8,128)(2,1)}, bf16[192,1024]{1,0:T(8,128)(2,1)}, u32[]{:S(2)}, u32[]{:S(2)}) collective-permute-start(bf16[192,1024]{1,0:T(8,128)(2,1)} %get-tuple-element.25), channel_id=1, source_target_pairs={{1,0},{2,1},{3,2},{4,3},{5,4},{6,5},{7,6},{8,7},{9,8},{10,9},{11,1... | collective-permute-start | bytes 1179656 | tf_op jit(solution)/shard_map/ppermute | solution.py:154
  86.8 126.4 %collective-permute-start.6 = (bf16[192,1024]{1,0:T(8,128)(2,1)}, bf16[192,1024]{1,0:T(8,128)(2,1)}, u32[]{:S(2)}, u32[]{:S(2)}) collective-permute-start(bf16[192,1024]{1,0:T(8,128)(2,1)} %get-tuple-element.26), channel_id=1, source_target_pairs={{2,0},{3,1},{4,2},{5,3},{6,4},{7,5},{8,6},{9,7},{10,8},{11,9},{12,... | collective-permute-start | bytes 1179656 | tf_op jit(solution)/shard_map/ppermute | solution.py:154
  91.5 121.8 %copy-start.2 = (bf16[768,512]{1,0:T(8,128)(2,1)S(1)}, bf16[768,512]{1,0:T(8,128)(2,1)}, u32[]{:S(2)}) copy-start(bf16[768,512]{1,0:T(8,128)(2,1)} %copy.25) | copy-start | bytes 2359300
  92.5 118.6 %copy-start.5 = (f32[222,1024]{1,0:T(8,128)S(1)}, f32[222,1024]{1,0:T(8,128)}, u32[]{:S(2)}) copy-start(f32[222,1024]{1,0:T(8,128)} %add_divide_fusion) | copy-start | bytes 2727940
  (35 other events, 446.4 us)
